TPU v7x, 32 devices: a whole 2x2x4 slice. The times are simulated.
32 devices in a mesh: grp: 2 (over core), row: 2 (over y), col: 8 (over z, x).
Axes of the slice: x: 2, y: 2, z: 4, core: 2. Of those that a mesh axis runs over, the one named last changes fastest.
Arguments:
- load: float32 [4, 8, 1024, 256], P(('grp', 'row'), 'col'), may hold values from -6 to 6
- guess: float32 [4, 8, 1024, 256], P(('grp', 'row'), 'col'), may hold values from -6 to 6
- interface_op: bfloat16 [4, 8, 1024, 1024], P(('grp', 'row'), 'col'), may hold values from -1 to 5
- precond: bfloat16 [4, 8, 1024, 1024], P(('grp', 'row'), 'col'), may hold values from -1 to 2
- basis: bfloat16 [4, 8, 1024, 64], P(('grp', 'row'), 'col'), may hold values from -0.375 to 0.375
- coarse_inverse: bfloat16 [2048, 2048], P(('grp', 'row'), 'col'), may hold values from -0.1875 to 0.1875
- edge_rows: int32 [4, 8, 1024], P(('grp', 'row'), 'col'), may hold values from 0 to 1023, each once within a row
- coarse_slot: int32 [4, 8, 64], P(('grp', 'row'), 'col'), may hold values from 0 to 63, each once within a row
Outputs:
- displacement: float32 [4, 8, 1024, 256], P(('grp', 'row'), 'col')
Inputs may be any that keep to these rules, and one draw needn't show every extreme that they name: `edge_rows`: each subdomain lists each of its 1024 interface rows once. `coarse_slot`: each subdomain gives each of its 64 basis vectors a different offset.
All inputs are finite; a program needn't handle non-finite values.
Results may differ from a plain program's by a relative error of at most 0.0095.
Values may be sent and summed in bfloat16 or wider, within the bound.
No kernel may reach another device: no remote copies, remote signals or barrier semaphores. Data moves between devices by JAX's collectives and lax.ppermute only.
A program may use at most 64 MiB of HBM per device.

v0:
```python
import jax
import jax.numpy as jnp
from jax import lax
from jax.sharding import PartitionSpec as P

ITERS = 2


OMEGA = 0.6


def extended(shard, sides, width):
    for axis, dim in sides:
        size, length = (lax.axis_size(axis), shard.shape[dim])
        up = [(i, (i + 1) % size) for i in range(size - 1)]
        down = [(j, i) for i, j in up]
        last = lax.slice_in_dim(shard, length - width, length, axis=dim)
        first = lax.slice_in_dim(shard, 0, width, axis=dim)
        before = lax.ppermute(last, axis, up)
        after = lax.ppermute(first, axis, down)
        shard = jnp.concatenate([before, shard, after], axis=dim)
    return shard


def body(load, guess, interface_op, precond, basis, coarse_inverse, edge_rows, coarse_slot):
    local_load = load[0, 0]
    current = guess[0, 0]
    operator_block = interface_op[0, 0]
    precond_block = precond[0, 0]
    basis_block = basis[0, 0]
    row_order = edge_rows[0, 0]
    slot_order = coarse_slot[0, 0]
    n_unknowns, n_cases = local_load.shape
    edge_len = n_unknowns // 4
    n_basis = basis_block.shape[1]
    block_len = coarse_inverse.shape[1]
    grid_rows = lax.axis_size(("grp", "row"))
    grid_cols = lax.axis_size("col")
    my_row = lax.axis_index(("grp", "row"))
    my_col = lax.axis_index("col")
    present = jnp.stack([my_col > 0, my_col < grid_cols - 1, my_row > 0, my_row < grid_rows - 1])
    present = present.astype(jnp.float32)[:, None, None]
    selector = (slot_order[:, None] == jnp.arange(n_basis, dtype=jnp.int32)[None, :]).astype(
        jnp.bfloat16
    )
    contract_first = (((0,), (0,)), ((), ()))

    def place(values):
        blank = jnp.zeros((n_unknowns, n_cases), jnp.float32)
        return blank.at[row_order].set(values.reshape(n_unknowns, n_cases))

    def traces(values):
        own = values[row_order].reshape(4, edge_len, n_cases)
        across_cols = extended(own[0:2], (("col", 0),), 1)
        across_rows = extended(own[2:4], ((("grp", "row"), 0),), 1)
        beside = jnp.stack([across_cols[0], across_cols[3], across_rows[0], across_rows[3]])
        return (own, beside)

    for sweep in range(ITERS):
        applied = jnp.dot(
            operator_block, current.astype(jnp.bfloat16), preferred_element_type=jnp.float32
        )
        own_applied, beside_applied = traces(applied)
        resid = local_load - applied - place(beside_applied)
        resid_bf = resid.astype(jnp.bfloat16)
        local_fix = jnp.dot(precond_block, resid_bf, preferred_element_type=jnp.float32)
        fine_own, fine_beside = traces(local_fix)
        smooth_fix = local_fix + 0.5 * place(present * (fine_beside - fine_own))
        coarse_res = lax.dot_general(
            basis_block, resid_bf, contract_first, preferred_element_type=jnp.float32
        ).astype(jnp.bfloat16)
        ordered = lax.dot_general(
            selector, coarse_res, contract_first, preferred_element_type=jnp.float32
        ).astype(jnp.bfloat16)
        row_block = lax.all_gather(ordered, "col", axis=0, tiled=True)
        source = lax.all_gather(row_block, ("grp", "row"), axis=0, tiled=True)
        offset = my_col * block_len
        column_part = lax.dynamic_slice_in_dim(source, offset, block_len, 0)
        summed = lax.psum_scatter(
            jnp.dot(coarse_inverse, column_part, preferred_element_type=jnp.float32),
            "col",
            scatter_dimension=0,
            tiled=True,
        ).astype(jnp.bfloat16)
        picked = jnp.dot(selector, summed, preferred_element_type=jnp.float32).astype(jnp.bfloat16)
        coarse_fix = jnp.dot(basis_block, picked, preferred_element_type=jnp.float32)
        current = current + OMEGA * (smooth_fix + coarse_fix)
    return current[None, None]


def solution(mesh):
    return jax.shard_map(
        body,
        mesh=mesh,
        in_specs=(
            P(("grp", "row"), "col", None, None),
            P(("grp", "row"), "col", None, None),
            P(("grp", "row"), "col", None, None),
            P(("grp", "row"), "col", None, None),
            P(("grp", "row"), "col", None, None),
            P(("grp", "row"), "col"),
            P(("grp", "row"), "col", None),
            P(("grp", "row"), "col", None),
        ),
        out_specs=P(("grp", "row"), "col", None, None),
        check_vma=False,
    )
```

profile of v0, /device:TPU:0, one launch (start us, length us, event | category | flops | bytes accessed | tf_op | source)
XLA Modules:
  0.0 328.5 jit_solution(16232925203345687816)
XLA Ops:
  10.1 4.7 %gather_fusion = f32[1024,256]{1,0:T(8,128)} fusion(f32[1024,256]{1,0:T(8,128)S(1)} %fusion.6, s32[1024]{0:T(1024)S(1)} %broadcast_clamp_fusion), kind=kCustom, calls=%fused_computation | custom fusion | bytes 2101248 | tf_op jit(solution)/shard_map/gather | solution.py:53
  16.0 4.9 %collective-permute-start = (f32[1,256,256]{2,1,0:T(8,128)S(1)}, f32[1,256,256]{2,1,0:T(8,128)S(1)}, u32[]{:S(2)}, u32[]{:S(2)}) collective-permute-start(f32[1,256,256]{2,1,0:T(8,128)S(1)} %get-tuple-element.17), channel_id=1, source_target_pairs={{0,1},{1,2},{2,3},{3,4},{4,5},{5,6},{6,7},{8,9},{9,10},{10,11},{11... | collective-permute-start | bytes 786440 | tf_op jit(solution)/shard_map/ppermute | solution.py:19
  20.9 3.4 %collective-permute-start.2 = (f32[1,256,256]{2,1,0:T(8,128)S(1)}, f32[1,256,256]{2,1,0:T(8,128)S(1)}, u32[]{:S(2)}, u32[]{:S(2)}) collective-permute-start(f32[1,256,256]{2,1,0:T(8,128)S(1)} %get-tuple-element.18), channel_id=1, source_target_pairs={{0,8},{8,16},{16,24},{1,9},{9,17},{17,25},{2,10},{10,18},{18,26},{... | collective-permute-start | bytes 786440 | tf_op jit(solution)/shard_map/ppermute | solution.py:19
  27.0 4.0 %collective-permute-done.2 = f32[1,256,256]{2,1,0:T(8,128)S(1)} collective-permute-done((f32[1,256,256]{2,1,0:T(8,128)S(1)}, f32[1,256,256]{2,1,0:T(8,128)S(1)}, u32[]{:S(2)}, u32[]{:S(2)}) %collective-permute-start.2) | collective-permute-done | bytes 262176 | tf_op jit(solution)/shard_map/ppermute | solution.py:19
  36.1 6.3 %scatter_custom_fusion = f32[1024,256]{1,0:T(8,128)} fusion(s32[1024]{0:T(1024)S(1)} %bitcast.145, f32[1024,256]{1,0:T(8,128)} %bitcast.140, f32[]{:T(128)} %constant.14.clone.1), kind=kCustom, calls=%fused_computation.58 | custom fusion | bytes 1049088 | tf_op jit(solution)/shard_map/scatter | solution.py:50
  46.3 34.9 %all_gather.12 = bf16[512,256]{1,0:T(8,128)(2,1)} all-gather(bf16[64,256]{1,0:T(8,128)(2,1)S(1)} %convolution_convert_fusion.5), channel_id=1, replica_groups=mesh['grp'=2,'row'=2,'col'=8] {'col'}, dimensions={0}, use_global_device_ids=true | all-gather | bytes 294912 | tf_op jit(solution)/shard_map/all_gather | solution.py:75
  81.2 15.8 %all-gather.3.cloned.1.call-done = bf16[2048,256]{1,0:T(8,128)(2,1)} async-done(((bf16[512,256]{1,0:T(8,128)(2,1)}), bf16[2048,256]{1,0:T(8,128)(2,1)}) %all-gather.3.cloned.1.call-update) | async-done | bytes 1048592 | tf_op jit(solution)/shard_map/all_gather | solution.py:76
  101.7 4.7 %gather_fusion.1 = f32[1024,256]{1,0:T(8,128)} fusion(f32[1024,256]{1,0:T(8,128)S(1)} %fusion.14, s32[1024]{0:T(1024)S(1)} %broadcast_clamp_fusion), kind=kCustom, calls=%fused_computation.1 | custom fusion | bytes 2101248 | tf_op jit(solution)/shard_map/gather | solution.py:53
  107.8 3.4 %collective-permute-start.4 = (f32[1,256,256]{2,1,0:T(8,128)S(1)}, f32[1,256,256]{2,1,0:T(8,128)S(1)}, u32[]{:S(2)}, u32[]{:S(2)}) collective-permute-start(f32[1,256,256]{2,1,0:T(8,128)S(1)} %get-tuple-element.13), channel_id=1, source_target_pairs={{0,1},{1,2},{2,3},{3,4},{4,5},{5,6},{6,7},{8,9},{9,10},{10,11},{11... | collective-permute-start | bytes 786440 | tf_op jit(solution)/shard_map/ppermute | solution.py:19
  112.5 4.6 %collective-permute-start.6 = (f32[1,256,256]{2,1,0:T(8,128)S(1)}, f32[1,256,256]{2,1,0:T(8,128)S(1)}, u32[]{:S(2)}, u32[]{:S(2)}) collective-permute-start(f32[1,256,256]{2,1,0:T(8,128)S(1)} %get-tuple-element.15), channel_id=1, source_target_pairs={{0,8},{8,16},{16,24},{1,9},{9,17},{17,25},{2,10},{10,18},{18,26},{... | collective-permute-start | bytes 786440 | tf_op jit(solution)/shard_map/ppermute | solution.py:19
  122.5 4.4 %collective-permute-done.5 = f32[1,256,256]{2,1,0:T(8,128)S(1)} collective-permute-done((f32[1,256,256]{2,1,0:T(8,128)S(1)}, f32[1,256,256]{2,1,0:T(8,128)S(1)}, u32[]{:S(2)}, u32[]{:S(2)}) %collective-permute-start.5) | collective-permute-done | bytes 262176 | tf_op jit(solution)/shard_map/ppermute | solution.py:20
  128.2 6.3 %scatter_custom_fusion.1 = f32[1024,256]{1,0:T(8,128)} fusion(s32[1024]{0:T(1024)S(1)} %bitcast.146, f32[1024,256]{1,0:T(8,128)} %fusion.25, f32[]{:T(128)} %constant.14.clone.1), kind=kCustom, calls=%fused_computation.56 | custom fusion | bytes 1049088 | tf_op jit(solution)/shard_map/scatter | solution.py:50
  134.5 28.8 %reduce-scatter.7.cloned.1.call-done = f32[64,256]{1,0:T(8,128)} async-done(((f32[512,256]{1,0:T(8,128)}), f32[64,256]{1,0:T(8,128)}) %reduce-scatter.7.cloned.1.call-update) | async-done | bytes 65552
  169.8 4.7 %gather_fusion.2 = f32[1024,256]{1,0:T(8,128)} fusion(f32[1024,256]{1,0:T(8,128)S(1)} %fusion.8, s32[1024]{0:T(1024)S(1)} %broadcast_clamp_fusion), kind=kCustom, calls=%fused_computation.2 | custom fusion | bytes 2101248 | tf_op jit(solution)/shard_map/gather | solution.py:53
  178.9 3.4 %collective-permute-start.10 = (f32[1,256,256]{2,1,0:T(8,128)S(1)}, f32[1,256,256]{2,1,0:T(8,128)S(1)}, u32[]{:S(2)}, u32[]{:S(2)}) collective-permute-start(f32[1,256,256]{2,1,0:T(8,128)S(1)} %get-tuple-element.10), channel_id=1, source_target_pairs={{0,8},{8,16},{16,24},{1,9},{9,17},{17,25},{2,10},{10,18},{18,26},{... | collective-permute-start | bytes 786440 | tf_op jit(solution)/shard_map/ppermute | solution.py:19
  186.3 4.3 %collective-permute-done.9 = f32[1,256,256]{2,1,0:T(8,128)S(1)} collective-permute-done((f32[1,256,256]{2,1,0:T(8,128)S(1)}, f32[1,256,256]{2,1,0:T(8,128)S(1)}, u32[]{:S(2)}, u32[]{:S(2)}) %collective-permute-start.9) | collective-permute-done | bytes 262176 | tf_op jit(solution)/shard_map/ppermute | solution.py:20
  193.3 6.3 %scatter_custom_fusion.2 = f32[1024,256]{1,0:T(8,128)} fusion(s32[1024]{0:T(1024)S(1)} %bitcast.147, f32[1024,256]{1,0:T(8,128)} %bitcast.141, f32[]{:T(128)} %constant.14.clone.1), kind=kCustom, calls=%fused_computation.54 | custom fusion | bytes 1049088 | tf_op jit(solution)/shard_map/scatter | solution.py:50
  203.4 33.6 %all_gather.14 = bf16[512,256]{1,0:T(8,128)(2,1)} all-gather(bf16[64,256]{1,0:T(8,128)(2,1)S(1)} %convolution_convert_fusion.3), channel_id=1, replica_groups=mesh['grp'=2,'row'=2,'col'=8] {'col'}, dimensions={0}, use_global_device_ids=true | all-gather | bytes 294912 | tf_op jit(solution)/shard_map/all_gather | solution.py:75
  237.2 14.9 %all-gather.5.cloned.1.call-done = bf16[2048,256]{1,0:T(8,128)(2,1)} async-done(((bf16[512,256]{1,0:T(8,128)(2,1)}), bf16[2048,256]{1,0:T(8,128)(2,1)}) %all-gather.5.cloned.1.call-update) | async-done | bytes 1048592 | tf_op jit(solution)/shard_map/all_gather | solution.py:76
  256.6 4.7 %gather_fusion.3 = f32[1024,256]{1,0:T(8,128)} fusion(f32[1024,256]{1,0:T(8,128)S(1)} %fusion.11, s32[1024]{0:T(1024)S(1)} %broadcast_clamp_fusion), kind=kCustom, calls=%fused_computation.3 | custom fusion | bytes 2101248 | tf_op jit(solution)/shard_map/gather | solution.py:53
  267.4 4.6 %collective-permute-start.14 = (f32[1,256,256]{2,1,0:T(8,128)S(1)}, f32[1,256,256]{2,1,0:T(8,128)S(1)}, u32[]{:S(2)}, u32[]{:S(2)}) collective-permute-start(f32[1,256,256]{2,1,0:T(8,128)S(1)} %get-tuple-element.7), channel_id=1, source_target_pairs={{0,8},{8,16},{16,24},{1,9},{9,17},{17,25},{2,10},{10,18},{18,26},{... | collective-permute-start | bytes 786440 | tf_op jit(solution)/shard_map/ppermute | solution.py:19
  277.5 4.4 %collective-permute-done.13 = f32[1,256,256]{2,1,0:T(8,128)S(1)} collective-permute-done((f32[1,256,256]{2,1,0:T(8,128)S(1)}, f32[1,256,256]{2,1,0:T(8,128)S(1)}, u32[]{:S(2)}, u32[]{:S(2)}) %collective-permute-start.13) | collective-permute-done | bytes 262176 | tf_op jit(solution)/shard_map/ppermute | solution.py:20
  283.1 6.3 %scatter_custom_fusion.3 = f32[1024,256]{1,0:T(8,128)} fusion(s32[1024]{0:T(1024)S(1)} %bitcast.148, f32[1024,256]{1,0:T(8,128)} %fusion.24, f32[]{:T(128)} %constant.14.clone.1), kind=kCustom, calls=%fused_computation.52 | custom fusion | bytes 1049088 | tf_op jit(solution)/shard_map/scatter | solution.py:50
  289.4 28.6 %reduce-scatter.9.cloned.1.call-done = f32[64,256]{1,0:T(8,128)} async-done(((f32[512,256]{1,0:T(8,128)}), f32[64,256]{1,0:T(8,128)}) %reduce-scatter.9.cloned.1.call-update) | async-done | bytes 65552
  (73 shorter events, 73.4 us)
Async XLA Ops:
  6.5 90.5 %all-gather.3.cloned.1.call-start = ((), (), s32[]{:S(2)}) async-start(), calls=%async_computation.2 | async-start | bytes 1310720 | tf_op jit(solution)/shard_map/all_gather | solution.py:76
  16.0 10.9 %collective-permute-start = (f32[1,256,256]{2,1,0:T(8,128)S(1)}, f32[1,256,256]{2,1,0:T(8,128)S(1)}, u32[]{:S(2)}, u32[]{:S(2)}) collective-permute-start(f32[1,256,256]{2,1,0:T(8,128)S(1)} %get-tuple-element.17), channel_id=1, source_target_pairs={{0,1},{1,2},{2,3},{3,4},{4,5},{5,6},{6,7},{8,9},{9,10},{10,11},{11... | collective-permute-start | bytes 786440 | tf_op jit(solution)/shard_map/ppermute | solution.py:19
  20.9 10.1 %collective-permute-start.2 = (f32[1,256,256]{2,1,0:T(8,128)S(1)}, f32[1,256,256]{2,1,0:T(8,128)S(1)}, u32[]{:S(2)}, u32[]{:S(2)}) collective-permute-start(f32[1,256,256]{2,1,0:T(8,128)S(1)} %get-tuple-element.18), channel_id=1, source_target_pairs={{0,8},{8,16},{16,24},{1,9},{9,17},{17,25},{2,10},{10,18},{18,26},{... | collective-permute-start | bytes 786440 | tf_op jit(solution)/shard_map/ppermute | solution.py:19
  24.4 9.4 %collective-permute-start.1 = (f32[1,256,256]{2,1,0:T(8,128)S(1)}, f32[1,256,256]{2,1,0:T(8,128)S(1)}, u32[]{:S(2)}, u32[]{:S(2)}) collective-permute-start(f32[1,256,256]{2,1,0:T(8,128)S(1)} %get-tuple-element.19), channel_id=1, source_target_pairs={{1,0},{2,1},{3,2},{4,3},{5,4},{6,5},{7,6},{9,8},{10,9},{11,10},{12... | collective-permute-start | bytes 786440 | tf_op jit(solution)/shard_map/ppermute | solution.py:20
  25.7 9.4 %collective-permute-start.3 = (f32[1,256,256]{2,1,0:T(8,128)S(1)}, f32[1,256,256]{2,1,0:T(8,128)S(1)}, u32[]{:S(2)}, u32[]{:S(2)}) collective-permute-start(f32[1,256,256]{2,1,0:T(8,128)S(1)} %get-tuple-element.20), channel_id=1, source_target_pairs={{8,0},{16,8},{24,16},{9,1},{17,9},{25,17},{10,2},{18,10},{26,18},{... | collective-permute-start | bytes 786440 | tf_op jit(solution)/shard_map/ppermute | solution.py:20
  42.4 2.6 copy-start.5
  42.4 54.7 %copy-start.4 = (bf16[512,256]{1,0:T(8,128)(2,1)S(1)}, bf16[512,256]{1,0:T(8,128)(2,1)}, u32[]{:S(2)}) copy-start(bf16[512,256]{1,0:T(8,128)(2,1)} %param.13) | copy-start | bytes 786436
  81.2 82.1 %reduce-scatter.7.cloned.1.call-start = ((), (), s32[]{:S(2)}) async-start(), calls=%async_computation.4 | async-start | bytes 589824
  99.3 152.8 %all-gather.5.cloned.1.call-start = ((), (), s32[]{:S(2)}) async-start(), calls=%async_computation.3 | async-start | bytes 1310720 | tf_op jit(solution)/shard_map/all_gather | solution.py:76
  106.4 20.6 %copy-start.1 = (f32[1024,256]{1,0:T(8,128)S(1)}, f32[1024,256]{1,0:T(8,128)}, u32[]{:S(2)}) copy-start(f32[1024,256]{1,0:T(8,128)} %gather_fusion.1) | copy-start | bytes 3145732
  107.8 10.7 %collective-permute-start.4 = (f32[1,256,256]{2,1,0:T(8,128)S(1)}, f32[1,256,256]{2,1,0:T(8,128)S(1)}, u32[]{:S(2)}, u32[]{:S(2)}) collective-permute-start(f32[1,256,256]{2,1,0:T(8,128)S(1)} %get-tuple-element.13), channel_id=1, source_target_pairs={{0,1},{1,2},{2,3},{3,4},{4,5},{5,6},{6,7},{8,9},{9,10},{10,11},{11... | collective-permute-start | bytes 786440 | tf_op jit(solution)/shard_map/ppermute | solution.py:19
  111.2 10.0 %collective-permute-start.7 = (f32[1,256,256]{2,1,0:T(8,128)S(1)}, f32[1,256,256]{2,1,0:T(8,128)S(1)}, u32[]{:S(2)}, u32[]{:S(2)}) collective-permute-start(f32[1,256,256]{2,1,0:T(8,128)S(1)} %get-tuple-element.14), channel_id=1, source_target_pairs={{8,0},{16,8},{24,16},{9,1},{17,9},{25,17},{10,2},{18,10},{26,18},{... | collective-permute-start | bytes 786440 | tf_op jit(solution)/shard_map/ppermute | solution.py:20
  112.5 10.1 %collective-permute-start.6 = (f32[1,256,256]{2,1,0:T(8,128)S(1)}, f32[1,256,256]{2,1,0:T(8,128)S(1)}, u32[]{:S(2)}, u32[]{:S(2)}) collective-permute-start(f32[1,256,256]{2,1,0:T(8,128)S(1)} %get-tuple-element.15), channel_id=1, source_target_pairs={{0,8},{8,16},{16,24},{1,9},{9,17},{17,25},{2,10},{10,18},{18,26},{... | collective-permute-start | bytes 786440 | tf_op jit(solution)/shard_map/ppermute | solution.py:19
  117.0 9.9 %collective-permute-start.5 = (f32[1,256,256]{2,1,0:T(8,128)S(1)}, f32[1,256,256]{2,1,0:T(8,128)S(1)}, u32[]{:S(2)}, u32[]{:S(2)}) collective-permute-start(f32[1,256,256]{2,1,0:T(8,128)S(1)} %get-tuple-element.16), channel_id=1, source_target_pairs={{1,0},{2,1},{3,2},{4,3},{5,4},{6,5},{7,6},{9,8},{10,9},{11,10},{12... | collective-permute-start | bytes 786440 | tf_op jit(solution)/shard_map/ppermute | solution.py:20
  175.7 9.4 %collective-permute-start.8 = (f32[1,256,256]{2,1,0:T(8,128)S(1)}, f32[1,256,256]{2,1,0:T(8,128)S(1)}, u32[]{:S(2)}, u32[]{:S(2)}) collective-permute-start(f32[1,256,256]{2,1,0:T(8,128)S(1)} %get-tuple-element.9), channel_id=1, source_target_pairs={{0,1},{1,2},{2,3},{3,4},{4,5},{5,6},{6,7},{8,9},{9,10},{10,11},{11... | collective-permute-start | bytes 786440 | tf_op jit(solution)/shard_map/ppermute | solution.py:19
  178.9 7.4 %collective-permute-start.10 = (f32[1,256,256]{2,1,0:T(8,128)S(1)}, f32[1,256,256]{2,1,0:T(8,128)S(1)}, u32[]{:S(2)}, u32[]{:S(2)}) collective-permute-start(f32[1,256,256]{2,1,0:T(8,128)S(1)} %get-tuple-element.10), channel_id=1, source_target_pairs={{0,8},{8,16},{16,24},{1,9},{9,17},{17,25},{2,10},{10,18},{18,26},{... | collective-permute-start | bytes 786440 | tf_op jit(solution)/shard_map/ppermute | solution.py:19
  182.3 8.3 %collective-permute-start.9 = (f32[1,256,256]{2,1,0:T(8,128)S(1)}, f32[1,256,256]{2,1,0:T(8,128)S(1)}, u32[]{:S(2)}, u32[]{:S(2)}) collective-permute-start(f32[1,256,256]{2,1,0:T(8,128)S(1)} %get-tuple-element.11), channel_id=1, source_target_pairs={{1,0},{2,1},{3,2},{4,3},{5,4},{6,5},{7,6},{9,8},{10,9},{11,10},{12... | collective-permute-start | bytes 786440 | tf_op jit(solution)/shard_map/ppermute | solution.py:20
  183.6 8.6 %collective-permute-start.11 = (f32[1,256,256]{2,1,0:T(8,128)S(1)}, f32[1,256,256]{2,1,0:T(8,128)S(1)}, u32[]{:S(2)}, u32[]{:S(2)}) collective-permute-start(f32[1,256,256]{2,1,0:T(8,128)S(1)} %get-tuple-element.12), channel_id=1, source_target_pairs={{8,0},{16,8},{24,16},{9,1},{17,9},{25,17},{10,2},{18,10},{26,18},{... | collective-permute-start | bytes 786440 | tf_op jit(solution)/shard_map/ppermute | solution.py:20
  237.1 80.9 %reduce-scatter.9.cloned.1.call-start = ((), (), s32[]{:S(2)}) async-start(), calls=%async_computation.5 | async-start | bytes 589824
  261.3 20.6 %copy-start.2 = (f32[1024,256]{1,0:T(8,128)S(1)}, f32[1024,256]{1,0:T(8,128)}, u32[]{:S(2)}) copy-start(f32[1024,256]{1,0:T(8,128)} %gather_fusion.3) | copy-start | bytes 3145732
  262.7 10.5 %collective-permute-start.12 = (f32[1,256,256]{2,1,0:T(8,128)S(1)}, f32[1,256,256]{2,1,0:T(8,128)S(1)}, u32[]{:S(2)}, u32[]{:S(2)}) collective-permute-start(f32[1,256,256]{2,1,0:T(8,128)S(1)} %get-tuple-element.5), channel_id=1, source_target_pairs={{0,1},{1,2},{2,3},{3,4},{4,5},{5,6},{6,7},{8,9},{9,10},{10,11},{11... | collective-permute-start | bytes 786440 | tf_op jit(solution)/shard_map/ppermute | solution.py:19
  266.1 10.1 %collective-permute-start.15 = (f32[1,256,256]{2,1,0:T(8,128)S(1)}, f32[1,256,256]{2,1,0:T(8,128)S(1)}, u32[]{:S(2)}, u32[]{:S(2)}) collective-permute-start(f32[1,256,256]{2,1,0:T(8,128)S(1)} %get-tuple-element.6), channel_id=1, source_target_pairs={{8,0},{16,8},{24,16},{9,1},{17,9},{25,17},{10,2},{18,10},{26,18},{... | collective-permute-start | bytes 786440 | tf_op jit(solution)/shard_map/ppermute | solution.py:20
  267.4 10.1 %collective-permute-start.14 = (f32[1,256,256]{2,1,0:T(8,128)S(1)}, f32[1,256,256]{2,1,0:T(8,128)S(1)}, u32[]{:S(2)}, u32[]{:S(2)}) collective-permute-start(f32[1,256,256]{2,1,0:T(8,128)S(1)} %get-tuple-element.7), channel_id=1, source_target_pairs={{0,8},{8,16},{16,24},{1,9},{9,17},{17,25},{2,10},{10,18},{18,26},{... | collective-permute-start | bytes 786440 | tf_op jit(solution)/shard_map/ppermute | solution.py:19
  271.9 9.9 %collective-permute-start.13 = (f32[1,256,256]{2,1,0:T(8,128)S(1)}, f32[1,256,256]{2,1,0:T(8,128)S(1)}, u32[]{:S(2)}, u32[]{:S(2)}) collective-permute-start(f32[1,256,256]{2,1,0:T(8,128)S(1)} %get-tuple-element.8), channel_id=1, source_target_pairs={{1,0},{2,1},{3,2},{4,3},{5,4},{6,5},{7,6},{9,8},{10,9},{11,10},{12... | collective-permute-start | bytes 786440 | tf_op jit(solution)/shard_map/ppermute | solution.py:20
  (2 other events, 4.2 us)
Sparse Core Ops, SparseCore 0:
  81.3 15.7 all-gather.2
  100.4 62.7 reduce-scatter.6
  237.2 14.7 all-gather.4
  255.2 62.7 reduce-scatter.8
where the time goes:
time: 330 us; the launch traced here: 329 us
  waiting for transfers between devices  120 us (36%)
  blocking collectives  68.5 us (21%)
  local copies, waits for them, and re-layouts  54.5 us (17%)
  starting transfers between devices  41.4 us (13%)
  matrix products  19.8 us (6%)
  between operations  13.4 us (4%)
  other arithmetic  10.5 us (3%)
    all_gather x2, blocking collectives, body(): row_block = lax.all_gather(ordered, 'col', axis=0, tiled=True)  68.5 us
    unnamed x6, waiting for transfers between devices  57.4 us
    ppermute x8, starting transfers between devices, extended(): before = lax.ppermute(last, axis, up)  30.8 us
    all_gather x2, waiting for transfers between devices, body(): source = lax.all_gather(row_block, ('grp', 'row'), axis=0, tiled=True)  30.7 us
    scatter x4, local copies, waits for them, and re-layouts, place(): return blank.at[row_order].set(values.reshape(n_unknowns, n_cases))  25.1 us
    ppermute x8, waiting for transfers between devices, extended(): after = lax.ppermute(first, axis, down)  24.3 us
    gather x4, local copies, waits for them, and re-layouts, traces(): own = values[row_order].reshape(4, edge_len, n_cases)  18.7 us
    ppermute x8, starting transfers between devices, extended(): after = lax.ppermute(first, axis, down)  10.5 us
  transfers between devices with their start and end apart: 20, of which 16 were waited for; matrix products, arithmetic and copies ran while one was open for 10% of the time, Pallas kernels for 0%

commit v1 on v0

v1 whole, which is shorter than its diff:
```python
import functools

import jax
import jax.numpy as jnp
from jax import lax
from jax.experimental import pallas as pl
from jax.experimental.pallas import tpu as pltpu
from jax.sharding import PartitionSpec as P

ITERS = 2
OMEGA = 0.6
AXES = ("grp", "row", "col")
BF = jnp.bfloat16
F32 = jnp.float32
VMEM_LIMIT = 24 << 20


def dot(a, b):
    return jnp.dot(a, b, preferred_element_type=F32)


def call(kernel, outs, args, flops, scratch=(), name=None):
    moved = sum(a.size * a.dtype.itemsize for a in args)
    return pl.pallas_call(
        kernel,
        out_shape=outs,
        scratch_shapes=list(scratch),
        compiler_params=pltpu.CompilerParams(vmem_limit_bytes=VMEM_LIMIT),
        cost_estimate=pl.CostEstimate(flops=flops, transcendentals=0, bytes_accessed=moved),
        name=name,
    )(*args)


def shape(dims, dtype):
    return jax.ShapeDtypeStruct(tuple(dims), dtype)


def pairs_of(sizes, where):
    grps, rows, cols = sizes
    flat = lambda g, r, c: (g * rows + r) * cols + c
    return [
        (flat(g, r, c), flat(*where(g, r, c)))
        for g in range(grps)
        for r in range(rows)
        for c in range(cols)
    ]


def matching(sizes, odd, along_cols):
    grps, rows, cols = sizes
    count = cols if along_cols else grps * rows

    def where(g, r, c):
        at = c if along_cols else g * rows + r
        to = at + 1 if at % 2 == odd else at - 1
        if 0 <= to < count:
            return (g, r, to) if along_cols else (to // rows, to % rows, c)
        if along_cols and grps == 2:
            return (1 - g, r, c)
        if not along_cols and cols % 4 == 0:
            return (g, r, c ^ 2)
        return (g, r, c)

    return pairs_of(sizes, where)


def send(value, pairs):
    return lax.ppermute(value, AXES, pairs)


def start_kernel(n, order_ref, op_ref, u_ref, sel_ref, applied_ref, *edges):
    order = jnp.broadcast_to(order_ref[...], (128, n)).T
    lanes = lax.broadcasted_iota(jnp.int32, (n, 128), 1)
    for j in range(n // 128):
        sel_ref[:, j * 128 : (j + 1) * 128] = jnp.where(order == lanes + j * 128, 1.0, 0.0).astype(BF)
    apply_kernel(op_ref, u_ref[...], sel_ref, applied_ref, edges)


def apply_kernel(op_ref, u, sel_ref, applied_ref, edges):
    applied = dot(op_ref[...], u.astype(BF))
    applied_ref[...] = applied
    split_edges(applied, sel_ref, edges)


def split_edges(field, sel_ref, edges):
    field = field.astype(BF)
    part = field.shape[0] // 4
    for m, edge in enumerate(edges):
        edge[...] = dot(sel_ref[m * part : (m + 1) * part, :], field).astype(BF)


def tables_kernel(order_ref, basis_t_ref, slot_ref, scatter_ref, based_ref, based_t_ref):
    n = scatter_ref.shape[0]
    part = n // 4
    for m in range(4):
        cols = slice(m * part, (m + 1) * part)
        rows = lax.broadcasted_iota(jnp.int32, (n, part), 0)
        scatter_ref[:, cols] = jnp.where(rows == order_ref[:, cols], 1.0, 0.0).astype(BF)
    nb = basis_t_ref.shape[0]
    pick = lax.broadcasted_iota(jnp.int32, (nb, nb), 0) == slot_ref[...]
    based_t = dot(jnp.where(pick, 1.0, 0.0).astype(BF), basis_t_ref[...])
    based_t_ref[...] = based_t.astype(BF)
    based_ref[...] = based_t.T.astype(BF)


def shared(sizes):
    grps, rows, cols = sizes
    a = lax.axis_index("grp") * rows + lax.axis_index("row")
    c = lax.axis_index("col")

    def partner(at, count, odd):
        up = at % 2 == odd
        return jnp.where(up, at + 1 < count, at > 0)

    return [
        partner(c, cols, 0),
        partner(c, cols, 1),
        partner(a, grps * rows, 0),
        partner(a, grps * rows, 1),
    ]


def resid_kernel(sizes, load_ref, applied_ref, scatter_ref, based_t_ref, n0, n1, n2, n3, resid_ref, coarse_ref, gathered):
    part = n0.shape[0]
    for m, (there, near) in enumerate(zip(shared(sizes), (n0, n1, n2, n3))):
        gathered[m * part : (m + 1) * part, :] = jnp.where(there, near[...], jnp.zeros_like(near))
    resid = load_ref[...] - applied_ref[...] - dot(scatter_ref[...], gathered[...])
    resid = resid.astype(BF)
    resid_ref[...] = resid
    coarse_ref[...] = dot(based_t_ref[...], resid).astype(BF)


def fix_kernel(pre_ref, resid_ref, sel_ref, fix_ref, *edges):
    fix = dot(pre_ref[...], resid_ref[...])
    fix_ref[...] = fix
    split_edges(fix, sel_ref, edges)


def update(sizes, u_ref, fix_ref, scatter_ref, based_ref, own, near, mine_ref, others, gathered):
    part = own[0].shape[0]
    for m, there in enumerate(shared(sizes)):
        jump = near[m][...].astype(F32) - own[m][...].astype(F32)
        gathered[m * part : (m + 1) * part, :] = jnp.where(there, jump, 0.0).astype(BF)
    solved = mine_ref[...]
    for other in others:
        solved = solved + other[...].astype(F32)
    coarse = dot(based_ref[...], solved.astype(BF))
    smooth = fix_ref[...] + 0.5 * dot(scatter_ref[...], gathered[...])
    return u_ref[...] + OMEGA * (smooth + coarse)


def next_kernel(sizes, others, op_ref, sel_ref, u_ref, fix_ref, scatter_ref, based_ref, *refs):
    own, near, mine, rest, refs = refs[:4], refs[4:8], refs[8], refs[9 : 9 + others], refs[9 + others :]
    out_ref, applied_ref, edges, gathered = refs[0], refs[1], refs[2:6], refs[6]
    u = update(sizes, u_ref, fix_ref, scatter_ref, based_ref, own, near, mine, rest, gathered)
    out_ref[...] = u
    apply_kernel(op_ref, u, sel_ref, applied_ref, edges)


def last_kernel(sizes, others, u_ref, fix_ref, scatter_ref, based_ref, *refs):
    own, near, mine, rest, refs = refs[:4], refs[4:8], refs[8], refs[9 : 9 + others], refs[9 + others :]
    out_ref, gathered = refs
    out_ref[...] = update(sizes, u_ref, fix_ref, scatter_ref, based_ref, own, near, mine, rest, gathered)


def regroup_kernel(geometry, nb, inverse_ref, *blocks):
    grid_rows, ratio, lines = geometry
    c = lax.axis_index("col")
    owner = c // ratio
    for k, block in enumerate(blocks):
        target = k ^ owner
        parity, pair = target % 2, target // 2
        for line in range(lines):
            rows = pl.ds(pl.multiple_of((2 * line + parity) * nb, nb), nb)
            cols = pl.ds(pl.multiple_of(pair * 2 * nb, 2 * nb), 2 * nb)
            block[line * nb : (line + 1) * nb, :] = inverse_ref[rows, cols]


def coarse_kernel(geometry, row_size, nb, moves, *refs):
    grid_rows, ratio, lines = geometry
    blocks, refs = refs[:grid_rows], refs[grid_rows:]
    vectors, refs = refs[: len(moves)], refs[len(moves) :]
    mine_ref, others, (stack, total) = refs[0], refs[1:lines], refs[lines:]
    g, r, c = (lax.axis_index(axis) for axis in AXES)
    for (dg, dr, dc), vector in zip(moves, vectors):
        at = (((g ^ dg) * row_size + (r ^ dr)) * 2 + ((c % 2) ^ dc)) * nb
        stack[pl.ds(pl.multiple_of(at, nb), nb), :] = vector[...]
    acc = None
    for k, block in enumerate(blocks):
        owner = k ^ (c % grid_rows)
        part = dot(block[...], stack[pl.ds(pl.multiple_of(owner * 2 * nb, 2 * nb), 2 * nb), :])
        acc = part if acc is None else acc + part
    total[...] = acc
    line = c // 2
    for k in range(lines):
        got = total[pl.ds(pl.multiple_of((line ^ k) * nb, nb), nb), :]
        if k == 0:
            mine_ref[...] = got
        else:
            others[k - 1][...] = got.astype(BF)


def body(load, guess, interface_op, precond, basis, coarse_inverse, edge_rows, coarse_slot):
    sizes = tuple(lax.axis_size(axis) for axis in AXES)
    grps, row_size, cols = sizes
    grid_rows = grps * row_size
    load, u, op, pre = load[0, 0], guess[0, 0], interface_op[0, 0], precond[0, 0]
    basis_t = jnp.swapaxes(basis[0, 0], 0, 1)
    slot = coarse_slot[0]
    n, cases = load.shape
    nb = basis_t.shape[0]
    part = n // 4
    ratio, lines = cols // grid_rows, cols // 2
    geometry = (grid_rows, ratio, lines)

    a = lax.axis_index("grp") * row_size + lax.axis_index("row")
    c = lax.axis_index("col")
    lists = edge_rows[0, 0].reshape(4, part)
    west, east, south, north = (lists[k] for k in range(4))
    even_c, even_a = c % 2 == 0, a % 2 == 0
    order = jnp.concatenate(
        [
            jnp.where(even_c, east, west),
            jnp.where(even_c, west, east),
            jnp.where(even_a, north, south),
            jnp.where(even_a, south, north),
        ]
    ).reshape(1, n)

    halo_pairs = [
        matching(sizes, 0, True),
        matching(sizes, 1, True),
        matching(sizes, 0, False),
        matching(sizes, 1, False),
    ]
    moves = [
        (dg, dr, dc) for dr in range(row_size) for dc in range(2) for dg in range(grps)
    ]

    def swap_pairs(dg, dr, dc):
        return pairs_of(sizes, lambda g, r, c: (g ^ dg, r ^ dr, c ^ dc))

    field = shape((n, cases), F32)
    edge = shape((part, cases), BF)
    square = shape((n, n), BF)
    flops = 2 * n * n * cases

    sel, applied, *edges = call(
        functools.partial(start_kernel, n), [square, field] + [edge] * 4, [order, op, u], 2 * flops, name="start"
    )
    near = [send(e, p) for e, p in zip(edges, halo_pairs)]
    scatter, based, based_t = call(
        tables_kernel,
        [square, shape((n, nb), BF), shape((nb, n), BF)],
        [order, basis_t, slot],
        n * n,
        name="tables",
    )
    blocks = call(
        functools.partial(regroup_kernel, geometry, nb),
        [shape((lines * nb, 2 * nb), BF)] * grid_rows,
        [coarse_inverse],
        n,
        name="regroup",
    )

    def target(k):
        return pairs_of(sizes, lambda g, r, c: (g, r, (c % ratio) * grid_rows + (k ^ (c // ratio))))

    blocks = [send(block, target(k)) for k, block in enumerate(blocks)]

    gathered = [pltpu.VMEM((n, cases), BF)]
    for sweep in range(ITERS):
        resid, coarse = call(
            functools.partial(resid_kernel, sizes),
            [shape((n, cases), BF), shape((nb, cases), BF)],
            [load, applied, scatter, based_t, *near],
            flops,
            gathered,
            name="resid",
        )
        vectors = {}
        for dr in range(row_size):
            for dc in range(2):
                far = coarse if (dr, dc) == (0, 0) else send(coarse, swap_pairs(0, dr, dc))
                vectors[0, dr, dc] = far
        for dr in range(row_size):
            for dc in range(2):
                for dg in range(1, grps):
                    vectors[dg, dr, dc] = send(vectors[0, dr, dc], swap_pairs(dg, 0, 0))
        fix, *own = call(
            fix_kernel, [field] + [edge] * 4, [pre, resid, sel], 2 * flops, name="fix"
        )
        near = [send(e, p) for e, p in zip(own, halo_pairs)]
        mine, *others = call(
            functools.partial(coarse_kernel, geometry, row_size, nb, moves),
            [shape((nb, cases), F32)] + [shape((nb, cases), BF)] * (lines - 1),
            [*blocks, *(vectors[move] for move in moves)],
            2 * lines * nb * 2 * nb * grid_rows * cases,
            [pltpu.VMEM((2 * grid_rows * nb, cases), BF), pltpu.VMEM((lines * nb, cases), F32)],
            name="coarse",
        )
        others = [send(o, swap_pairs(0, 0, 2 * (k + 1))) for k, o in enumerate(others)]
        args = [u, fix, scatter, based, *own, *near, mine, *others]
        if sweep < ITERS - 1:
            u, applied, *edges = call(
                functools.partial(next_kernel, sizes, len(others)),
                [field, field] + [edge] * 4,
                [op, sel, *args],
                3 * flops,
                gathered,
                name="next",
            )
            near = [send(e, p) for e, p in zip(edges, halo_pairs)]
        else:
            u = call(functools.partial(last_kernel, sizes, len(others)), field, args, flops, gathered, name="last")
    return u[None, None]


def solution(mesh):
    cells = P(("grp", "row"), "col", None, None)
    lists = P(("grp", "row"), "col", None)
    return jax.shard_map(
        body,
        mesh=mesh,
        in_specs=(cells, cells, cells, cells, cells, P(("grp", "row"), "col"), lists, lists),
        out_specs=cells,
        check_vma=False,
    )
```

time: 330 us -> 95.5 us (0.29)
  waiting for transfers between devices: 120 us -> 27.7 us
  blocking collectives: 68.5 us -> 0 us
  local copies, waits for them, and re-layouts: 54.5 us -> 2.84 us
  matrix products: 19.8 us -> 0 us
  Pallas kernels: 0 us -> 15.4 us
  between operations: 13.4 us -> 0.25 us
  other arithmetic: 10.5 us -> 0.74 us
  starting transfers between devices: 41.4 us -> 48.3 us
    all_gather x2 -> x0, blocking collectives: 68.5 us -> none  [body(): row_block = lax.all_gather(ordered, 'col', axis=0, tiled=True)]
    unnamed x6 -> x0, waiting for transfers between devices: 57.4 us -> none
    all_gather x2 -> x0, waiting for transfers between devices: 30.7 us -> none  [body(): source = lax.all_gather(row_block, ('grp', 'row'), axis=0, tiled=True)]
    scatter x4 -> x0, local copies, waits for them, and re-layouts: 25.1 us -> none  [place(): return blank.at[row_order].set(values.reshape(n_unknowns, n_cases))]
    dot_general x10 -> x0, matrix products: 19.8 us -> none  [the longest x2 6.05 us: body(): jnp.dot(basis_block, picked, preferred_element_type=jnp.float32)]
    gather x4 -> x0, local copies, waits for them, and re-layouts: 18.7 us -> none  [traces(): own = values[row_order].reshape(4, edge_len, n_cases)]
    pallas_call x0 -> x11, Pallas kernels: none -> 15.4 us  [call(): pl.pallas_call(kernel, out_shape=outs, scratch_shapes=list(scratch), comp...]
    ppermute x16 -> x40, starting transfers between devices: 41.3 us -> 48.3 us  [send(): return lax.ppermute(value, AXES, pairs)]
  transfers between devices with their start and end apart: 20 -> 40, of which waited for: 16 -> 15; matrix products, arithmetic and copies ran while one was open for 10% -> 0% of each run, Pallas kernels for 0% -> 8%
where the time goes in v1:
time: 95.5 us; the launch traced here: 95.2 us
  starting transfers between devices  48.3 us (51%)
  waiting for transfers between devices  27.7 us (29%)
  Pallas kernels  15.4 us (16%)
  local copies, waits for them, and re-layouts  2.84 us (3%)
    ppermute x40, starting transfers between devices, send(): return lax.ppermute(value, AXES, pairs)  48.3 us
    ppermute x40, waiting for transfers between devices, send(): return lax.ppermute(value, AXES, pairs)  27.7 us
    pallas_call x11, Pallas kernels, call(): pl.pallas_call(kernel, out_shape=outs, scratch_shapes=list(scratch), comp...  15.4 us
    unnamed x18, local copies, waits for them, and re-layouts  2.84 us
  transfers between devices with their start and end apart: 40, of which 15 were waited for; matrix products, arithmetic and copies ran while one was open for 0% of the time, Pallas kernels for 8%

profile of v1, /device:TPU:0, one launch (start us, length us, event | category | flops | bytes accessed | tf_op | source)
XLA Modules:
  0.0 95.2 jit_solution(3035989010313998475)
XLA Ops:
  3.6 2.3 %start.1 = (bf16[1024,1024]{1,0:T(8,128)(2,1)S(1)}, f32[1024,256]{1,0:T(8,128)S(1)}, bf16[256,256]{1,0:T(8,128)(2,1)S(1)}, bf16[256,256]{1,0:T(8,128)(2,1)S(1)},...) custom-call(s32[1,1024]{1,0:T(1,128)S(1)} %bitcast.23, bf16[1024,1024]{1,0:T(8,128)(2,1)S(1)} %bitcast.18, ...), custom_call_target="tpu_custom_call" | custom-call | flops 1073741824 | bytes 3149824 | tf_op jit(solution)/shard_map/start/pallas_call | solution.py:24
  5.9 3.0 %collective-permute-start = (bf16[256,256]{1,0:T(8,128)(2,1)S(1)}, bf16[256,256]{1,0:T(8,128)(2,1)S(1)}, u32[]{:S(2)}, u32[]{:S(2)}) collective-permute-start(bf16[256,256]{1,0:T(8,128)(2,1)S(1)} %get-tuple-element.50), channel_id=1, source_target_pairs={{0,1},{1,0},{2,3},{3,2},{4,5},{5,4},{6,7},{7,6},{8,9},{9,8},{10,11... | collective-permute-start | bytes 393224 | tf_op jit(solution)/shard_map/ppermute | solution.py:68
  10.5 2.0 %collective-permute-start.3 = (bf16[256,256]{1,0:T(8,128)(2,1)S(1)}, bf16[256,256]{1,0:T(8,128)(2,1)S(1)}, u32[]{:S(2)}, u32[]{:S(2)}) collective-permute-start(bf16[256,256]{1,0:T(8,128)(2,1)S(1)} %get-tuple-element.53), channel_id=1, source_target_pairs={{0,2},{1,3},{2,0},{3,1},{4,6},{5,7},{6,4},{7,5},{8,16},{9,17},{10,... | collective-permute-start | bytes 393224 | tf_op jit(solution)/shard_map/ppermute | solution.py:68
  14.5 5.3 %collective-permute-start.9 = (bf16[256,128]{1,0:T(8,128)(2,1)S(1)}, bf16[256,128]{1,0:T(8,128)(2,1)S(1)}, u32[]{:S(2)}, u32[]{:S(2)}) collective-permute-start(bf16[256,128]{1,0:T(8,128)(2,1)S(1)} %get-tuple-element.62), channel_id=1, source_target_pairs={{0,1},{1,5},{2,0},{3,4},{4,3},{5,7},{6,2},{7,6},{8,9},{9,13},{10,8... | collective-permute-start | bytes 196616 | tf_op jit(solution)/shard_map/ppermute | solution.py:68
  20.9 2.4 %collective-permute-start.17 = (bf16[64,256]{1,0:T(8,128)(2,1)S(1)}, bf16[64,256]{1,0:T(8,128)(2,1)S(1)}, u32[]{:S(2)}, u32[]{:S(2)}) collective-permute-start(bf16[64,256]{1,0:T(8,128)(2,1)S(1)} %get-tuple-element.65.refs_4_), channel_id=1, source_target_pairs={{0,9},{1,8},{2,11},{3,10},{4,13},{5,12},{6,15},{7,14},{8,1},{9,0},... | collective-permute-start | bytes 98312 | tf_op jit(solution)/shard_map/ppermute | solution.py:68
  23.3 2.9 %collective-permute-start.15 = (bf16[64,256]{1,0:T(8,128)(2,1)S(1)}, bf16[64,256]{1,0:T(8,128)(2,1)S(1)}, u32[]{:S(2)}, u32[]{:S(2)}) collective-permute-start(bf16[64,256]{1,0:T(8,128)(2,1)S(1)} %get-tuple-element.65.refs_4_), channel_id=1, source_target_pairs={{0,8},{1,9},{2,10},{3,11},{4,12},{5,13},{6,14},{7,15},{8,0},{9,1},... | collective-permute-start | bytes 98312 | tf_op jit(solution)/shard_map/ppermute | solution.py:68
  26.2 3.1 %collective-permute-start.11 = (bf16[256,128]{1,0:T(8,128)(2,1)S(1)}, bf16[256,128]{1,0:T(8,128)(2,1)S(1)}, u32[]{:S(2)}, u32[]{:S(2)}) collective-permute-start(bf16[256,128]{1,0:T(8,128)(2,1)S(1)} %get-tuple-element.64), channel_id=1, source_target_pairs={{0,3},{1,7},{2,2},{3,6},{4,1},{5,5},{6,0},{7,4},{8,11},{9,15},{10,... | collective-permute-start | bytes 196616 | tf_op jit(solution)/shard_map/ppermute | solution.py:68
  30.4 2.2 %fix.2 = (f32[1024,256]{1,0:T(8,128)S(1)}, bf16[256,256]{1,0:T(8,128)(2,1)S(1)}, bf16[256,256]{1,0:T(8,128)(2,1)S(1)}, bf16[256,256]{1,0:T(8,128)(2,1)S(1)}, bf16[256,256]{1,0:T(8,128)(2,1)S(1)}) custom-call(bf16[1024,1024]{1,0:T(8,128)(2,1)S(1)} %bitcast.14, bf16[1024,256]{1,0:T(8,128)(2,1)S(1)} %get-tuple-element.54.resid_ref, ...), custom_call_target="tpu_custom_call" | custom-call | flops 1073741824 | bytes 4718592 | tf_op jit(solution)/shard_map/fix/pallas_call | solution.py:24
  34.2 2.2 %collective-permute-start.4 = (bf16[256,256]{1,0:T(8,128)(2,1)S(1)}, bf16[256,256]{1,0:T(8,128)(2,1)S(1)}, u32[]{:S(2)}, u32[]{:S(2)}) collective-permute-start(bf16[256,256]{1,0:T(8,128)(2,1)S(1)} %get-tuple-element.57.refs_0_), channel_id=1, source_target_pairs={{0,1},{1,0},{2,3},{3,2},{4,5},{5,4},{6,7},{7,6},{8,9},{9,8},{10,11... | collective-permute-start | bytes 393224 | tf_op jit(solution)/shard_map/ppermute | solution.py:68
  39.4 3.5 %collective-permute-done.19.refs_9_ = bf16[64,256]{1,0:T(8,128)(2,1)S(1)} collective-permute-done((bf16[64,256]{1,0:T(8,128)(2,1)S(1)}, bf16[64,256]{1,0:T(8,128)(2,1)S(1)}, u32[]{:S(2)}, u32[]{:S(2)}) %collective-permute-start.19) | collective-permute-done | bytes 32800 | tf_op jit(solution)/shard_map/ppermute | solution.py:68
  42.9 2.0 %collective-permute-start.20 = (bf16[64,256]{1,0:T(8,128)(2,1)S(1)}, bf16[64,256]{1,0:T(8,128)(2,1)S(1)}, u32[]{:S(2)}, u32[]{:S(2)}) collective-permute-start(bf16[64,256]{1,0:T(8,128)(2,1)S(1)} %get-tuple-element.68), channel_id=1, source_target_pairs={{0,4},{1,5},{2,6},{3,7},{4,0},{5,1},{6,2},{7,3},{8,12},{9,13},{10,... | collective-permute-start | bytes 98312 | tf_op jit(solution)/shard_map/ppermute | solution.py:68
  44.9 2.8 %collective-permute-done.20.refs_10_ = bf16[64,256]{1,0:T(8,128)(2,1)S(1)} collective-permute-done((bf16[64,256]{1,0:T(8,128)(2,1)S(1)}, bf16[64,256]{1,0:T(8,128)(2,1)S(1)}, u32[]{:S(2)}, u32[]{:S(2)}) %collective-permute-start.20) | collective-permute-done | bytes 32800 | tf_op jit(solution)/shard_map/ppermute | solution.py:68
  47.7 1.8 %collective-permute-start.21 = (bf16[64,256]{1,0:T(8,128)(2,1)S(1)}, bf16[64,256]{1,0:T(8,128)(2,1)S(1)}, u32[]{:S(2)}, u32[]{:S(2)}) collective-permute-start(bf16[64,256]{1,0:T(8,128)(2,1)S(1)} %get-tuple-element.69), channel_id=1, source_target_pairs={{0,6},{1,7},{2,4},{3,5},{4,2},{5,3},{6,0},{7,1},{8,14},{9,15},{10,... | collective-permute-start | bytes 98312 | tf_op jit(solution)/shard_map/ppermute | solution.py:68
  49.5 3.9 %collective-permute-done.21.refs_11_ = bf16[64,256]{1,0:T(8,128)(2,1)S(1)} collective-permute-done((bf16[64,256]{1,0:T(8,128)(2,1)S(1)}, bf16[64,256]{1,0:T(8,128)(2,1)S(1)}, u32[]{:S(2)}, u32[]{:S(2)}) %collective-permute-start.21) | collective-permute-done | bytes 32800 | tf_op jit(solution)/shard_map/ppermute | solution.py:68
  53.4 2.9 %next.1 = (f32[1024,256]{1,0:T(8,128)S(1)}, f32[1024,256]{1,0:T(8,128)S(1)}, bf16[256,256]{1,0:T(8,128)(2,1)S(1)}, bf16[256,256]{1,0:T(8,128)(2,1)S(1)}, bf16[25...) custom-call(bf16[1024,1024]{1,0:T(8,128)(2,1)S(1)} %bitcast.19, bf16[1024,1024]{1,0:T(8,128)(2,1)S(1)} %get-tuple-element.46.sel_ref, ...), custom_call_target="tpu_custom_call" | custom-call | flops 1610612736 | bytes 9732096 | tf_op jit(solution)/shard_map/next/pallas_call | solution.py:24
  57.5 3.3 %collective-permute-start.25 = (bf16[256,256]{1,0:T(8,128)(2,1)S(1)}, bf16[256,256]{1,0:T(8,128)(2,1)S(1)}, u32[]{:S(2)}, u32[]{:S(2)}) collective-permute-start(bf16[256,256]{1,0:T(8,128)(2,1)S(1)} %get-tuple-element.75), channel_id=1, source_target_pairs={{0,2},{1,3},{2,0},{3,1},{4,6},{5,7},{6,4},{7,5},{8,16},{9,17},{10,... | collective-permute-start | bytes 393224 | tf_op jit(solution)/shard_map/ppermute | solution.py:68
  66.8 2.0 %collective-permute-start.31 = (bf16[64,256]{1,0:T(8,128)(2,1)S(1)}, bf16[64,256]{1,0:T(8,128)(2,1)S(1)}, u32[]{:S(2)}, u32[]{:S(2)}) collective-permute-start(bf16[64,256]{1,0:T(8,128)(2,1)S(1)} %get-tuple-element.82.refs_4_), channel_id=1, source_target_pairs={{0,1},{1,0},{2,3},{3,2},{4,5},{5,4},{6,7},{7,6},{8,9},{9,8},{10,11... | collective-permute-start | bytes 98312 | tf_op jit(solution)/shard_map/ppermute | solution.py:68
  71.1 2.2 %fix.3 = (f32[1024,256]{1,0:T(8,128)S(1)}, bf16[256,256]{1,0:T(8,128)(2,1)S(1)}, bf16[256,256]{1,0:T(8,128)(2,1)S(1)}, bf16[256,256]{1,0:T(8,128)(2,1)S(1)}, bf16[256,256]{1,0:T(8,128)(2,1)S(1)}) custom-call(bf16[1024,1024]{1,0:T(8,128)(2,1)S(1)} %bitcast.15, bf16[1024,256]{1,0:T(8,128)(2,1)S(1)} %get-tuple-element.76.resid_ref, ...), custom_call_target="tpu_custom_call" | custom-call | flops 1073741824 | bytes 4718592 | tf_op jit(solution)/shard_map/fix/pallas_call | solution.py:24
  75.7 2.8 %collective-permute-start.29 = (bf16[256,256]{1,0:T(8,128)(2,1)S(1)}, bf16[256,256]{1,0:T(8,128)(2,1)S(1)}, u32[]{:S(2)}, u32[]{:S(2)}) collective-permute-start(bf16[256,256]{1,0:T(8,128)(2,1)S(1)} %get-tuple-element.81.refs_3_), channel_id=1, source_target_pairs={{0,2},{1,3},{2,0},{3,1},{4,6},{5,7},{6,4},{7,5},{8,16},{9,17},{10,... | collective-permute-start | bytes 393224 | tf_op jit(solution)/shard_map/ppermute | solution.py:68
  78.9 3.9 %collective-permute-done.37.refs_9_ = bf16[64,256]{1,0:T(8,128)(2,1)S(1)} collective-permute-done((bf16[64,256]{1,0:T(8,128)(2,1)S(1)}, bf16[64,256]{1,0:T(8,128)(2,1)S(1)}, u32[]{:S(2)}, u32[]{:S(2)}) %collective-permute-start.37) | collective-permute-done | bytes 32800 | tf_op jit(solution)/shard_map/ppermute | solution.py:68
  84.5 3.1 %collective-permute-done.38.refs_10_ = bf16[64,256]{1,0:T(8,128)(2,1)S(1)} collective-permute-done((bf16[64,256]{1,0:T(8,128)(2,1)S(1)}, bf16[64,256]{1,0:T(8,128)(2,1)S(1)}, u32[]{:S(2)}, u32[]{:S(2)}) %collective-permute-start.38) | collective-permute-done | bytes 32800 | tf_op jit(solution)/shard_map/ppermute | solution.py:68
  87.6 2.4 %collective-permute-start.39 = (bf16[64,256]{1,0:T(8,128)(2,1)S(1)}, bf16[64,256]{1,0:T(8,128)(2,1)S(1)}, u32[]{:S(2)}, u32[]{:S(2)}) collective-permute-start(bf16[64,256]{1,0:T(8,128)(2,1)S(1)} %get-tuple-element.86), channel_id=1, source_target_pairs={{0,6},{1,7},{2,4},{3,5},{4,2},{5,3},{6,0},{7,1},{8,14},{9,15},{10,... | collective-permute-start | bytes 98312 | tf_op jit(solution)/shard_map/ppermute | solution.py:68
  90.0 3.3 %collective-permute-done.39.refs_11_ = bf16[64,256]{1,0:T(8,128)(2,1)S(1)} collective-permute-done((bf16[64,256]{1,0:T(8,128)(2,1)S(1)}, bf16[64,256]{1,0:T(8,128)(2,1)S(1)}, u32[]{:S(2)}, u32[]{:S(2)}) %collective-permute-start.39) | collective-permute-done | bytes 32800 | tf_op jit(solution)/shard_map/ppermute | solution.py:68
  93.3 1.9 %last.1 = f32[1024,256]{1,0:T(8,128)} custom-call(f32[1024,256]{1,0:T(8,128)S(1)} %get-tuple-element.70.u_ref, f32[1024,256]{1,0:T(8,128)S(1)} %get-tuple-element.77.fix_ref, bf16[1024,1024]{1,0:T(8,128)(2,1)S(1)} %get-tuple-element.48.scatter_ref, bf16[1024,64]{1,0:T(8,128)(2,1)S(1)} %get-tuple-element.56.based_ref, ...), custom_call_target="tpu_custom_call" | custom-call | flops 536870912 | bytes 5537792 | tf_op jit(solution)/shard_map/last/pallas_call | solution.py:24
  (87 shorter events, 27.8 us)
Async XLA Ops:
  5.9 8.6 %collective-permute-start = (bf16[256,256]{1,0:T(8,128)(2,1)S(1)}, bf16[256,256]{1,0:T(8,128)(2,1)S(1)}, u32[]{:S(2)}, u32[]{:S(2)}) collective-permute-start(bf16[256,256]{1,0:T(8,128)(2,1)S(1)} %get-tuple-element.50), channel_id=1, source_target_pairs={{0,1},{1,0},{2,3},{3,2},{4,5},{5,4},{6,7},{7,6},{8,9},{9,8},{10,11... | collective-permute-start | bytes 393224 | tf_op jit(solution)/shard_map/ppermute | solution.py:68
  9.0 10.9 %collective-permute-start.1 = (bf16[256,256]{1,0:T(8,128)(2,1)S(1)}, bf16[256,256]{1,0:T(8,128)(2,1)S(1)}, u32[]{:S(2)}, u32[]{:S(2)}) collective-permute-start(bf16[256,256]{1,0:T(8,128)(2,1)S(1)} %get-tuple-element.51), channel_id=1, source_target_pairs={{0,16},{1,2},{2,1},{3,4},{4,3},{5,6},{6,5},{7,23},{8,24},{9,10},{1... | collective-permute-start | bytes 393224 | tf_op jit(solution)/shard_map/ppermute | solution.py:68
  9.0 11.0 %collective-permute-start.2 = (bf16[256,256]{1,0:T(8,128)(2,1)S(1)}, bf16[256,256]{1,0:T(8,128)(2,1)S(1)}, u32[]{:S(2)}, u32[]{:S(2)}) collective-permute-start(bf16[256,256]{1,0:T(8,128)(2,1)S(1)} %get-tuple-element.52), channel_id=1, source_target_pairs={{0,8},{1,9},{2,10},{3,11},{4,12},{5,13},{6,14},{7,15},{8,0},{9,1},... | collective-permute-start | bytes 393224 | tf_op jit(solution)/shard_map/ppermute | solution.py:68
  10.5 9.4 %collective-permute-start.3 = (bf16[256,256]{1,0:T(8,128)(2,1)S(1)}, bf16[256,256]{1,0:T(8,128)(2,1)S(1)}, u32[]{:S(2)}, u32[]{:S(2)}) collective-permute-start(bf16[256,256]{1,0:T(8,128)(2,1)S(1)} %get-tuple-element.53), channel_id=1, source_target_pairs={{0,2},{1,3},{2,0},{3,1},{4,6},{5,7},{6,4},{7,5},{8,16},{9,17},{10,... | collective-permute-start | bytes 393224 | tf_op jit(solution)/shard_map/ppermute | solution.py:68
  12.6 13.6 %collective-permute-start.8 = (bf16[256,128]{1,0:T(8,128)(2,1)S(1)}, bf16[256,128]{1,0:T(8,128)(2,1)S(1)}, u32[]{:S(2)}, u32[]{:S(2)}) collective-permute-start(bf16[256,128]{1,0:T(8,128)(2,1)S(1)} %get-tuple-element.61), channel_id=1, source_target_pairs={{0,0},{1,4},{2,1},{3,5},{4,2},{5,6},{6,3},{7,7},{8,8},{9,12},{10,9... | collective-permute-start | bytes 196616 | tf_op jit(solution)/shard_map/ppermute | solution.py:68
  14.5 11.7 %collective-permute-start.9 = (bf16[256,128]{1,0:T(8,128)(2,1)S(1)}, bf16[256,128]{1,0:T(8,128)(2,1)S(1)}, u32[]{:S(2)}, u32[]{:S(2)}) collective-permute-start(bf16[256,128]{1,0:T(8,128)(2,1)S(1)} %get-tuple-element.62), channel_id=1, source_target_pairs={{0,1},{1,5},{2,0},{3,4},{4,3},{5,7},{6,2},{7,6},{8,9},{9,13},{10,8... | collective-permute-start | bytes 196616 | tf_op jit(solution)/shard_map/ppermute | solution.py:68
  19.8 9.5 %collective-permute-start.10 = (bf16[256,128]{1,0:T(8,128)(2,1)S(1)}, bf16[256,128]{1,0:T(8,128)(2,1)S(1)}, u32[]{:S(2)}, u32[]{:S(2)}) collective-permute-start(bf16[256,128]{1,0:T(8,128)(2,1)S(1)} %get-tuple-element.63), channel_id=1, source_target_pairs={{0,2},{1,6},{2,3},{3,7},{4,0},{5,4},{6,1},{7,5},{8,10},{9,14},{10,... | collective-permute-start | bytes 196616 | tf_op jit(solution)/shard_map/ppermute | solution.py:68
  20.9 8.5 %collective-permute-start.17 = (bf16[64,256]{1,0:T(8,128)(2,1)S(1)}, bf16[64,256]{1,0:T(8,128)(2,1)S(1)}, u32[]{:S(2)}, u32[]{:S(2)}) collective-permute-start(bf16[64,256]{1,0:T(8,128)(2,1)S(1)} %get-tuple-element.65.refs_4_), channel_id=1, source_target_pairs={{0,9},{1,8},{2,11},{3,10},{4,13},{5,12},{6,15},{7,14},{8,1},{9,0},... | collective-permute-start | bytes 98312 | tf_op jit(solution)/shard_map/ppermute | solution.py:68
  23.3 6.6 %collective-permute-start.15 = (bf16[64,256]{1,0:T(8,128)(2,1)S(1)}, bf16[64,256]{1,0:T(8,128)(2,1)S(1)}, u32[]{:S(2)}, u32[]{:S(2)}) collective-permute-start(bf16[64,256]{1,0:T(8,128)(2,1)S(1)} %get-tuple-element.65.refs_4_), channel_id=1, source_target_pairs={{0,8},{1,9},{2,10},{3,11},{4,12},{5,13},{6,14},{7,15},{8,0},{9,1},... | collective-permute-start | bytes 98312 | tf_op jit(solution)/shard_map/ppermute | solution.py:68
  26.2 8.0 %collective-permute-start.11 = (bf16[256,128]{1,0:T(8,128)(2,1)S(1)}, bf16[256,128]{1,0:T(8,128)(2,1)S(1)}, u32[]{:S(2)}, u32[]{:S(2)}) collective-permute-start(bf16[256,128]{1,0:T(8,128)(2,1)S(1)} %get-tuple-element.64), channel_id=1, source_target_pairs={{0,3},{1,7},{2,2},{3,6},{4,1},{5,5},{6,0},{7,4},{8,11},{9,15},{10,... | collective-permute-start | bytes 196616 | tf_op jit(solution)/shard_map/ppermute | solution.py:68
  29.3 7.0 %collective-permute-start.12 = (bf16[64,256]{1,0:T(8,128)(2,1)S(1)}, bf16[64,256]{1,0:T(8,128)(2,1)S(1)}, u32[]{:S(2)}, u32[]{:S(2)}) collective-permute-start(bf16[64,256]{1,0:T(8,128)(2,1)S(1)} %get-tuple-element.65.refs_4_), channel_id=1, source_target_pairs={{0,16},{1,17},{2,18},{3,19},{4,20},{5,21},{6,22},{7,23},{8,24},{9,... | collective-permute-start | bytes 98312 | tf_op jit(solution)/shard_map/ppermute | solution.py:68
  29.4 6.9 %collective-permute-start.18 = (bf16[64,256]{1,0:T(8,128)(2,1)S(1)}, bf16[64,256]{1,0:T(8,128)(2,1)S(1)}, u32[]{:S(2)}, u32[]{:S(2)}) collective-permute-start(bf16[64,256]{1,0:T(8,128)(2,1)S(1)} %collective-permute-done.17.refs_10_), channel_id=1, source_target_pairs={{0,16},{1,17},{2,18},{3,19},{4,20},{5,21},{6,22},{7,23},{8,24},{9,... | collective-permute-start | bytes 98312 | tf_op jit(solution)/shard_map/ppermute | solution.py:68
  29.9 7.1 %collective-permute-start.16 = (bf16[64,256]{1,0:T(8,128)(2,1)S(1)}, bf16[64,256]{1,0:T(8,128)(2,1)S(1)}, u32[]{:S(2)}, u32[]{:S(2)}) collective-permute-start(bf16[64,256]{1,0:T(8,128)(2,1)S(1)} %collective-permute-done.15.refs_8_), channel_id=1, source_target_pairs={{0,16},{1,17},{2,18},{3,19},{4,20},{5,21},{6,22},{7,23},{8,24},{9,... | collective-permute-start | bytes 98312 | tf_op jit(solution)/shard_map/ppermute | solution.py:68
  30.1 8.3 %collective-permute-start.14 = (bf16[64,256]{1,0:T(8,128)(2,1)S(1)}, bf16[64,256]{1,0:T(8,128)(2,1)S(1)}, u32[]{:S(2)}, u32[]{:S(2)}) collective-permute-start(bf16[64,256]{1,0:T(8,128)(2,1)S(1)} %collective-permute-done.13.refs_6_), channel_id=1, source_target_pairs={{0,16},{1,17},{2,18},{3,19},{4,20},{5,21},{6,22},{7,23},{8,24},{9,... | collective-permute-start | bytes 98312 | tf_op jit(solution)/shard_map/ppermute | solution.py:68
  34.2 19.3 %collective-permute-start.4 = (bf16[256,256]{1,0:T(8,128)(2,1)S(1)}, bf16[256,256]{1,0:T(8,128)(2,1)S(1)}, u32[]{:S(2)}, u32[]{:S(2)}) collective-permute-start(bf16[256,256]{1,0:T(8,128)(2,1)S(1)} %get-tuple-element.57.refs_0_), channel_id=1, source_target_pairs={{0,1},{1,0},{2,3},{3,2},{4,5},{5,4},{6,7},{7,6},{8,9},{9,8},{10,11... | collective-permute-start | bytes 393224 | tf_op jit(solution)/shard_map/ppermute | solution.py:68
  36.3 17.1 %collective-permute-start.5 = (bf16[256,256]{1,0:T(8,128)(2,1)S(1)}, bf16[256,256]{1,0:T(8,128)(2,1)S(1)}, u32[]{:S(2)}, u32[]{:S(2)}) collective-permute-start(bf16[256,256]{1,0:T(8,128)(2,1)S(1)} %get-tuple-element.58.refs_1_), channel_id=1, source_target_pairs={{0,16},{1,2},{2,1},{3,4},{4,3},{5,6},{6,5},{7,23},{8,24},{9,10},{1... | collective-permute-start | bytes 393224 | tf_op jit(solution)/shard_map/ppermute | solution.py:68
  36.3 17.1 %collective-permute-start.6 = (bf16[256,256]{1,0:T(8,128)(2,1)S(1)}, bf16[256,256]{1,0:T(8,128)(2,1)S(1)}, u32[]{:S(2)}, u32[]{:S(2)}) collective-permute-start(bf16[256,256]{1,0:T(8,128)(2,1)S(1)} %get-tuple-element.59.refs_2_), channel_id=1, source_target_pairs={{0,8},{1,9},{2,10},{3,11},{4,12},{5,13},{6,14},{7,15},{8,0},{9,1},... | collective-permute-start | bytes 393224 | tf_op jit(solution)/shard_map/ppermute | solution.py:68
  36.9 16.5 %collective-permute-start.7 = (bf16[256,256]{1,0:T(8,128)(2,1)S(1)}, bf16[256,256]{1,0:T(8,128)(2,1)S(1)}, u32[]{:S(2)}, u32[]{:S(2)}) collective-permute-start(bf16[256,256]{1,0:T(8,128)(2,1)S(1)} %get-tuple-element.60.refs_3_), channel_id=1, source_target_pairs={{0,2},{1,3},{2,0},{3,1},{4,6},{5,7},{6,4},{7,5},{8,16},{9,17},{10,... | collective-permute-start | bytes 393224 | tf_op jit(solution)/shard_map/ppermute | solution.py:68
  57.5 6.8 %collective-permute-start.25 = (bf16[256,256]{1,0:T(8,128)(2,1)S(1)}, bf16[256,256]{1,0:T(8,128)(2,1)S(1)}, u32[]{:S(2)}, u32[]{:S(2)}) collective-permute-start(bf16[256,256]{1,0:T(8,128)(2,1)S(1)} %get-tuple-element.75), channel_id=1, source_target_pairs={{0,2},{1,3},{2,0},{3,1},{4,6},{5,7},{6,4},{7,5},{8,16},{9,17},{10,... | collective-permute-start | bytes 393224 | tf_op jit(solution)/shard_map/ppermute | solution.py:68
  70.7 7.8 %collective-permute-start.32 = (bf16[64,256]{1,0:T(8,128)(2,1)S(1)}, bf16[64,256]{1,0:T(8,128)(2,1)S(1)}, u32[]{:S(2)}, u32[]{:S(2)}) collective-permute-start(bf16[64,256]{1,0:T(8,128)(2,1)S(1)} %collective-permute-done.31.refs_6_), channel_id=1, source_target_pairs={{0,16},{1,17},{2,18},{3,19},{4,20},{5,21},{6,22},{7,23},{8,24},{9,... | collective-permute-start | bytes 98312 | tf_op jit(solution)/shard_map/ppermute | solution.py:68
  73.4 19.9 %collective-permute-start.26 = (bf16[256,256]{1,0:T(8,128)(2,1)S(1)}, bf16[256,256]{1,0:T(8,128)(2,1)S(1)}, u32[]{:S(2)}, u32[]{:S(2)}) collective-permute-start(bf16[256,256]{1,0:T(8,128)(2,1)S(1)} %get-tuple-element.78.refs_0_), channel_id=1, source_target_pairs={{0,1},{1,0},{2,3},{3,2},{4,5},{5,4},{6,7},{7,6},{8,9},{9,8},{10,11... | collective-permute-start | bytes 393224 | tf_op jit(solution)/shard_map/ppermute | solution.py:68
  75.0 18.4 %collective-permute-start.27 = (bf16[256,256]{1,0:T(8,128)(2,1)S(1)}, bf16[256,256]{1,0:T(8,128)(2,1)S(1)}, u32[]{:S(2)}, u32[]{:S(2)}) collective-permute-start(bf16[256,256]{1,0:T(8,128)(2,1)S(1)} %get-tuple-element.79.refs_1_), channel_id=1, source_target_pairs={{0,16},{1,2},{2,1},{3,4},{4,3},{5,6},{6,5},{7,23},{8,24},{9,10},{1... | collective-permute-start | bytes 393224 | tf_op jit(solution)/shard_map/ppermute | solution.py:68
  75.2 18.1 %collective-permute-start.28 = (bf16[256,256]{1,0:T(8,128)(2,1)S(1)}, bf16[256,256]{1,0:T(8,128)(2,1)S(1)}, u32[]{:S(2)}, u32[]{:S(2)}) collective-permute-start(bf16[256,256]{1,0:T(8,128)(2,1)S(1)} %get-tuple-element.80.refs_2_), channel_id=1, source_target_pairs={{0,8},{1,9},{2,10},{3,11},{4,12},{5,13},{6,14},{7,15},{8,0},{9,1},... | collective-permute-start | bytes 393224 | tf_op jit(solution)/shard_map/ppermute | solution.py:68
  75.7 17.6 %collective-permute-start.29 = (bf16[256,256]{1,0:T(8,128)(2,1)S(1)}, bf16[256,256]{1,0:T(8,128)(2,1)S(1)}, u32[]{:S(2)}, u32[]{:S(2)}) collective-permute-start(bf16[256,256]{1,0:T(8,128)(2,1)S(1)} %get-tuple-element.81.refs_3_), channel_id=1, source_target_pairs={{0,2},{1,3},{2,0},{3,1},{4,6},{5,7},{6,4},{7,5},{8,16},{9,17},{10,... | collective-permute-start | bytes 393224 | tf_op jit(solution)/shard_map/ppermute | solution.py:68
  (25 other events, 181.4 us)

commit v2 on v1

v2 whole, which is shorter than its diff:
```python
import functools

import jax
import jax.numpy as jnp
from jax import lax
from jax.experimental import pallas as pl
from jax.experimental.pallas import tpu as pltpu
from jax.sharding import PartitionSpec as P


ITERS = 2
OMEGA = 0.6
AXES = ("grp", "row", "col")
BF = jnp.bfloat16
F32 = jnp.float32
VMEM_LIMIT = 24 << 20


def dot(a, b):
    return jnp.dot(a, b, preferred_element_type=F32)


def call(kernel, outs, args, flops, scratch=()):
    moved = sum(a.size * a.dtype.itemsize for a in args)
    return pl.pallas_call(
        kernel,
        out_shape=outs,
        scratch_shapes=list(scratch),
        compiler_params=pltpu.CompilerParams(vmem_limit_bytes=VMEM_LIMIT),
        cost_estimate=pl.CostEstimate(flops=flops, transcendentals=0, bytes_accessed=moved),
    )(*args)


def shape(dims, dtype):
    return jax.ShapeDtypeStruct(tuple(dims), dtype)


def pairs_of(sizes, where):
    grps, rows, cols = sizes
    flat = lambda g, r, c: (g * rows + r) * cols + c
    return [
        (flat(g, r, c), flat(*where(g, r, c)))
        for g in range(grps)
        for r in range(rows)
        for c in range(cols)
    ]


def matching(sizes, odd, along_cols):
    grps, rows, cols = sizes
    count = cols if along_cols else grps * rows

    def where(g, r, c):
        at = c if along_cols else g * rows + r
        to = at + 1 if at % 2 == odd else at - 1
        if 0 <= to < count:
            return (g, r, to) if along_cols else (to // rows, to % rows, c)
        if along_cols and grps == 2:
            return (1 - g, r, c)
        if not along_cols and cols % 4 == 0:
            return (g, r, c ^ 2)
        return (g, r, c)

    return pairs_of(sizes, where)


def send(value, pairs):
    return lax.ppermute(value, AXES, pairs)


def edge_of(sizes, m):
    _, rows, _ = sizes
    if m < 2:
        at, up, down = lax.axis_index("col"), 1, 0
    else:
        at, up, down = lax.axis_index("grp") * rows + lax.axis_index("row"), 3, 2
    return jnp.where(at % 2 == m % 2, up, down)


def edge_list(sizes, lists_ref, m):
    part = lists_ref.shape[1] // 4
    at = pl.multiple_of(edge_of(sizes, m) * part, part)
    return lists_ref[:, pl.ds(at, part)]


def start_kernel(sizes, lists_ref, op_ref, u_ref, sel_ref, applied_ref, *edges):
    n = sel_ref.shape[0]
    part = n // 4
    for m in range(4):
        names = jnp.broadcast_to(edge_list(sizes, lists_ref, m), (128, part)).T
        lanes = lax.broadcasted_iota(jnp.int32, (part, 128), 1)
        for j in range(n // 128):
            hit = names == lanes + j * 128
            sel_ref[m * part : (m + 1) * part, j * 128 : (j + 1) * 128] = jnp.where(hit, 1.0, 0.0).astype(BF)
    applied = dot(op_ref[...], u_ref[...].astype(BF))
    applied_ref[...] = applied
    applied = applied.astype(BF)
    for m, edge in enumerate(edges):
        edge[...] = dot(sel_ref[m * part : (m + 1) * part, :], applied).astype(BF)


def tables_kernel(sizes, lists_ref, basis_t_ref, slot_ref, scatter_ref, based_ref, based_t_ref):
    n = scatter_ref.shape[0]
    part = n // 4
    for m in range(4):
        rows = lax.broadcasted_iota(jnp.int32, (n, part), 0)
        hit = rows == edge_list(sizes, lists_ref, m)
        scatter_ref[:, m * part : (m + 1) * part] = jnp.where(hit, 1.0, 0.0).astype(BF)
    nb = basis_t_ref.shape[0]
    pick = lax.broadcasted_iota(jnp.int32, (nb, nb), 0) == slot_ref[...]
    based_t = dot(jnp.where(pick, 1.0, 0.0).astype(BF), basis_t_ref[...])
    based_t_ref[...] = based_t.astype(BF)
    based_ref[...] = based_t.T.astype(BF)


def prepare_kernel(sel_ref, pre_ref, op_ref, based_ref, pre_sel_ref, lift_ref, lift_sel_ref):
    pre_sel_ref[...] = dot(sel_ref[...], pre_ref[...]).astype(BF)
    lift = dot(op_ref[...], based_ref[...]).astype(BF)
    lift_ref[...] = lift
    lift_sel_ref[...] = dot(sel_ref[...], lift).astype(BF)


def shared(sizes):
    grps, rows, cols = sizes
    a = lax.axis_index("grp") * rows + lax.axis_index("row")
    c = lax.axis_index("col")

    def partner(at, count, odd):
        up = at % 2 == odd
        return jnp.where(up, at + 1 < count, at > 0)

    return [
        partner(c, cols, 0),
        partner(c, cols, 1),
        partner(a, grps * rows, 0),
        partner(a, grps * rows, 1),
    ]


def resid_kernel(sizes, load_ref, applied_ref, scatter_ref, based_t_ref, n0, n1, n2, n3, resid_ref, coarse_ref, gathered):
    part = n0.shape[0]
    for m, (there, near) in enumerate(zip(shared(sizes), (n0, n1, n2, n3))):
        gathered[m * part : (m + 1) * part, :] = jnp.where(there, near[...], jnp.zeros_like(near))
    resid = load_ref[...] - applied_ref[...] - dot(scatter_ref[...], gathered[...])
    resid = resid.astype(BF)
    resid_ref[...] = resid
    coarse_ref[...] = dot(based_t_ref[...], resid).astype(BF)


def fix_kernel(pre_sel_ref, resid_ref, fix_ref, *edges):
    part = edges[0].shape[0]
    for m, edge in enumerate(edges):
        rows = slice(m * part, (m + 1) * part)
        fix = dot(pre_sel_ref[rows, :], resid_ref[...])
        fix_ref[rows, :] = fix
        edge[...] = fix.astype(BF)


def smoothed(sizes, u, fix_ref, scatter_ref, near, blended):
    part = near[0].shape[0]
    for m, there in enumerate(shared(sizes)):
        rows = slice(m * part, (m + 1) * part)
        fix = fix_ref[rows, :]
        both = 0.5 * (fix + near[m][...].astype(F32))
        blended[rows, :] = jnp.where(there, both, fix).astype(BF)
    return u + OMEGA * dot(scatter_ref[...], blended[...])


def middle_kernel(sizes, op_ref, sel_ref, u_ref, fix_ref, scatter_ref, *refs):
    near, (out_ref, applied_ref, edge_ref, blended) = refs[:4], refs[4:]
    u = smoothed(sizes, u_ref[...], fix_ref, scatter_ref, near, blended)
    out_ref[...] = u
    applied = dot(op_ref[...], u.astype(BF))
    applied_ref[...] = applied
    edge_ref[...] = dot(sel_ref[...], applied.astype(BF))


def solution_of(mine_ref, others):
    solved = mine_ref[...]
    for other in others:
        solved = solved + other[...].astype(F32)
    return solved.astype(BF)


def next_kernel(lift_ref, lift_sel_ref, applied_ref, edge_ref, mine_ref, *refs):
    others, (solved_ref, out_ref, *edges) = refs[:-6], refs[-6:]
    solved = solution_of(mine_ref, others)
    solved_ref[...] = solved
    part = edges[0].shape[0]
    for m, edge in enumerate(edges):
        rows = slice(m * part, (m + 1) * part)
        edge[...] = (edge_ref[rows, :] + OMEGA * dot(lift_sel_ref[rows, :], solved)).astype(BF)
    out_ref[...] = applied_ref[...] + OMEGA * dot(lift_ref[...], solved)


def late_kernel(sizes, u_ref, fix_ref, scatter_ref, based_ref, solved_ref, *refs):
    near, (out_ref, blended) = refs[:4], refs[4:]
    u = u_ref[...] + OMEGA * dot(based_ref[...], solved_ref[...])
    out_ref[...] = smoothed(sizes, u, fix_ref, scatter_ref, near, blended)


def last_kernel(u_ref, based_ref, mine_ref, *refs):
    others, out_ref = refs[:-1], refs[-1]
    out_ref[...] = u_ref[...] + OMEGA * dot(based_ref[...], solution_of(mine_ref, others))


def regroup_kernel(geometry, nb, inverse_ref, *blocks):
    _, ratio, lines = geometry
    c = lax.axis_index("col")
    owner = c // ratio
    for k, block in enumerate(blocks):
        target = k ^ owner
        parity, pair = target % 2, target // 2
        for line in range(lines):
            rows = pl.ds(pl.multiple_of((2 * line + parity) * nb, nb), nb)
            cols = pl.ds(pl.multiple_of(pair * 2 * nb, 2 * nb), 2 * nb)
            block[line * nb : (line + 1) * nb, :] = inverse_ref[rows, cols]


def coarse_kernel(geometry, row_size, nb, moves, *refs):
    grid_rows, _, lines = geometry
    blocks, refs = refs[:grid_rows], refs[grid_rows:]
    vectors, refs = refs[: len(moves)], refs[len(moves) :]
    mine_ref, others, (stack, total) = refs[0], refs[1:lines], refs[lines:]
    g, r, c = (lax.axis_index(axis) for axis in AXES)
    for (dg, dr, dc), vector in zip(moves, vectors):
        at = (((g ^ dg) * row_size + (r ^ dr)) * 2 + ((c % 2) ^ dc)) * nb
        stack[pl.ds(pl.multiple_of(at, nb), nb), :] = vector[...]
    acc = None
    for k, block in enumerate(blocks):
        owner = k ^ (c % grid_rows)
        part = dot(block[...], stack[pl.ds(pl.multiple_of(owner * 2 * nb, 2 * nb), 2 * nb), :])
        acc = part if acc is None else acc + part
    total[...] = acc
    line = c // 2
    for k in range(lines):
        got = total[pl.ds(pl.multiple_of((line ^ k) * nb, nb), nb), :]
        if k == 0:
            mine_ref[...] = got
        else:
            others[k - 1][...] = got.astype(BF)


def body(load, guess, interface_op, precond, basis, coarse_inverse, edge_rows, coarse_slot):
    sizes = tuple(lax.axis_size(axis) for axis in AXES)
    grps, row_size, cols = sizes
    grid_rows = grps * row_size
    load, u, op, pre = load[0, 0], guess[0, 0], interface_op[0, 0], precond[0, 0]
    basis_t = jnp.swapaxes(basis[0, 0], 0, 1)
    slot, lists = coarse_slot[0], edge_rows[0]
    n, cases = load.shape
    nb = basis_t.shape[0]
    part = n // 4
    ratio, lines = cols // grid_rows, cols // 2
    geometry = (grid_rows, ratio, lines)

    halo_pairs = [matching(sizes, m % 2, m < 2) for m in range(4)]
    far_moves = [(dr, dc) for dr in range(row_size) for dc in range(2)]
    moves = [(dg, dr, dc) for dr, dc in far_moves for dg in range(grps)]

    def swap_pairs(dg, dr, dc):
        return pairs_of(sizes, lambda g, r, c: (g ^ dg, r ^ dr, c ^ dc))

    def target(k):
        return pairs_of(sizes, lambda g, r, c: (g, r, (c % ratio) * grid_rows + (k ^ (c // ratio))))

    field = shape((n, cases), F32)
    edge = shape((part, cases), BF)
    square = shape((n, n), BF)
    thin = shape((n, nb), BF)
    vector = shape((nb, cases), BF)
    flops = 2 * n * n * cases

    def halo(edges):
        return [send(e, p) for e, p in zip(edges, halo_pairs)]

    blocks = call(
        functools.partial(regroup_kernel, geometry, nb),
        [shape((lines * nb, 2 * nb), BF)] * grid_rows,
        [coarse_inverse],
        n,
    )
    blocks = [send(block, target(k)) for k, block in enumerate(blocks)]
    sel, applied, *edges = call(
        functools.partial(start_kernel, sizes), [square, field] + [edge] * 4, [lists, op, u], 2 * flops
    )
    near = halo(edges)
    scatter, based, based_t = call(
        functools.partial(tables_kernel, sizes), [square, thin, shape((nb, n), BF)], [lists, basis_t, slot], n * n
    )
    pre_sel, lift, lift_sel = call(prepare_kernel, [square, thin, thin], [sel, pre, op, based], 2 * n * n * n)

    scratch = [pltpu.VMEM((n, cases), BF)]
    for sweep in range(ITERS):
        resid, coarse = call(
            functools.partial(resid_kernel, sizes),
            [shape((n, cases), BF), vector],
            [load, applied, scatter, based_t, *near],
            flops,
            scratch,
        )
        vectors = {}
        for dr, dc in far_moves:
            got = coarse if dr + dc == 0 else send(coarse, swap_pairs(0, dr, dc))
            vectors[0, dr, dc] = got
            for dg in range(1, grps):
                vectors[dg, dr, dc] = send(got, swap_pairs(dg, 0, 0))
        fix, *own = call(fix_kernel, [field] + [edge] * 4, [pre_sel, resid], flops)
        near = halo(own)
        mine, *others = call(
            functools.partial(coarse_kernel, geometry, row_size, nb, moves),
            [shape((nb, cases), F32)] + [vector] * (lines - 1),
            [*blocks, *(vectors[move] for move in moves)],
            2 * lines * nb * 2 * nb * grid_rows * cases,
            [pltpu.VMEM((2 * grid_rows * nb, cases), BF), pltpu.VMEM((lines * nb, cases), F32)],
        )
        others = [send(o, swap_pairs(0, 0, 2 * (k + 1))) for k, o in enumerate(others)]
        if sweep < ITERS - 1:
            inputs = [u, fix, scatter, *near]
            u, applied, edge_part = call(
                functools.partial(middle_kernel, sizes), [field] * 3, [op, sel, *inputs], 3 * flops, scratch
            )
            solved, applied, *edges = call(
                next_kernel,
                [vector, field] + [edge] * 4,
                [lift, lift_sel, applied, edge_part, mine, *others],
                n * nb * cases,
            )
            near = halo(edges)
        else:
            u = call(
                functools.partial(late_kernel, sizes), field, [u, fix, scatter, based, solved, *near], flops, scratch
            )
            u = call(last_kernel, field, [u, based, mine, *others], n * nb * cases)
    return u[None, None]


def solution(mesh):
    cells = P(("grp", "row"), "col", None, None)
    lists = P(("grp", "row"), "col", None)

    return jax.shard_map(
        body,
        mesh=mesh,
        in_specs=(cells, cells, cells, cells, cells, P(("grp", "row"), "col"), lists, lists),
        out_specs=cells,
        check_vma=False,
    )
```

time: 95.5 us -> 86.9 us (0.910)
  waiting for transfers between devices: 27.7 us -> 17.6 us
  local copies, waits for them, and re-layouts: 2.84 us -> 5.12 us
  starting transfers between devices: 48.3 us -> 46.1 us
  Pallas kernels: 15.4 us -> 17.4 us
    ppermute x40, waiting for transfers between devices: 27.7 us -> 17.6 us  [send(): return lax.ppermute(value, AXES, pairs)]
    unnamed x18 -> x20, local copies, waits for them, and re-layouts: 2.84 us -> 5.12 us
    ppermute x40, starting transfers between devices: 48.3 us -> 46.1 us  [send(): return lax.ppermute(value, AXES, pairs)]
    pallas_call x11 -> x14, Pallas kernels: 15.4 us -> 17.4 us  [call(): pl.pallas_call(kernel, out_shape=outs, scratch_shapes=list(scratch), comp...]
  transfers between devices with their start and end apart: 40 -> 40, of which waited for: 15 -> 13; matrix products, arithmetic and copies ran while one was open for 0% -> 0% of each run, Pallas kernels for 8% -> 14%
where the time goes in v2:
time: 86.9 us; the launch traced here: 86.6 us
  starting transfers between devices  46.1 us (53%)
  waiting for transfers between devices  17.6 us (20%)
  Pallas kernels  17.4 us (20%)
  local copies, waits for them, and re-layouts  5.12 us (6%)
    ppermute x40, starting transfers between devices, send(): return lax.ppermute(value, AXES, pairs)  46.1 us
    ppermute x40, waiting for transfers between devices, send(): return lax.ppermute(value, AXES, pairs)  17.6 us
    pallas_call x14, Pallas kernels, call(): pl.pallas_call(kernel, out_shape=outs, scratch_shapes=list(scratch), comp...  17.4 us
    unnamed x20, local copies, waits for them, and re-layouts  5.12 us
  transfers between devices with their start and end apart: 40, of which 13 were waited for; matrix products, arithmetic and copies ran while one was open for 0% of the time, Pallas kernels for 14%

profile of v2, /device:TPU:0, one launch (start us, length us, event | category | flops | bytes accessed | tf_op | source)
XLA Modules:
  0.0 86.6 jit_solution(10143506441962588305)
XLA Ops:
  0.0 1.6 %copy-done.1 = bf16[1,1,1024,1024]{3,2,1,0:T(8,128)(2,1)S(1)} copy-done((bf16[1,1,1024,1024]{3,2,1,0:T(8,128)(2,1)S(1)}, bf16[1,1,1024,1024]{3,2,1,0:T(8,128)(2,1)}, u32[]{:S(2)}) %copy-start.1) | copy-done | bytes 2097176
  3.5 2.3 %shard_map.82 = (bf16[1024,1024]{1,0:T(8,128)(2,1)S(1)}, f32[1024,256]{1,0:T(8,128)S(1)}, bf16[256,256]{1,0:T(8,128)(2,1)S(1)}, bf16[256,256]{1,0:T(8,128)(2,1)S...) custom-call(s32[1,1024]{1,0:T(1,128)S(1)} %bitcast.18, bf16[1024,1024]{1,0:T(8,128)(2,1)S(1)} %bitcast.12, ...), custom_call_target="tpu_custom_call" | custom-call | flops 1073741824 | bytes 3149824 | tf_op jit(solution)/shard_map/pallas_call | solution.py:25
  5.9 3.0 %collective-permute-start = (bf16[256,256]{1,0:T(8,128)(2,1)S(1)}, bf16[256,256]{1,0:T(8,128)(2,1)S(1)}, u32[]{:S(2)}, u32[]{:S(2)}) collective-permute-start(bf16[256,256]{1,0:T(8,128)(2,1)S(1)} %get-tuple-element.58), channel_id=1, source_target_pairs={{0,1},{1,0},{2,3},{3,2},{4,5},{5,4},{6,7},{7,6},{8,9},{9,8},{10,11... | collective-permute-start | bytes 393224 | tf_op jit(solution)/shard_map/ppermute | solution.py:68
  8.9 1.5 %collective-permute-start.2 = (bf16[256,256]{1,0:T(8,128)(2,1)S(1)}, bf16[256,256]{1,0:T(8,128)(2,1)S(1)}, u32[]{:S(2)}, u32[]{:S(2)}) collective-permute-start(bf16[256,256]{1,0:T(8,128)(2,1)S(1)} %get-tuple-element.60), channel_id=1, source_target_pairs={{0,8},{1,9},{2,10},{3,11},{4,12},{5,13},{6,14},{7,15},{8,0},{9,1},... | collective-permute-start | bytes 393224 | tf_op jit(solution)/shard_map/ppermute | solution.py:68
  10.4 2.0 %collective-permute-start.3 = (bf16[256,256]{1,0:T(8,128)(2,1)S(1)}, bf16[256,256]{1,0:T(8,128)(2,1)S(1)}, u32[]{:S(2)}, u32[]{:S(2)}) collective-permute-start(bf16[256,256]{1,0:T(8,128)(2,1)S(1)} %get-tuple-element.61), channel_id=1, source_target_pairs={{0,2},{1,3},{2,0},{3,1},{4,6},{5,7},{6,4},{7,5},{8,16},{9,17},{10,... | collective-permute-start | bytes 393224 | tf_op jit(solution)/shard_map/ppermute | solution.py:68
  14.5 5.3 %collective-permute-start.9 = (bf16[256,128]{1,0:T(8,128)(2,1)S(1)}, bf16[256,128]{1,0:T(8,128)(2,1)S(1)}, u32[]{:S(2)}, u32[]{:S(2)}) collective-permute-start(bf16[256,128]{1,0:T(8,128)(2,1)S(1)} %get-tuple-element.74), channel_id=1, source_target_pairs={{0,1},{1,5},{2,0},{3,4},{4,3},{5,7},{6,2},{7,6},{8,9},{9,13},{10,8... | collective-permute-start | bytes 196616 | tf_op jit(solution)/shard_map/ppermute | solution.py:68
  19.9 1.6 %copy-done.9 = bf16[1,1,1024,1024]{3,2,1,0:T(8,128)(2,1)S(1)} copy-done((bf16[1,1,1024,1024]{3,2,1,0:T(8,128)(2,1)S(1)}, bf16[1,1,1024,1024]{3,2,1,0:T(8,128)(2,1)}, u32[]{:S(2)}) %copy-start.9) | copy-done | bytes 2097176
  21.5 4.4 %shard_map.84 = (bf16[1024,1024]{1,0:T(8,128)(2,1)S(1)}, bf16[1024,64]{1,0:T(8,128)(2,1)S(1)}, bf16[1024,64]{1,0:T(8,128)(2,1)S(1)}) custom-call(bf16[1024,1024]{1,0:T(8,128)(2,1)S(1)} %get-tuple-element.52.sel_ref, bf16[1024,1024]{1,0:T(8,128)(2,1)S(1)} %bitcast.21, bf16[1024,1024]{1,0:T(8,128)(2,1)S(1)} %bitcast.13, ...), custom_call_target="tpu_custom_call" | custom-call | flops 2147483648 | bytes 6422528 | tf_op jit(solution)/shard_map/pallas_call | solution.py:25
  25.9 4.8 %collective-permute-start.11 = (bf16[256,128]{1,0:T(8,128)(2,1)S(1)}, bf16[256,128]{1,0:T(8,128)(2,1)S(1)}, u32[]{:S(2)}, u32[]{:S(2)}) collective-permute-start(bf16[256,128]{1,0:T(8,128)(2,1)S(1)} %get-tuple-element.76), channel_id=1, source_target_pairs={{0,3},{1,7},{2,2},{3,6},{4,1},{5,5},{6,0},{7,4},{8,11},{9,15},{10,... | collective-permute-start | bytes 196616 | tf_op jit(solution)/shard_map/ppermute | solution.py:68
  32.9 2.5 %collective-permute-start.17 = (bf16[64,256]{1,0:T(8,128)(2,1)S(1)}, bf16[64,256]{1,0:T(8,128)(2,1)S(1)}, u32[]{:S(2)}, u32[]{:S(2)}) collective-permute-start(bf16[64,256]{1,0:T(8,128)(2,1)S(1)} %get-tuple-element.77.refs_4_), channel_id=1, source_target_pairs={{0,9},{1,8},{2,11},{3,10},{4,13},{5,12},{6,15},{7,14},{8,1},{9,0},... | collective-permute-start | bytes 98312 | tf_op jit(solution)/shard_map/ppermute | solution.py:68
  36.1 1.5 %collective-permute-start.4 = (bf16[256,256]{1,0:T(8,128)(2,1)S(1)}, bf16[256,256]{1,0:T(8,128)(2,1)S(1)}, u32[]{:S(2)}, u32[]{:S(2)}) collective-permute-start(bf16[256,256]{1,0:T(8,128)(2,1)S(1)} %get-tuple-element.64), channel_id=1, source_target_pairs={{0,1},{1,0},{2,3},{3,2},{4,5},{5,4},{6,7},{7,6},{8,9},{9,8},{10,11... | collective-permute-start | bytes 393224 | tf_op jit(solution)/shard_map/ppermute | solution.py:68
  37.7 2.3 %collective-permute-start.7 = (bf16[256,256]{1,0:T(8,128)(2,1)S(1)}, bf16[256,256]{1,0:T(8,128)(2,1)S(1)}, u32[]{:S(2)}, u32[]{:S(2)}) collective-permute-start(bf16[256,256]{1,0:T(8,128)(2,1)S(1)} %get-tuple-element.67), channel_id=1, source_target_pairs={{0,2},{1,3},{2,0},{3,1},{4,6},{5,7},{6,4},{7,5},{8,16},{9,17},{10,... | collective-permute-start | bytes 393224 | tf_op jit(solution)/shard_map/ppermute | solution.py:68
  44.0 1.5 %collective-permute-start.19 = (bf16[64,256]{1,0:T(8,128)(2,1)S(1)}, bf16[64,256]{1,0:T(8,128)(2,1)S(1)}, u32[]{:S(2)}, u32[]{:S(2)}) collective-permute-start(bf16[64,256]{1,0:T(8,128)(2,1)S(1)} %get-tuple-element.79), channel_id=1, source_target_pairs={{0,2},{1,3},{2,0},{3,1},{4,6},{5,7},{6,4},{7,5},{8,10},{9,11},{10,... | collective-permute-start | bytes 98312 | tf_op jit(solution)/shard_map/ppermute | solution.py:68
  45.5 3.4 %collective-permute-start.20 = (bf16[64,256]{1,0:T(8,128)(2,1)S(1)}, bf16[64,256]{1,0:T(8,128)(2,1)S(1)}, u32[]{:S(2)}, u32[]{:S(2)}) collective-permute-start(bf16[64,256]{1,0:T(8,128)(2,1)S(1)} %get-tuple-element.80), channel_id=1, source_target_pairs={{0,4},{1,5},{2,6},{3,7},{4,0},{5,1},{6,2},{7,3},{8,12},{9,13},{10,... | collective-permute-start | bytes 98312 | tf_op jit(solution)/shard_map/ppermute | solution.py:68
  48.9 2.8 %shard_map.87 = (f32[1024,256]{1,0:T(8,128)S(1)}, f32[1024,256]{1,0:T(8,128)S(1)}, f32[1024,256]{1,0:T(8,128)S(1)}) custom-call(bf16[1024,1024]{1,0:T(8,128)(2,1)S(1)} %bitcast.14, bf16[1024,1024]{1,0:T(8,128)(2,1)S(1)} %get-tuple-element.52.sel_ref, f32[1024,256]{1,0:T(8,128)S(1)} %bitcast.16, f32[1024,256]{1,0:T(8,128)S(1)} %get-tuple-element.63.fix_ref, ...), custom_call_target="tpu_custom_call" | custom-call | flops 1610612736 | bytes 8912896 | tf_op jit(solution)/shard_map/pallas_call | solution.py:25
  51.8 2.8 %collective-permute-done.21.refs_2_ = bf16[64,256]{1,0:T(8,128)(2,1)S(1)} collective-permute-done((bf16[64,256]{1,0:T(8,128)(2,1)S(1)}, bf16[64,256]{1,0:T(8,128)(2,1)S(1)}, u32[]{:S(2)}, u32[]{:S(2)}) %collective-permute-start.21) | collective-permute-done | bytes 32800 | tf_op jit(solution)/shard_map/ppermute | solution.py:68
  55.6 3.3 %collective-permute-start.25 = (bf16[256,256]{1,0:T(8,128)(2,1)S(1)}, bf16[256,256]{1,0:T(8,128)(2,1)S(1)}, u32[]{:S(2)}, u32[]{:S(2)}) collective-permute-start(bf16[256,256]{1,0:T(8,128)(2,1)S(1)} %get-tuple-element.86), channel_id=1, source_target_pairs={{0,2},{1,3},{2,0},{3,1},{4,6},{5,7},{6,4},{7,5},{8,16},{9,17},{10,... | collective-permute-start | bytes 393224 | tf_op jit(solution)/shard_map/ppermute | solution.py:68
  61.1 1.8 %collective-permute-done.25.n3 = bf16[256,256]{1,0:T(8,128)(2,1)S(1)} collective-permute-done((bf16[256,256]{1,0:T(8,128)(2,1)S(1)}, bf16[256,256]{1,0:T(8,128)(2,1)S(1)}, u32[]{:S(2)}, u32[]{:S(2)}) %collective-permute-start.25) | collective-permute-done | bytes 131104 | tf_op jit(solution)/shard_map/ppermute | solution.py:68
  65.4 2.1 %collective-permute-start.35 = (bf16[64,256]{1,0:T(8,128)(2,1)S(1)}, bf16[64,256]{1,0:T(8,128)(2,1)S(1)}, u32[]{:S(2)}, u32[]{:S(2)}) collective-permute-start(bf16[64,256]{1,0:T(8,128)(2,1)S(1)} %get-tuple-element.94.refs_4_), channel_id=1, source_target_pairs={{0,9},{1,8},{2,11},{3,10},{4,13},{5,12},{6,15},{7,14},{8,1},{9,0},... | collective-permute-start | bytes 98312 | tf_op jit(solution)/shard_map/ppermute | solution.py:68
  69.7 2.1 %collective-permute-start.29 = (bf16[256,256]{1,0:T(8,128)(2,1)S(1)}, bf16[256,256]{1,0:T(8,128)(2,1)S(1)}, u32[]{:S(2)}, u32[]{:S(2)}) collective-permute-start(bf16[256,256]{1,0:T(8,128)(2,1)S(1)} %get-tuple-element.93), channel_id=1, source_target_pairs={{0,2},{1,3},{2,0},{3,1},{4,6},{5,7},{6,4},{7,5},{8,16},{9,17},{10,... | collective-permute-start | bytes 393224 | tf_op jit(solution)/shard_map/ppermute | solution.py:68
  75.8 1.8 %collective-permute-start.37 = (bf16[64,256]{1,0:T(8,128)(2,1)S(1)}, bf16[64,256]{1,0:T(8,128)(2,1)S(1)}, u32[]{:S(2)}, u32[]{:S(2)}) collective-permute-start(bf16[64,256]{1,0:T(8,128)(2,1)S(1)} %get-tuple-element.96), channel_id=1, source_target_pairs={{0,2},{1,3},{2,0},{3,1},{4,6},{5,7},{6,4},{7,5},{8,10},{9,11},{10,... | collective-permute-start | bytes 98312 | tf_op jit(solution)/shard_map/ppermute | solution.py:68
  77.6 2.0 %collective-permute-start.38 = (bf16[64,256]{1,0:T(8,128)(2,1)S(1)}, bf16[64,256]{1,0:T(8,128)(2,1)S(1)}, u32[]{:S(2)}, u32[]{:S(2)}) collective-permute-start(bf16[64,256]{1,0:T(8,128)(2,1)S(1)} %get-tuple-element.97), channel_id=1, source_target_pairs={{0,4},{1,5},{2,6},{3,7},{4,0},{5,1},{6,2},{7,3},{8,12},{9,13},{10,... | collective-permute-start | bytes 98312 | tf_op jit(solution)/shard_map/ppermute | solution.py:68
  81.3 1.6 %collective-permute-done.38.refs_1_ = bf16[64,256]{1,0:T(8,128)(2,1)S(1)} collective-permute-done((bf16[64,256]{1,0:T(8,128)(2,1)S(1)}, bf16[64,256]{1,0:T(8,128)(2,1)S(1)}, u32[]{:S(2)}, u32[]{:S(2)}) %collective-permute-start.38) | collective-permute-done | bytes 32800 | tf_op jit(solution)/shard_map/ppermute | solution.py:68
  82.8 2.5 %collective-permute-done.39.refs_2_ = bf16[64,256]{1,0:T(8,128)(2,1)S(1)} collective-permute-done((bf16[64,256]{1,0:T(8,128)(2,1)S(1)}, bf16[64,256]{1,0:T(8,128)(2,1)S(1)}, u32[]{:S(2)}, u32[]{:S(2)}) %collective-permute-start.39) | collective-permute-done | bytes 32800 | tf_op jit(solution)/shard_map/ppermute | solution.py:68
  (90 shorter events, 25.6 us)
Async XLA Ops:
  5.9 8.6 %collective-permute-start = (bf16[256,256]{1,0:T(8,128)(2,1)S(1)}, bf16[256,256]{1,0:T(8,128)(2,1)S(1)}, u32[]{:S(2)}, u32[]{:S(2)}) collective-permute-start(bf16[256,256]{1,0:T(8,128)(2,1)S(1)} %get-tuple-element.58), channel_id=1, source_target_pairs={{0,1},{1,0},{2,3},{3,2},{4,5},{5,4},{6,7},{7,6},{8,9},{9,8},{10,11... | collective-permute-start | bytes 393224 | tf_op jit(solution)/shard_map/ppermute | solution.py:68
  8.9 10.9 %collective-permute-start.1 = (bf16[256,256]{1,0:T(8,128)(2,1)S(1)}, bf16[256,256]{1,0:T(8,128)(2,1)S(1)}, u32[]{:S(2)}, u32[]{:S(2)}) collective-permute-start(bf16[256,256]{1,0:T(8,128)(2,1)S(1)} %get-tuple-element.59), channel_id=1, source_target_pairs={{0,16},{1,2},{2,1},{3,4},{4,3},{5,6},{6,5},{7,23},{8,24},{9,10},{1... | collective-permute-start | bytes 393224 | tf_op jit(solution)/shard_map/ppermute | solution.py:68
  8.9 17.0 %collective-permute-start.2 = (bf16[256,256]{1,0:T(8,128)(2,1)S(1)}, bf16[256,256]{1,0:T(8,128)(2,1)S(1)}, u32[]{:S(2)}, u32[]{:S(2)}) collective-permute-start(bf16[256,256]{1,0:T(8,128)(2,1)S(1)} %get-tuple-element.60), channel_id=1, source_target_pairs={{0,8},{1,9},{2,10},{3,11},{4,12},{5,13},{6,14},{7,15},{8,0},{9,1},... | collective-permute-start | bytes 393224 | tf_op jit(solution)/shard_map/ppermute | solution.py:68
  10.4 20.3 %collective-permute-start.3 = (bf16[256,256]{1,0:T(8,128)(2,1)S(1)}, bf16[256,256]{1,0:T(8,128)(2,1)S(1)}, u32[]{:S(2)}, u32[]{:S(2)}) collective-permute-start(bf16[256,256]{1,0:T(8,128)(2,1)S(1)} %get-tuple-element.61), channel_id=1, source_target_pairs={{0,2},{1,3},{2,0},{3,1},{4,6},{5,7},{6,4},{7,5},{8,16},{9,17},{10,... | collective-permute-start | bytes 393224 | tf_op jit(solution)/shard_map/ppermute | solution.py:68
  12.5 19.3 %collective-permute-start.8 = (bf16[256,128]{1,0:T(8,128)(2,1)S(1)}, bf16[256,128]{1,0:T(8,128)(2,1)S(1)}, u32[]{:S(2)}, u32[]{:S(2)}) collective-permute-start(bf16[256,128]{1,0:T(8,128)(2,1)S(1)} %get-tuple-element.73), channel_id=1, source_target_pairs={{0,0},{1,4},{2,1},{3,5},{4,2},{5,6},{6,3},{7,7},{8,8},{9,12},{10,9... | collective-permute-start | bytes 196616 | tf_op jit(solution)/shard_map/ppermute | solution.py:68
  14.5 18.5 %collective-permute-start.9 = (bf16[256,128]{1,0:T(8,128)(2,1)S(1)}, bf16[256,128]{1,0:T(8,128)(2,1)S(1)}, u32[]{:S(2)}, u32[]{:S(2)}) collective-permute-start(bf16[256,128]{1,0:T(8,128)(2,1)S(1)} %get-tuple-element.74), channel_id=1, source_target_pairs={{0,1},{1,5},{2,0},{3,4},{4,3},{5,7},{6,2},{7,6},{8,9},{9,13},{10,8... | collective-permute-start | bytes 196616 | tf_op jit(solution)/shard_map/ppermute | solution.py:68
  19.8 13.2 %collective-permute-start.10 = (bf16[256,128]{1,0:T(8,128)(2,1)S(1)}, bf16[256,128]{1,0:T(8,128)(2,1)S(1)}, u32[]{:S(2)}, u32[]{:S(2)}) collective-permute-start(bf16[256,128]{1,0:T(8,128)(2,1)S(1)} %get-tuple-element.75), channel_id=1, source_target_pairs={{0,2},{1,6},{2,3},{3,7},{4,0},{5,4},{6,1},{7,5},{8,10},{9,14},{10,... | collective-permute-start | bytes 196616 | tf_op jit(solution)/shard_map/ppermute | solution.py:68
  25.9 10.2 %collective-permute-start.11 = (bf16[256,128]{1,0:T(8,128)(2,1)S(1)}, bf16[256,128]{1,0:T(8,128)(2,1)S(1)}, u32[]{:S(2)}, u32[]{:S(2)}) collective-permute-start(bf16[256,128]{1,0:T(8,128)(2,1)S(1)} %get-tuple-element.76), channel_id=1, source_target_pairs={{0,3},{1,7},{2,2},{3,6},{4,1},{5,5},{6,0},{7,4},{8,11},{9,15},{10,... | collective-permute-start | bytes 196616 | tf_op jit(solution)/shard_map/ppermute | solution.py:68
  31.7 5.9 %collective-permute-start.12 = (bf16[64,256]{1,0:T(8,128)(2,1)S(1)}, bf16[64,256]{1,0:T(8,128)(2,1)S(1)}, u32[]{:S(2)}, u32[]{:S(2)}) collective-permute-start(bf16[64,256]{1,0:T(8,128)(2,1)S(1)} %get-tuple-element.77.refs_4_), channel_id=1, source_target_pairs={{0,16},{1,17},{2,18},{3,19},{4,20},{5,21},{6,22},{7,23},{8,24},{9,... | collective-permute-start | bytes 98312 | tf_op jit(solution)/shard_map/ppermute | solution.py:68
  31.8 5.8 %collective-permute-start.13 = (bf16[64,256]{1,0:T(8,128)(2,1)S(1)}, bf16[64,256]{1,0:T(8,128)(2,1)S(1)}, u32[]{:S(2)}, u32[]{:S(2)}) collective-permute-start(bf16[64,256]{1,0:T(8,128)(2,1)S(1)} %get-tuple-element.77.refs_4_), channel_id=1, source_target_pairs={{0,1},{1,0},{2,3},{3,2},{4,5},{5,4},{6,7},{7,6},{8,9},{9,8},{10,11... | collective-permute-start | bytes 98312 | tf_op jit(solution)/shard_map/ppermute | solution.py:68
  32.9 7.1 %collective-permute-start.17 = (bf16[64,256]{1,0:T(8,128)(2,1)S(1)}, bf16[64,256]{1,0:T(8,128)(2,1)S(1)}, u32[]{:S(2)}, u32[]{:S(2)}) collective-permute-start(bf16[64,256]{1,0:T(8,128)(2,1)S(1)} %get-tuple-element.77.refs_4_), channel_id=1, source_target_pairs={{0,9},{1,8},{2,11},{3,10},{4,13},{5,12},{6,15},{7,14},{8,1},{9,0},... | collective-permute-start | bytes 98312 | tf_op jit(solution)/shard_map/ppermute | solution.py:68
  36.1 9.4 %collective-permute-start.4 = (bf16[256,256]{1,0:T(8,128)(2,1)S(1)}, bf16[256,256]{1,0:T(8,128)(2,1)S(1)}, u32[]{:S(2)}, u32[]{:S(2)}) collective-permute-start(bf16[256,256]{1,0:T(8,128)(2,1)S(1)} %get-tuple-element.64), channel_id=1, source_target_pairs={{0,1},{1,0},{2,3},{3,2},{4,5},{5,4},{6,7},{7,6},{8,9},{9,8},{10,11... | collective-permute-start | bytes 393224 | tf_op jit(solution)/shard_map/ppermute | solution.py:68
  37.6 11.3 %collective-permute-start.5 = (bf16[256,256]{1,0:T(8,128)(2,1)S(1)}, bf16[256,256]{1,0:T(8,128)(2,1)S(1)}, u32[]{:S(2)}, u32[]{:S(2)}) collective-permute-start(bf16[256,256]{1,0:T(8,128)(2,1)S(1)} %get-tuple-element.65), channel_id=1, source_target_pairs={{0,16},{1,2},{2,1},{3,4},{4,3},{5,6},{6,5},{7,23},{8,24},{9,10},{1... | collective-permute-start | bytes 393224 | tf_op jit(solution)/shard_map/ppermute | solution.py:68
  37.6 11.3 %collective-permute-start.6 = (bf16[256,256]{1,0:T(8,128)(2,1)S(1)}, bf16[256,256]{1,0:T(8,128)(2,1)S(1)}, u32[]{:S(2)}, u32[]{:S(2)}) collective-permute-start(bf16[256,256]{1,0:T(8,128)(2,1)S(1)} %get-tuple-element.66), channel_id=1, source_target_pairs={{0,8},{1,9},{2,10},{3,11},{4,12},{5,13},{6,14},{7,15},{8,0},{9,1},... | collective-permute-start | bytes 393224 | tf_op jit(solution)/shard_map/ppermute | solution.py:68
  37.7 11.2 %collective-permute-start.7 = (bf16[256,256]{1,0:T(8,128)(2,1)S(1)}, bf16[256,256]{1,0:T(8,128)(2,1)S(1)}, u32[]{:S(2)}, u32[]{:S(2)}) collective-permute-start(bf16[256,256]{1,0:T(8,128)(2,1)S(1)} %get-tuple-element.67), channel_id=1, source_target_pairs={{0,2},{1,3},{2,0},{3,1},{4,6},{5,7},{6,4},{7,5},{8,16},{9,17},{10,... | collective-permute-start | bytes 393224 | tf_op jit(solution)/shard_map/ppermute | solution.py:68
  44.0 7.8 %collective-permute-start.19 = (bf16[64,256]{1,0:T(8,128)(2,1)S(1)}, bf16[64,256]{1,0:T(8,128)(2,1)S(1)}, u32[]{:S(2)}, u32[]{:S(2)}) collective-permute-start(bf16[64,256]{1,0:T(8,128)(2,1)S(1)} %get-tuple-element.79), channel_id=1, source_target_pairs={{0,2},{1,3},{2,0},{3,1},{4,6},{5,7},{6,4},{7,5},{8,10},{9,11},{10,... | collective-permute-start | bytes 98312 | tf_op jit(solution)/shard_map/ppermute | solution.py:68
  45.5 6.3 %collective-permute-start.20 = (bf16[64,256]{1,0:T(8,128)(2,1)S(1)}, bf16[64,256]{1,0:T(8,128)(2,1)S(1)}, u32[]{:S(2)}, u32[]{:S(2)}) collective-permute-start(bf16[64,256]{1,0:T(8,128)(2,1)S(1)} %get-tuple-element.80), channel_id=1, source_target_pairs={{0,4},{1,5},{2,6},{3,7},{4,0},{5,1},{6,2},{7,3},{8,12},{9,13},{10,... | collective-permute-start | bytes 98312 | tf_op jit(solution)/shard_map/ppermute | solution.py:68
  55.2 5.9 %collective-permute-start.24 = (bf16[256,256]{1,0:T(8,128)(2,1)S(1)}, bf16[256,256]{1,0:T(8,128)(2,1)S(1)}, u32[]{:S(2)}, u32[]{:S(2)}) collective-permute-start(bf16[256,256]{1,0:T(8,128)(2,1)S(1)} %get-tuple-element.85), channel_id=1, source_target_pairs={{0,8},{1,9},{2,10},{3,11},{4,12},{5,13},{6,14},{7,15},{8,0},{9,1},... | collective-permute-start | bytes 393224 | tf_op jit(solution)/shard_map/ppermute | solution.py:68
  55.6 7.4 %collective-permute-start.25 = (bf16[256,256]{1,0:T(8,128)(2,1)S(1)}, bf16[256,256]{1,0:T(8,128)(2,1)S(1)}, u32[]{:S(2)}, u32[]{:S(2)}) collective-permute-start(bf16[256,256]{1,0:T(8,128)(2,1)S(1)} %get-tuple-element.86), channel_id=1, source_target_pairs={{0,2},{1,3},{2,0},{3,1},{4,6},{5,7},{6,4},{7,5},{8,16},{9,17},{10,... | collective-permute-start | bytes 393224 | tf_op jit(solution)/shard_map/ppermute | solution.py:68
  65.4 6.5 %collective-permute-start.35 = (bf16[64,256]{1,0:T(8,128)(2,1)S(1)}, bf16[64,256]{1,0:T(8,128)(2,1)S(1)}, u32[]{:S(2)}, u32[]{:S(2)}) collective-permute-start(bf16[64,256]{1,0:T(8,128)(2,1)S(1)} %get-tuple-element.94.refs_4_), channel_id=1, source_target_pairs={{0,9},{1,8},{2,11},{3,10},{4,13},{5,12},{6,15},{7,14},{8,1},{9,0},... | collective-permute-start | bytes 98312 | tf_op jit(solution)/shard_map/ppermute | solution.py:68
  68.2 9.4 %collective-permute-start.26 = (bf16[256,256]{1,0:T(8,128)(2,1)S(1)}, bf16[256,256]{1,0:T(8,128)(2,1)S(1)}, u32[]{:S(2)}, u32[]{:S(2)}) collective-permute-start(bf16[256,256]{1,0:T(8,128)(2,1)S(1)} %get-tuple-element.90), channel_id=1, source_target_pairs={{0,1},{1,0},{2,3},{3,2},{4,5},{5,4},{6,7},{7,6},{8,9},{9,8},{10,11... | collective-permute-start | bytes 393224 | tf_op jit(solution)/shard_map/ppermute | solution.py:68
  68.6 11.0 %collective-permute-start.27 = (bf16[256,256]{1,0:T(8,128)(2,1)S(1)}, bf16[256,256]{1,0:T(8,128)(2,1)S(1)}, u32[]{:S(2)}, u32[]{:S(2)}) collective-permute-start(bf16[256,256]{1,0:T(8,128)(2,1)S(1)} %get-tuple-element.91), channel_id=1, source_target_pairs={{0,16},{1,2},{2,1},{3,4},{4,3},{5,6},{6,5},{7,23},{8,24},{9,10},{1... | collective-permute-start | bytes 393224 | tf_op jit(solution)/shard_map/ppermute | solution.py:68
  68.6 11.8 %collective-permute-start.28 = (bf16[256,256]{1,0:T(8,128)(2,1)S(1)}, bf16[256,256]{1,0:T(8,128)(2,1)S(1)}, u32[]{:S(2)}, u32[]{:S(2)}) collective-permute-start(bf16[256,256]{1,0:T(8,128)(2,1)S(1)} %get-tuple-element.92), channel_id=1, source_target_pairs={{0,8},{1,9},{2,10},{3,11},{4,12},{5,13},{6,14},{7,15},{8,0},{9,1},... | collective-permute-start | bytes 393224 | tf_op jit(solution)/shard_map/ppermute | solution.py:68
  69.7 10.6 %collective-permute-start.29 = (bf16[256,256]{1,0:T(8,128)(2,1)S(1)}, bf16[256,256]{1,0:T(8,128)(2,1)S(1)}, u32[]{:S(2)}, u32[]{:S(2)}) collective-permute-start(bf16[256,256]{1,0:T(8,128)(2,1)S(1)} %get-tuple-element.93), channel_id=1, source_target_pairs={{0,2},{1,3},{2,0},{3,1},{4,6},{5,7},{6,4},{7,5},{8,16},{9,17},{10,... | collective-permute-start | bytes 393224 | tf_op jit(solution)/shard_map/ppermute | solution.py:68
  (26 other events, 135.1 us)

commit v3 on v2

--- a/solution.py
+++ b/solution.py
@@ -14,21 +14,36 @@
 BF = jnp.bfloat16
 F32 = jnp.float32
 VMEM_LIMIT = 24 << 20
+CHUNKS = 4
 
 
 def dot(a, b):
     return jnp.dot(a, b, preferred_element_type=F32)
 
 
-def call(kernel, outs, args, flops, scratch=()):
+def call(kernel, outs, args, flops, scratch=(), far=(), far_out=False):
     moved = sum(a.size * a.dtype.itemsize for a in args)
+    vmem, hbm = pl.BlockSpec(memory_space=pltpu.VMEM), pl.BlockSpec(memory_space=pltpu.HBM)
+    out_spec = hbm if far_out else vmem
     return pl.pallas_call(
         kernel,
         out_shape=outs,
+        in_specs=[hbm if k in far else vmem for k in range(len(args))],
+        out_specs=[out_spec] * len(outs) if isinstance(outs, list) else out_spec,
         scratch_shapes=list(scratch),
         compiler_params=pltpu.CompilerParams(vmem_limit_bytes=VMEM_LIMIT),
         cost_estimate=pl.CostEstimate(flops=flops, transcendentals=0, bytes_accessed=moved),
     )(*args)
+
+
+def chunk_copies(source, target, sems, first, count):
+    rows = source.shape[0] // count
+    return [
+        pltpu.make_async_copy(
+            source.at[pl.ds(k * rows, rows)], target.at[pl.ds(k * rows, rows)], sems.at[first + k]
+        )
+        for k in range(count)
+    ]
 
 
 def shape(dims, dtype):
@@ -83,7 +98,12 @@
     return lists_ref[:, pl.ds(at, part)]
 
 
-def start_kernel(sizes, lists_ref, op_ref, u_ref, sel_ref, applied_ref, *edges):
+def start_kernel(sizes, lists_ref, op_hbm, u_hbm, sel_ref, op_ref, u_ref, applied_ref, *refs):
+    edges, sems = refs[:-1], refs[-1]
+    u_copies = chunk_copies(u_hbm, u_ref, sems, 0, CHUNKS)
+    op_copies = chunk_copies(op_hbm, op_ref, sems, CHUNKS, CHUNKS)
+    for copy in u_copies + op_copies:
+        copy.start()
     n = sel_ref.shape[0]
     part = n // 4
     for m in range(4):
@@ -92,14 +112,25 @@
         for j in range(n // 128):
             hit = names == lanes + j * 128
             sel_ref[m * part : (m + 1) * part, j * 128 : (j + 1) * 128] = jnp.where(hit, 1.0, 0.0).astype(BF)
-    applied = dot(op_ref[...], u_ref[...].astype(BF))
-    applied_ref[...] = applied
-    applied = applied.astype(BF)
+    for copy in u_copies:
+        copy.wait()
+    u = u_ref[...].astype(BF)
+    rows = n // CHUNKS
+    for k, copy in enumerate(op_copies):
+        copy.wait()
+        applied_ref[k * rows : (k + 1) * rows, :] = dot(op_ref[k * rows : (k + 1) * rows, :], u)
+    applied = applied_ref[...].astype(BF)
     for m, edge in enumerate(edges):
         edge[...] = dot(sel_ref[m * part : (m + 1) * part, :], applied).astype(BF)
 
 
-def tables_kernel(sizes, lists_ref, basis_t_ref, slot_ref, scatter_ref, based_ref, based_t_ref):
+def tables_kernel(
+    sizes, lists_ref, basis_t_ref, slot_ref, sel_ref, pre_hbm, load_hbm,
+    scatter_ref, based_ref, based_t_ref, pre_sel_ref, load_ref, pre_ref, sems,
+):
+    copies = chunk_copies(pre_hbm, pre_ref, sems, 0, CHUNKS) + chunk_copies(load_hbm, load_ref, sems, CHUNKS, CHUNKS)
+    for copy in copies:
+        copy.start()
     n = scatter_ref.shape[0]
     part = n // 4
     for m in range(4):
@@ -111,10 +142,12 @@
     based_t = dot(jnp.where(pick, 1.0, 0.0).astype(BF), basis_t_ref[...])
     based_t_ref[...] = based_t.astype(BF)
     based_ref[...] = based_t.T.astype(BF)
-
-
-def prepare_kernel(sel_ref, pre_ref, op_ref, based_ref, pre_sel_ref, lift_ref, lift_sel_ref):
+    for copy in copies:
+        copy.wait()
     pre_sel_ref[...] = dot(sel_ref[...], pre_ref[...]).astype(BF)
+
+
+def lift_kernel(sel_ref, op_ref, based_ref, lift_ref, lift_sel_ref):
     lift = dot(op_ref[...], based_ref[...]).astype(BF)
     lift_ref[...] = lift
     lift_sel_ref[...] = dot(sel_ref[...], lift).astype(BF)
@@ -200,8 +233,16 @@
 
 
 def last_kernel(u_ref, based_ref, mine_ref, *refs):
-    others, out_ref = refs[:-1], refs[-1]
-    out_ref[...] = u_ref[...] + OMEGA * dot(based_ref[...], solution_of(mine_ref, others))
+    others, (out_hbm, total, sems) = refs[:-3], refs[-3:]
+    solved = solution_of(mine_ref, others)
+    copies = chunk_copies(total, out_hbm, sems, 0, CHUNKS)
+    rows = total.shape[0] // CHUNKS
+    for k, copy in enumerate(copies):
+        at = slice(k * rows, (k + 1) * rows)
+        total[at, :] = u_ref[at, :] + OMEGA * dot(based_ref[at, :], solved)
+        copy.start()
+    for copy in copies:
+        copy.wait()
 
 
 def regroup_kernel(geometry, nb, inverse_ref, *blocks):
@@ -217,28 +258,71 @@
             block[line * nb : (line + 1) * nb, :] = inverse_ref[rows, cols]
 
 
-def coarse_kernel(geometry, row_size, nb, moves, *refs):
+def split_kernel(nb, inverse_hbm, keep_ref, give_ref, sems):
+    parity = lax.axis_index("col") % 2
+    copies = []
+    for line in range(keep_ref.shape[0] // nb):
+        for k, (ref, mine) in enumerate(((keep_ref, parity), (give_ref, 1 - parity))):
+            rows = pl.ds(pl.multiple_of((2 * line + mine) * nb, nb), nb)
+            copies.append(
+                pltpu.make_async_copy(inverse_hbm.at[rows], ref.at[pl.ds(line * nb, nb)], sems.at[2 * line + k])
+            )
+    for copy in copies:
+        copy.start()
+    for copy in copies:
+        copy.wait()
+
+
+def upper_kernel(top, mine_ref, got_ref, keep_ref, give_ref):
+    c = lax.axis_index("col")
+    same = c % 2 == c // top
+    keep_ref[...] = jnp.where(same, mine_ref[...], got_ref[...])
+    give_ref[...] = jnp.where(same, got_ref[...], mine_ref[...])
+
+
+def lower_kernel(first_ref, second_ref, keep_ref, give_ref):
+    low = (lax.axis_index("col") // 2) % 2
+    half = first_ref.shape[1] // 2
+    for k, source in enumerate((first_ref, second_ref)):
+        left, right = source[:, :half], source[:, half:]
+        keep_ref[:, k * half : (k + 1) * half] = jnp.where(low == 0, left, right)
+        give_ref[:, k * half : (k + 1) * half] = jnp.where(low == 0, right, left)
+
+
+def coarse_kernel(stepwise, geometry, row_size, nb, moves, *refs):
     grid_rows, _, lines = geometry
-    blocks, refs = refs[:grid_rows], refs[grid_rows:]
+    width = 2 * nb
+    count = 2 if stepwise else grid_rows
+    arrays, refs = refs[:count], refs[count:]
     vectors, refs = refs[: len(moves)], refs[len(moves) :]
     mine_ref, others, (stack, total) = refs[0], refs[1:lines], refs[lines:]
     g, r, c = (lax.axis_index(axis) for axis in AXES)
+    line = c // 2
     for (dg, dr, dc), vector in zip(moves, vectors):
         at = (((g ^ dg) * row_size + (r ^ dr)) * 2 + ((c % 2) ^ dc)) * nb
         stack[pl.ds(pl.multiple_of(at, nb), nb), :] = vector[...]
+    if stepwise:
+        blocks = [
+            (arrays[k // 2][:, (k % 2) * width : (k % 2 + 1) * width], line ^ (2 * (k % 2) + k // 2)) for k in range(4)
+        ]
+    else:
+        blocks = [(array[...], k ^ (c % grid_rows)) for k, array in enumerate(arrays)]
     acc = None
-    for k, block in enumerate(blocks):
-        owner = k ^ (c % grid_rows)
-        part = dot(block[...], stack[pl.ds(pl.multiple_of(owner * 2 * nb, 2 * nb), 2 * nb), :])
+    for block, owner in blocks:
+        part = dot(block, stack[pl.ds(pl.multiple_of(owner * width, width), width), :])
         acc = part if acc is None else acc + part
     total[...] = acc
-    line = c // 2
     for k in range(lines):
         got = total[pl.ds(pl.multiple_of((line ^ k) * nb, nb), nb), :]
         if k == 0:
             mine_ref[...] = got
         else:
             others[k - 1][...] = got.astype(BF)
+
+
+def in_steps(sizes):
+    grps, row_size, cols = sizes
+    return grps * row_size == 4 and cols == 2 * grps * row_size
 
 
 def body(load, guess, interface_op, precond, basis, coarse_inverse, edge_rows, coarse_slot):
@@ -274,21 +358,50 @@
     def halo(edges):
         return [send(e, p) for e, p in zip(edges, halo_pairs)]
 
-    blocks = call(
-        functools.partial(regroup_kernel, geometry, nb),
-        [shape((lines * nb, 2 * nb), BF)] * grid_rows,
-        [coarse_inverse],
-        n,
-    )
-    blocks = [send(block, target(k)) for k, block in enumerate(blocks)]
-    sel, applied, *edges = call(
-        functools.partial(start_kernel, sizes), [square, field] + [edge] * 4, [lists, op, u], 2 * flops
+    stepwise = in_steps(sizes)
+    if stepwise:
+        half = shape((lines * nb, coarse_inverse.shape[1]), BF)
+        keep, give = call(
+            functools.partial(split_kernel, nb),
+            [half, half],
+            [coarse_inverse],
+            n,
+            [pltpu.SemaphoreType.DMA((2 * lines,))],
+            far=(0,),
+        )
+        got = send(give, swap_pairs(0, 0, 1))
+    else:
+        blocks = call(
+            functools.partial(regroup_kernel, geometry, nb),
+            [shape((lines * nb, 2 * nb), BF)] * grid_rows,
+            [coarse_inverse],
+            n,
+        )
+        blocks = [send(block, target(k)) for k, block in enumerate(blocks)]
+    sems = pltpu.SemaphoreType.DMA((2 * CHUNKS,))
+    sel, op, u, applied, *edges = call(
+        functools.partial(start_kernel, sizes),
+        [square, square, field, field] + [edge] * 4,
+        [lists, op, u],
+        2 * flops,
+        [sems],
+        far=(1, 2),
     )
     near = halo(edges)
-    scatter, based, based_t = call(
-        functools.partial(tables_kernel, sizes), [square, thin, shape((nb, n), BF)], [lists, basis_t, slot], n * n
+    if stepwise:
+        keep, give = call(functools.partial(upper_kernel, cols // 2), [half, half], [keep, got], n)
+        got = send(give, swap_pairs(0, 0, cols // 2))
+    scatter, based, based_t, pre_sel, load = call(
+        functools.partial(tables_kernel, sizes),
+        [square, thin, shape((nb, n), BF), square, field],
+        [lists, basis_t, slot, sel, pre, load],
+        2 * n * n * n,
+        [pltpu.VMEM((n, n), BF), sems],
+        far=(4, 5),
     )
-    pre_sel, lift, lift_sel = call(prepare_kernel, [square, thin, thin], [sel, pre, op, based], 2 * n * n * n)
+    if stepwise:
+        keep, give = call(lower_kernel, [half, half], [keep, got], n)
+        blocks = [keep, send(give, swap_pairs(0, 0, 2))]
 
     scratch = [pltpu.VMEM((n, cases), BF)]
     for sweep in range(ITERS):
@@ -308,7 +421,7 @@
         fix, *own = call(fix_kernel, [field] + [edge] * 4, [pre_sel, resid], flops)
         near = halo(own)
         mine, *others = call(
-            functools.partial(coarse_kernel, geometry, row_size, nb, moves),
+            functools.partial(coarse_kernel, stepwise, geometry, row_size, nb, moves),
             [shape((nb, cases), F32)] + [vector] * (lines - 1),
             [*blocks, *(vectors[move] for move in moves)],
             2 * lines * nb * 2 * nb * grid_rows * cases,
@@ -316,6 +429,7 @@
         )
         others = [send(o, swap_pairs(0, 0, 2 * (k + 1))) for k, o in enumerate(others)]
         if sweep < ITERS - 1:
+            lift, lift_sel = call(lift_kernel, [thin, thin], [sel, op, based], n * n * nb)
             inputs = [u, fix, scatter, *near]
             u, applied, edge_part = call(
                 functools.partial(middle_kernel, sizes), [field] * 3, [op, sel, *inputs], 3 * flops, scratch
@@ -331,7 +445,14 @@
             u = call(
                 functools.partial(late_kernel, sizes), field, [u, fix, scatter, based, solved, *near], flops, scratch
             )
-            u = call(last_kernel, field, [u, based, mine, *others], n * nb * cases)
+            u = call(
+                last_kernel,
+                field,
+                [u, based, mine, *others],
+                n * nb * cases,
+                [pltpu.VMEM((n, cases), F32), pltpu.SemaphoreType.DMA((CHUNKS,))],
+                far_out=True,
+            )
     return u[None, None]
 
 

time: 86.9 us -> 80.3 us (0.924)
  waiting for transfers between devices: 17.6 us -> 11.9 us
  starting transfers between devices: 46.1 us -> 44.1 us
  Pallas kernels: 17.4 us -> 19.1 us
    ppermute x40 -> x39, waiting for transfers between devices: 17.6 us -> 11.9 us  [send(): return lax.ppermute(value, AXES, pairs)]
    ppermute x40 -> x39, starting transfers between devices: 46.1 us -> 44.1 us  [send(): return lax.ppermute(value, AXES, pairs)]
    pallas_call x14 -> x16, Pallas kernels: 17.4 us -> 19.1 us  [call(): pl.pallas_call(kernel, out_shape=outs, in_specs=[hbm if k in far else vme...]
    unnamed x20 -> x16, local copies, waits for them, and re-layouts: 5.12 us -> 4.47 us
  transfers between devices with their start and end apart: 40 -> 39, of which waited for: 13 -> 11; matrix products, arithmetic and copies ran while one was open for 0% -> 0% of each run, Pallas kernels for 14% -> 20%
where the time goes in v3:
time: 80.3 us; the launch traced here: 80 us
  starting transfers between devices  44.1 us (55%)
  Pallas kernels  19.1 us (24%)
  waiting for transfers between devices  11.9 us (15%)
  local copies, waits for them, and re-layouts  4.47 us (6%)
    ppermute x39, starting transfers between devices, send(): return lax.ppermute(value, AXES, pairs)  44.1 us
    pallas_call x16, Pallas kernels, call(): pl.pallas_call(kernel, out_shape=outs, in_specs=[hbm if k in far else vme...  19.1 us
    ppermute x39, waiting for transfers between devices, send(): return lax.ppermute(value, AXES, pairs)  11.9 us
    unnamed x16, local copies, waits for them, and re-layouts  4.47 us
  transfers between devices with their start and end apart: 39, of which 11 were waited for; matrix products, arithmetic and copies ran while one was open for 0% of the time, Pallas kernels for 20%

profile of v3, /device:TPU:0, one launch (start us, length us, event | category | flops | bytes accessed | tf_op | source)
XLA Modules:
  0.0 80.0 jit_solution(3422245772272684270)
XLA Ops:
  1.4 3.0 %collective-permute-start.8 = (bf16[256,256]{1,0:T(8,128)(2,1)S(1)}, bf16[256,256]{1,0:T(8,128)(2,1)S(1)}, u32[]{:S(2)}, u32[]{:S(2)}) collective-permute-start(bf16[256,256]{1,0:T(8,128)(2,1)S(1)} %get-tuple-element.82), channel_id=1, source_target_pairs={{0,1},{1,0},{2,3},{3,2},{4,5},{5,4},{6,7},{7,6},{8,9},{9,8},{10,11... | collective-permute-start | bytes 393224 | tf_op jit(solution)/shard_map/ppermute | solution.py:83
  4.4 1.6 %copy-done.1 = bf16[1,1,1024,1024]{3,2,1,0:T(8,128)(2,1)S(1)} copy-done((bf16[1,1,1024,1024]{3,2,1,0:T(8,128)(2,1)S(1)}, bf16[1,1,1024,1024]{3,2,1,0:T(8,128)(2,1)}, u32[]{:S(2)}) %copy-start.1) | copy-done | bytes 2097176
  7.9 3.1 %shard_map.82 = (bf16[1024,1024]{1,0:T(8,128)(2,1)S(1)}, bf16[1024,1024]{1,0:T(8,128)(2,1)S(1)}, f32[1024,256]{1,0:T(8,128)S(1)}, f32[1024,256]{1,0:T(8,128)S(1)...) custom-call(s32[1,1024]{1,0:T(1,128)S(1)} %bitcast.15, ...), custom_call_target="tpu_custom_call" | custom-call | flops 1073741824 | bytes 3149824 | tf_op jit(solution)/shard_map/pallas_call | solution.py:28
  11.1 2.0 %collective-permute-start.2 = (bf16[256,256]{1,0:T(8,128)(2,1)S(1)}, bf16[256,256]{1,0:T(8,128)(2,1)S(1)}, u32[]{:S(2)}, u32[]{:S(2)}) collective-permute-start(bf16[256,256]{1,0:T(8,128)(2,1)S(1)} %get-tuple-element.67), channel_id=1, source_target_pairs={{0,8},{1,9},{2,10},{3,11},{4,12},{5,13},{6,14},{7,15},{8,0},{9,1},... | collective-permute-start | bytes 393224 | tf_op jit(solution)/shard_map/ppermute | solution.py:83
  13.1 2.9 %collective-permute-start.3 = (bf16[256,256]{1,0:T(8,128)(2,1)S(1)}, bf16[256,256]{1,0:T(8,128)(2,1)S(1)}, u32[]{:S(2)}, u32[]{:S(2)}) collective-permute-start(bf16[256,256]{1,0:T(8,128)(2,1)S(1)} %get-tuple-element.68), channel_id=1, source_target_pairs={{0,2},{1,3},{2,0},{3,1},{4,6},{5,7},{6,4},{7,5},{8,16},{9,17},{10,... | collective-permute-start | bytes 393224 | tf_op jit(solution)/shard_map/ppermute | solution.py:83
  16.1 2.7 %collective-permute-start.9 = (bf16[256,256]{1,0:T(8,128)(2,1)S(1)}, bf16[256,256]{1,0:T(8,128)(2,1)S(1)}, u32[]{:S(2)}, u32[]{:S(2)}) collective-permute-start(bf16[256,256]{1,0:T(8,128)(2,1)S(1)} %get-tuple-element.84), channel_id=1, source_target_pairs={{0,4},{1,5},{2,6},{3,7},{4,0},{5,1},{6,2},{7,3},{8,12},{9,13},{10,... | collective-permute-start | bytes 393224 | tf_op jit(solution)/shard_map/ppermute | solution.py:83
  18.8 4.0 %shard_map.83 = (bf16[1024,1024]{1,0:T(8,128)(2,1)S(1)}, bf16[1024,64]{1,0:T(8,128)(2,1)S(1)}, bf16[64,1024]{1,0:T(8,128)(2,1)S(1)}, bf16[1024,1024]{1,0:T(8,128)(2,1)S(1)}, f32[1024,256]{1,0:T(8,128)S(1)}) custom-call(s32[1,1024]{1,0:T(1,128)S(1)} %bitcast.16, bf16[64,1024]{1,0:T(8,128)(2,1)S(1)} %bitcast.14, s32[1,64]{1,0:T(1,128)S(1)} %bitcast.17, ...), custom_call_target="tpu_custom_call" | custom-call | flops 2147483648 | bytes 5378304 | tf_op jit(solution)/shard_map/pallas_call | solution.py:28
  24.7 2.6 %collective-permute-start.16 = (bf16[64,256]{1,0:T(8,128)(2,1)S(1)}, bf16[64,256]{1,0:T(8,128)(2,1)S(1)}, u32[]{:S(2)}, u32[]{:S(2)}) collective-permute-start(bf16[64,256]{1,0:T(8,128)(2,1)S(1)} %get-tuple-element.87.refs_2_), channel_id=1, source_target_pairs={{0,9},{1,8},{2,11},{3,10},{4,13},{5,12},{6,15},{7,14},{8,1},{9,0},... | collective-permute-start | bytes 98312 | tf_op jit(solution)/shard_map/ppermute | solution.py:83
  32.3 1.9 %collective-permute-start.6 = (bf16[256,256]{1,0:T(8,128)(2,1)S(1)}, bf16[256,256]{1,0:T(8,128)(2,1)S(1)}, u32[]{:S(2)}, u32[]{:S(2)}) collective-permute-start(bf16[256,256]{1,0:T(8,128)(2,1)S(1)} %get-tuple-element.73), channel_id=1, source_target_pairs={{0,8},{1,9},{2,10},{3,11},{4,12},{5,13},{6,14},{7,15},{8,0},{9,1},... | collective-permute-start | bytes 393224 | tf_op jit(solution)/shard_map/ppermute | solution.py:83
  34.2 3.1 %collective-permute-start.7 = (bf16[256,256]{1,0:T(8,128)(2,1)S(1)}, bf16[256,256]{1,0:T(8,128)(2,1)S(1)}, u32[]{:S(2)}, u32[]{:S(2)}) collective-permute-start(bf16[256,256]{1,0:T(8,128)(2,1)S(1)} %get-tuple-element.74), channel_id=1, source_target_pairs={{0,2},{1,3},{2,0},{3,1},{4,6},{5,7},{6,4},{7,5},{8,16},{9,17},{10,... | collective-permute-start | bytes 393224 | tf_op jit(solution)/shard_map/ppermute | solution.py:83
  37.3 2.2 %shard_map.87 = (bf16[1024,64]{1,0:T(8,128)(2,1)S(1)}, bf16[1024,64]{1,0:T(8,128)(2,1)S(1)}) custom-call(bf16[1024,1024]{1,0:T(8,128)(2,1)S(1)} %get-tuple-element.58.sel_ref, bf16[1024,1024]{1,0:T(8,128)(2,1)S(1)} %get-tuple-element.57.op_ref, bf16[1024,64]{1,0:T(8,128)(2,1)S(1)} %get-tuple-element.76.based_ref), custom_call_target="tpu_custom_call" | custom-call | flops 67108864 | bytes 4325376 | tf_op jit(solution)/shard_map/pallas_call | solution.py:28
  39.9 1.5 %collective-permute-start.19 = (bf16[64,256]{1,0:T(8,128)(2,1)S(1)}, bf16[64,256]{1,0:T(8,128)(2,1)S(1)}, u32[]{:S(2)}, u32[]{:S(2)}) collective-permute-start(bf16[64,256]{1,0:T(8,128)(2,1)S(1)} %get-tuple-element.90), channel_id=1, source_target_pairs={{0,4},{1,5},{2,6},{3,7},{4,0},{5,1},{6,2},{7,3},{8,12},{9,13},{10,... | collective-permute-start | bytes 98312 | tf_op jit(solution)/shard_map/ppermute | solution.py:83
  41.4 2.9 %collective-permute-start.20 = (bf16[64,256]{1,0:T(8,128)(2,1)S(1)}, bf16[64,256]{1,0:T(8,128)(2,1)S(1)}, u32[]{:S(2)}, u32[]{:S(2)}) collective-permute-start(bf16[64,256]{1,0:T(8,128)(2,1)S(1)} %get-tuple-element.91), channel_id=1, source_target_pairs={{0,6},{1,7},{2,4},{3,5},{4,2},{5,3},{6,0},{7,1},{8,14},{9,15},{10,... | collective-permute-start | bytes 98312 | tf_op jit(solution)/shard_map/ppermute | solution.py:83
  44.3 2.8 %shard_map.86 = (f32[1024,256]{1,0:T(8,128)S(1)}, f32[1024,256]{1,0:T(8,128)S(1)}, f32[1024,256]{1,0:T(8,128)S(1)}) custom-call(bf16[1024,1024]{1,0:T(8,128)(2,1)S(1)} %get-tuple-element.57.op_ref, bf16[1024,1024]{1,0:T(8,128)(2,1)S(1)} %get-tuple-element.58.sel_ref, f32[1024,256]{1,0:T(8,128)S(1)} %get-tuple-element.59.u_ref, ...), custom_call_target="tpu_custom_call" | custom-call | flops 1610612736 | bytes 8912896 | tf_op jit(solution)/shard_map/pallas_call | solution.py:28
  47.6 1.4 %collective-permute-start.21 = (bf16[256,256]{1,0:T(8,128)(2,1)S(1)}, bf16[256,256]{1,0:T(8,128)(2,1)S(1)}, u32[]{:S(2)}, u32[]{:S(2)}) collective-permute-start(bf16[256,256]{1,0:T(8,128)(2,1)S(1)} %get-tuple-element.93), channel_id=1, source_target_pairs={{0,1},{1,0},{2,3},{3,2},{4,5},{5,4},{6,7},{7,6},{8,9},{9,8},{10,11... | collective-permute-start | bytes 393224 | tf_op jit(solution)/shard_map/ppermute | solution.py:83
  49.9 2.4 %collective-permute-start.24 = (bf16[256,256]{1,0:T(8,128)(2,1)S(1)}, bf16[256,256]{1,0:T(8,128)(2,1)S(1)}, u32[]{:S(2)}, u32[]{:S(2)}) collective-permute-start(bf16[256,256]{1,0:T(8,128)(2,1)S(1)} %get-tuple-element.96), channel_id=1, source_target_pairs={{0,2},{1,3},{2,0},{3,1},{4,6},{5,7},{6,4},{7,5},{8,16},{9,17},{10,... | collective-permute-start | bytes 393224 | tf_op jit(solution)/shard_map/ppermute | solution.py:83
  52.6 2.3 %collective-permute-done.23.n2 = bf16[256,256]{1,0:T(8,128)(2,1)S(1)} collective-permute-done((bf16[256,256]{1,0:T(8,128)(2,1)S(1)}, bf16[256,256]{1,0:T(8,128)(2,1)S(1)}, u32[]{:S(2)}, u32[]{:S(2)}) %collective-permute-start.23) | collective-permute-done | bytes 131104 | tf_op jit(solution)/shard_map/ppermute | solution.py:83
  57.3 1.7 %collective-permute-start.32 = (bf16[64,256]{1,0:T(8,128)(2,1)S(1)}, bf16[64,256]{1,0:T(8,128)(2,1)S(1)}, u32[]{:S(2)}, u32[]{:S(2)}) collective-permute-start(bf16[64,256]{1,0:T(8,128)(2,1)S(1)} %get-tuple-element.104.refs_2_), channel_id=1, source_target_pairs={{0,8},{1,9},{2,10},{3,11},{4,12},{5,13},{6,14},{7,15},{8,0},{9,1},... | collective-permute-start | bytes 98312 | tf_op jit(solution)/shard_map/ppermute | solution.py:83
  59.0 1.6 %collective-permute-start.34 = (bf16[64,256]{1,0:T(8,128)(2,1)S(1)}, bf16[64,256]{1,0:T(8,128)(2,1)S(1)}, u32[]{:S(2)}, u32[]{:S(2)}) collective-permute-start(bf16[64,256]{1,0:T(8,128)(2,1)S(1)} %get-tuple-element.104.refs_2_), channel_id=1, source_target_pairs={{0,9},{1,8},{2,11},{3,10},{4,13},{5,12},{6,15},{7,14},{8,1},{9,0},... | collective-permute-start | bytes 98312 | tf_op jit(solution)/shard_map/ppermute | solution.py:83
  61.6 1.7 %collective-permute-start.27 = (bf16[256,256]{1,0:T(8,128)(2,1)S(1)}, bf16[256,256]{1,0:T(8,128)(2,1)S(1)}, u32[]{:S(2)}, u32[]{:S(2)}) collective-permute-start(bf16[256,256]{1,0:T(8,128)(2,1)S(1)} %get-tuple-element.102), channel_id=1, source_target_pairs={{0,8},{1,9},{2,10},{3,11},{4,12},{5,13},{6,14},{7,15},{8,0},{9,1},... | collective-permute-start | bytes 393224 | tf_op jit(solution)/shard_map/ppermute | solution.py:83
  63.4 2.7 %collective-permute-start.28 = (bf16[256,256]{1,0:T(8,128)(2,1)S(1)}, bf16[256,256]{1,0:T(8,128)(2,1)S(1)}, u32[]{:S(2)}, u32[]{:S(2)}) collective-permute-start(bf16[256,256]{1,0:T(8,128)(2,1)S(1)} %get-tuple-element.103), channel_id=1, source_target_pairs={{0,2},{1,3},{2,0},{3,1},{4,6},{5,7},{6,4},{7,5},{8,16},{9,17},{10,... | collective-permute-start | bytes 393224 | tf_op jit(solution)/shard_map/ppermute | solution.py:83
  70.7 2.2 %collective-permute-start.37 = (bf16[64,256]{1,0:T(8,128)(2,1)S(1)}, bf16[64,256]{1,0:T(8,128)(2,1)S(1)}, u32[]{:S(2)}, u32[]{:S(2)}) collective-permute-start(bf16[64,256]{1,0:T(8,128)(2,1)S(1)} %get-tuple-element.107), channel_id=1, source_target_pairs={{0,4},{1,5},{2,6},{3,7},{4,0},{5,1},{6,2},{7,3},{8,12},{9,13},{10,... | collective-permute-start | bytes 98312 | tf_op jit(solution)/shard_map/ppermute | solution.py:83
  72.9 1.5 %collective-permute-start.38 = (bf16[64,256]{1,0:T(8,128)(2,1)S(1)}, bf16[64,256]{1,0:T(8,128)(2,1)S(1)}, u32[]{:S(2)}, u32[]{:S(2)}) collective-permute-start(bf16[64,256]{1,0:T(8,128)(2,1)S(1)} %get-tuple-element.108), channel_id=1, source_target_pairs={{0,6},{1,7},{2,4},{3,5},{4,2},{5,3},{6,0},{7,1},{8,14},{9,15},{10,... | collective-permute-start | bytes 98312 | tf_op jit(solution)/shard_map/ppermute | solution.py:83
  75.9 2.7 %collective-permute-done.38.refs_2_ = bf16[64,256]{1,0:T(8,128)(2,1)S(1)} collective-permute-done((bf16[64,256]{1,0:T(8,128)(2,1)S(1)}, bf16[64,256]{1,0:T(8,128)(2,1)S(1)}, u32[]{:S(2)}, u32[]{:S(2)}) %collective-permute-start.38) | collective-permute-done | bytes 32800 | tf_op jit(solution)/shard_map/ppermute | solution.py:83
  (86 shorter events, 23.2 us)
Async XLA Ops:
  1.4 14.7 %collective-permute-start.8 = (bf16[256,256]{1,0:T(8,128)(2,1)S(1)}, bf16[256,256]{1,0:T(8,128)(2,1)S(1)}, u32[]{:S(2)}, u32[]{:S(2)}) collective-permute-start(bf16[256,256]{1,0:T(8,128)(2,1)S(1)} %get-tuple-element.82), channel_id=1, source_target_pairs={{0,1},{1,0},{2,3},{3,2},{4,5},{5,4},{6,7},{7,6},{8,9},{9,8},{10,11... | collective-permute-start | bytes 393224 | tf_op jit(solution)/shard_map/ppermute | solution.py:83
  11.0 11.8 %collective-permute-start = (bf16[256,256]{1,0:T(8,128)(2,1)S(1)}, bf16[256,256]{1,0:T(8,128)(2,1)S(1)}, u32[]{:S(2)}, u32[]{:S(2)}) collective-permute-start(bf16[256,256]{1,0:T(8,128)(2,1)S(1)} %get-tuple-element.65), channel_id=1, source_target_pairs={{0,1},{1,0},{2,3},{3,2},{4,5},{5,4},{6,7},{7,6},{8,9},{9,8},{10,11... | collective-permute-start | bytes 393224 | tf_op jit(solution)/shard_map/ppermute | solution.py:83
  11.1 11.7 %collective-permute-start.1 = (bf16[256,256]{1,0:T(8,128)(2,1)S(1)}, bf16[256,256]{1,0:T(8,128)(2,1)S(1)}, u32[]{:S(2)}, u32[]{:S(2)}) collective-permute-start(bf16[256,256]{1,0:T(8,128)(2,1)S(1)} %get-tuple-element.66), channel_id=1, source_target_pairs={{0,16},{1,2},{2,1},{3,4},{4,3},{5,6},{6,5},{7,23},{8,24},{9,10},{1... | collective-permute-start | bytes 393224 | tf_op jit(solution)/shard_map/ppermute | solution.py:83
  11.1 11.7 %collective-permute-start.2 = (bf16[256,256]{1,0:T(8,128)(2,1)S(1)}, bf16[256,256]{1,0:T(8,128)(2,1)S(1)}, u32[]{:S(2)}, u32[]{:S(2)}) collective-permute-start(bf16[256,256]{1,0:T(8,128)(2,1)S(1)} %get-tuple-element.67), channel_id=1, source_target_pairs={{0,8},{1,9},{2,10},{3,11},{4,12},{5,13},{6,14},{7,15},{8,0},{9,1},... | collective-permute-start | bytes 393224 | tf_op jit(solution)/shard_map/ppermute | solution.py:83
  13.1 9.7 %collective-permute-start.3 = (bf16[256,256]{1,0:T(8,128)(2,1)S(1)}, bf16[256,256]{1,0:T(8,128)(2,1)S(1)}, u32[]{:S(2)}, u32[]{:S(2)}) collective-permute-start(bf16[256,256]{1,0:T(8,128)(2,1)S(1)} %get-tuple-element.68), channel_id=1, source_target_pairs={{0,2},{1,3},{2,0},{3,1},{4,6},{5,7},{6,4},{7,5},{8,16},{9,17},{10,... | collective-permute-start | bytes 393224 | tf_op jit(solution)/shard_map/ppermute | solution.py:83
  16.1 13.5 %collective-permute-start.9 = (bf16[256,256]{1,0:T(8,128)(2,1)S(1)}, bf16[256,256]{1,0:T(8,128)(2,1)S(1)}, u32[]{:S(2)}, u32[]{:S(2)}) collective-permute-start(bf16[256,256]{1,0:T(8,128)(2,1)S(1)} %get-tuple-element.84), channel_id=1, source_target_pairs={{0,4},{1,5},{2,6},{3,7},{4,0},{5,1},{6,2},{7,3},{8,12},{9,13},{10,... | collective-permute-start | bytes 393224 | tf_op jit(solution)/shard_map/ppermute | solution.py:83
  29.6 9.9 %collective-permute-start.10 = (bf16[256,256]{1,0:T(8,128)(2,1)S(1)}, bf16[256,256]{1,0:T(8,128)(2,1)S(1)}, u32[]{:S(2)}, u32[]{:S(2)}) collective-permute-start(bf16[256,256]{1,0:T(8,128)(2,1)S(1)} %get-tuple-element.86), channel_id=1, source_target_pairs={{0,2},{1,3},{2,0},{3,1},{4,6},{5,7},{6,4},{7,5},{8,10},{9,11},{10,... | collective-permute-start | bytes 393224 | tf_op jit(solution)/shard_map/ppermute | solution.py:83
  31.7 8.2 %collective-permute-start.4 = (bf16[256,256]{1,0:T(8,128)(2,1)S(1)}, bf16[256,256]{1,0:T(8,128)(2,1)S(1)}, u32[]{:S(2)}, u32[]{:S(2)}) collective-permute-start(bf16[256,256]{1,0:T(8,128)(2,1)S(1)} %get-tuple-element.71), channel_id=1, source_target_pairs={{0,1},{1,0},{2,3},{3,2},{4,5},{5,4},{6,7},{7,6},{8,9},{9,8},{10,11... | collective-permute-start | bytes 393224 | tf_op jit(solution)/shard_map/ppermute | solution.py:83
  32.3 9.1 %collective-permute-start.5 = (bf16[256,256]{1,0:T(8,128)(2,1)S(1)}, bf16[256,256]{1,0:T(8,128)(2,1)S(1)}, u32[]{:S(2)}, u32[]{:S(2)}) collective-permute-start(bf16[256,256]{1,0:T(8,128)(2,1)S(1)} %get-tuple-element.72), channel_id=1, source_target_pairs={{0,16},{1,2},{2,1},{3,4},{4,3},{5,6},{6,5},{7,23},{8,24},{9,10},{1... | collective-permute-start | bytes 393224 | tf_op jit(solution)/shard_map/ppermute | solution.py:83
  32.3 12.0 %collective-permute-start.6 = (bf16[256,256]{1,0:T(8,128)(2,1)S(1)}, bf16[256,256]{1,0:T(8,128)(2,1)S(1)}, u32[]{:S(2)}, u32[]{:S(2)}) collective-permute-start(bf16[256,256]{1,0:T(8,128)(2,1)S(1)} %get-tuple-element.73), channel_id=1, source_target_pairs={{0,8},{1,9},{2,10},{3,11},{4,12},{5,13},{6,14},{7,15},{8,0},{9,1},... | collective-permute-start | bytes 393224 | tf_op jit(solution)/shard_map/ppermute | solution.py:83
  34.2 10.1 %collective-permute-start.7 = (bf16[256,256]{1,0:T(8,128)(2,1)S(1)}, bf16[256,256]{1,0:T(8,128)(2,1)S(1)}, u32[]{:S(2)}, u32[]{:S(2)}) collective-permute-start(bf16[256,256]{1,0:T(8,128)(2,1)S(1)} %get-tuple-element.74), channel_id=1, source_target_pairs={{0,2},{1,3},{2,0},{3,1},{4,6},{5,7},{6,4},{7,5},{8,16},{9,17},{10,... | collective-permute-start | bytes 393224 | tf_op jit(solution)/shard_map/ppermute | solution.py:83
  39.8 7.3 %collective-permute-start.18 = (bf16[64,256]{1,0:T(8,128)(2,1)S(1)}, bf16[64,256]{1,0:T(8,128)(2,1)S(1)}, u32[]{:S(2)}, u32[]{:S(2)}) collective-permute-start(bf16[64,256]{1,0:T(8,128)(2,1)S(1)} %get-tuple-element.89), channel_id=1, source_target_pairs={{0,2},{1,3},{2,0},{3,1},{4,6},{5,7},{6,4},{7,5},{8,10},{9,11},{10,... | collective-permute-start | bytes 98312 | tf_op jit(solution)/shard_map/ppermute | solution.py:83
  39.9 7.2 %collective-permute-start.19 = (bf16[64,256]{1,0:T(8,128)(2,1)S(1)}, bf16[64,256]{1,0:T(8,128)(2,1)S(1)}, u32[]{:S(2)}, u32[]{:S(2)}) collective-permute-start(bf16[64,256]{1,0:T(8,128)(2,1)S(1)} %get-tuple-element.90), channel_id=1, source_target_pairs={{0,4},{1,5},{2,6},{3,7},{4,0},{5,1},{6,2},{7,3},{8,12},{9,13},{10,... | collective-permute-start | bytes 98312 | tf_op jit(solution)/shard_map/ppermute | solution.py:83
  41.4 5.8 %collective-permute-start.20 = (bf16[64,256]{1,0:T(8,128)(2,1)S(1)}, bf16[64,256]{1,0:T(8,128)(2,1)S(1)}, u32[]{:S(2)}, u32[]{:S(2)}) collective-permute-start(bf16[64,256]{1,0:T(8,128)(2,1)S(1)} %get-tuple-element.91), channel_id=1, source_target_pairs={{0,6},{1,7},{2,4},{3,5},{4,2},{5,3},{6,0},{7,1},{8,14},{9,15},{10,... | collective-permute-start | bytes 98312 | tf_op jit(solution)/shard_map/ppermute | solution.py:83
  49.0 5.9 %collective-permute-start.23 = (bf16[256,256]{1,0:T(8,128)(2,1)S(1)}, bf16[256,256]{1,0:T(8,128)(2,1)S(1)}, u32[]{:S(2)}, u32[]{:S(2)}) collective-permute-start(bf16[256,256]{1,0:T(8,128)(2,1)S(1)} %get-tuple-element.95), channel_id=1, source_target_pairs={{0,8},{1,9},{2,10},{3,11},{4,12},{5,13},{6,14},{7,15},{8,0},{9,1},... | collective-permute-start | bytes 393224 | tf_op jit(solution)/shard_map/ppermute | solution.py:83
  49.9 5.6 %collective-permute-start.24 = (bf16[256,256]{1,0:T(8,128)(2,1)S(1)}, bf16[256,256]{1,0:T(8,128)(2,1)S(1)}, u32[]{:S(2)}, u32[]{:S(2)}) collective-permute-start(bf16[256,256]{1,0:T(8,128)(2,1)S(1)} %get-tuple-element.96), channel_id=1, source_target_pairs={{0,2},{1,3},{2,0},{3,1},{4,6},{5,7},{6,4},{7,5},{8,16},{9,17},{10,... | collective-permute-start | bytes 393224 | tf_op jit(solution)/shard_map/ppermute | solution.py:83
  57.3 6.0 %collective-permute-start.32 = (bf16[64,256]{1,0:T(8,128)(2,1)S(1)}, bf16[64,256]{1,0:T(8,128)(2,1)S(1)}, u32[]{:S(2)}, u32[]{:S(2)}) collective-permute-start(bf16[64,256]{1,0:T(8,128)(2,1)S(1)} %get-tuple-element.104.refs_2_), channel_id=1, source_target_pairs={{0,8},{1,9},{2,10},{3,11},{4,12},{5,13},{6,14},{7,15},{8,0},{9,1},... | collective-permute-start | bytes 98312 | tf_op jit(solution)/shard_map/ppermute | solution.py:83
  59.0 7.0 %collective-permute-start.34 = (bf16[64,256]{1,0:T(8,128)(2,1)S(1)}, bf16[64,256]{1,0:T(8,128)(2,1)S(1)}, u32[]{:S(2)}, u32[]{:S(2)}) collective-permute-start(bf16[64,256]{1,0:T(8,128)(2,1)S(1)} %get-tuple-element.104.refs_2_), channel_id=1, source_target_pairs={{0,9},{1,8},{2,11},{3,10},{4,13},{5,12},{6,15},{7,14},{8,1},{9,0},... | collective-permute-start | bytes 98312 | tf_op jit(solution)/shard_map/ppermute | solution.py:83
  61.3 9.4 %collective-permute-start.25 = (bf16[256,256]{1,0:T(8,128)(2,1)S(1)}, bf16[256,256]{1,0:T(8,128)(2,1)S(1)}, u32[]{:S(2)}, u32[]{:S(2)}) collective-permute-start(bf16[256,256]{1,0:T(8,128)(2,1)S(1)} %get-tuple-element.100), channel_id=1, source_target_pairs={{0,1},{1,0},{2,3},{3,2},{4,5},{5,4},{6,7},{7,6},{8,9},{9,8},{10,11... | collective-permute-start | bytes 393224 | tf_op jit(solution)/shard_map/ppermute | solution.py:83
  61.6 11.3 %collective-permute-start.26 = (bf16[256,256]{1,0:T(8,128)(2,1)S(1)}, bf16[256,256]{1,0:T(8,128)(2,1)S(1)}, u32[]{:S(2)}, u32[]{:S(2)}) collective-permute-start(bf16[256,256]{1,0:T(8,128)(2,1)S(1)} %get-tuple-element.101), channel_id=1, source_target_pairs={{0,16},{1,2},{2,1},{3,4},{4,3},{5,6},{6,5},{7,23},{8,24},{9,10},{1... | collective-permute-start | bytes 393224 | tf_op jit(solution)/shard_map/ppermute | solution.py:83
  61.6 12.8 %collective-permute-start.27 = (bf16[256,256]{1,0:T(8,128)(2,1)S(1)}, bf16[256,256]{1,0:T(8,128)(2,1)S(1)}, u32[]{:S(2)}, u32[]{:S(2)}) collective-permute-start(bf16[256,256]{1,0:T(8,128)(2,1)S(1)} %get-tuple-element.102), channel_id=1, source_target_pairs={{0,8},{1,9},{2,10},{3,11},{4,12},{5,13},{6,14},{7,15},{8,0},{9,1},... | collective-permute-start | bytes 393224 | tf_op jit(solution)/shard_map/ppermute | solution.py:83
  63.4 11.1 %collective-permute-start.28 = (bf16[256,256]{1,0:T(8,128)(2,1)S(1)}, bf16[256,256]{1,0:T(8,128)(2,1)S(1)}, u32[]{:S(2)}, u32[]{:S(2)}) collective-permute-start(bf16[256,256]{1,0:T(8,128)(2,1)S(1)} %get-tuple-element.103), channel_id=1, source_target_pairs={{0,2},{1,3},{2,0},{3,1},{4,6},{5,7},{6,4},{7,5},{8,16},{9,17},{10,... | collective-permute-start | bytes 393224 | tf_op jit(solution)/shard_map/ppermute | solution.py:83
  70.0 5.4 %collective-permute-start.36 = (bf16[64,256]{1,0:T(8,128)(2,1)S(1)}, bf16[64,256]{1,0:T(8,128)(2,1)S(1)}, u32[]{:S(2)}, u32[]{:S(2)}) collective-permute-start(bf16[64,256]{1,0:T(8,128)(2,1)S(1)} %get-tuple-element.106), channel_id=1, source_target_pairs={{0,2},{1,3},{2,0},{3,1},{4,6},{5,7},{6,4},{7,5},{8,10},{9,11},{10,... | collective-permute-start | bytes 98312 | tf_op jit(solution)/shard_map/ppermute | solution.py:83
  72.9 5.7 %collective-permute-start.38 = (bf16[64,256]{1,0:T(8,128)(2,1)S(1)}, bf16[64,256]{1,0:T(8,128)(2,1)S(1)}, u32[]{:S(2)}, u32[]{:S(2)}) collective-permute-start(bf16[64,256]{1,0:T(8,128)(2,1)S(1)} %get-tuple-element.108), channel_id=1, source_target_pairs={{0,6},{1,7},{2,4},{3,5},{4,2},{5,3},{6,0},{7,1},{8,14},{9,15},{10,... | collective-permute-start | bytes 98312 | tf_op jit(solution)/shard_map/ppermute | solution.py:83
  (23 other events, 105.6 us)

commit v4 on v3

--- a/solution.py
+++ b/solution.py
@@ -25,6 +25,7 @@
     moved = sum(a.size * a.dtype.itemsize for a in args)
     vmem, hbm = pl.BlockSpec(memory_space=pltpu.VMEM), pl.BlockSpec(memory_space=pltpu.HBM)
     out_spec = hbm if far_out else vmem
+    args = [pltpu.with_memory_space_constraint(a, pltpu.HBM) if k in far else a for k, a in enumerate(args)]
     return pl.pallas_call(
         kernel,
         out_shape=outs,
@@ -98,12 +99,26 @@
     return lists_ref[:, pl.ds(at, part)]
 
 
-def start_kernel(sizes, lists_ref, op_hbm, u_hbm, sel_ref, op_ref, u_ref, applied_ref, *refs):
-    edges, sems = refs[:-1], refs[-1]
-    u_copies = chunk_copies(u_hbm, u_ref, sems, 0, CHUNKS)
-    op_copies = chunk_copies(op_hbm, op_ref, sems, CHUNKS, CHUNKS)
-    for copy in u_copies + op_copies:
+def load_kernel(sizes, nb, lists_hbm, op_hbm, u_hbm, *refs):
+    if len(refs) > 5:
+        inverse_hbm, lists_ref, sel_ref, op_ref, u_ref, keep_ref, give_ref, sems = refs
+    else:
+        lists_ref, sel_ref, op_ref, u_ref, sems = refs
+    named = pltpu.make_async_copy(lists_hbm, lists_ref, sems.at[0])
+    copies = []
+    if len(refs) > 5:
+        parity = lax.axis_index("col") % 2
+        lines = keep_ref.shape[0] // nb
+        for line in range(lines):
+            for k, (ref, mine) in enumerate(((keep_ref, parity), (give_ref, 1 - parity))):
+                rows = pl.ds(pl.multiple_of((2 * line + mine) * nb, nb), nb)
+                sem = sems.at[1 + 2 * CHUNKS + 2 * line + k]
+                copies.append(pltpu.make_async_copy(inverse_hbm.at[rows], ref.at[pl.ds(line * nb, nb)], sem))
+    copies += chunk_copies(u_hbm, u_ref, sems, 1, CHUNKS)
+    copies += chunk_copies(op_hbm, op_ref, sems, 1 + CHUNKS, CHUNKS)
+    for copy in [named] + copies:
         copy.start()
+    named.wait()
     n = sel_ref.shape[0]
     part = n // 4
     for m in range(4):
@@ -112,25 +127,24 @@
         for j in range(n // 128):
             hit = names == lanes + j * 128
             sel_ref[m * part : (m + 1) * part, j * 128 : (j + 1) * 128] = jnp.where(hit, 1.0, 0.0).astype(BF)
-    for copy in u_copies:
+    for copy in copies:
         copy.wait()
-    u = u_ref[...].astype(BF)
-    rows = n // CHUNKS
-    for k, copy in enumerate(op_copies):
-        copy.wait()
-        applied_ref[k * rows : (k + 1) * rows, :] = dot(op_ref[k * rows : (k + 1) * rows, :], u)
-    applied = applied_ref[...].astype(BF)
+
+
+def apply_kernel(op_ref, u_ref, sel_ref, applied_ref, *edges):
+    applied = dot(op_ref[...], u_ref[...].astype(BF))
+    applied_ref[...] = applied
+    split_edges(applied, sel_ref, edges)
+
+
+def split_edges(field, sel_ref, edges):
+    field = field.astype(BF)
+    part = edges[0].shape[0]
     for m, edge in enumerate(edges):
-        edge[...] = dot(sel_ref[m * part : (m + 1) * part, :], applied).astype(BF)
-
-
-def tables_kernel(
-    sizes, lists_ref, basis_t_ref, slot_ref, sel_ref, pre_hbm, load_hbm,
-    scatter_ref, based_ref, based_t_ref, pre_sel_ref, load_ref, pre_ref, sems,
-):
-    copies = chunk_copies(pre_hbm, pre_ref, sems, 0, CHUNKS) + chunk_copies(load_hbm, load_ref, sems, CHUNKS, CHUNKS)
-    for copy in copies:
-        copy.start()
+        edge[...] = dot(sel_ref[m * part : (m + 1) * part, :], field).astype(BF)
+
+
+def tables_kernel(sizes, lists_ref, basis_t_ref, slot_ref, scatter_ref, based_ref, based_t_ref):
     n = scatter_ref.shape[0]
     part = n // 4
     for m in range(4):
@@ -142,15 +156,10 @@
     based_t = dot(jnp.where(pick, 1.0, 0.0).astype(BF), basis_t_ref[...])
     based_t_ref[...] = based_t.astype(BF)
     based_ref[...] = based_t.T.astype(BF)
-    for copy in copies:
-        copy.wait()
-    pre_sel_ref[...] = dot(sel_ref[...], pre_ref[...]).astype(BF)
-
-
-def lift_kernel(sel_ref, op_ref, based_ref, lift_ref, lift_sel_ref):
-    lift = dot(op_ref[...], based_ref[...]).astype(BF)
-    lift_ref[...] = lift
-    lift_sel_ref[...] = dot(sel_ref[...], lift).astype(BF)
+
+
+def product_kernel(left_ref, right_ref, out_ref):
+    out_ref[...] = dot(left_ref[...], right_ref[...]).astype(BF)
 
 
 def shared(sizes):
@@ -170,14 +179,35 @@
     ]
 
 
-def resid_kernel(sizes, load_ref, applied_ref, scatter_ref, based_t_ref, n0, n1, n2, n3, resid_ref, coarse_ref, gathered):
-    part = n0.shape[0]
-    for m, (there, near) in enumerate(zip(shared(sizes), (n0, n1, n2, n3))):
-        gathered[m * part : (m + 1) * part, :] = jnp.where(there, near[...], jnp.zeros_like(near))
-    resid = load_ref[...] - applied_ref[...] - dot(scatter_ref[...], gathered[...])
-    resid = resid.astype(BF)
+def scattered(sizes, scatter_ref, near, which):
+    part = near[0].shape[0]
+    there = shared(sizes)
+    total = None
+    for m, got in zip(which, near):
+        got = jnp.where(there[m], got[...], jnp.zeros_like(got))
+        add = dot(scatter_ref[:, m * part : (m + 1) * part], got)
+        total = add if total is None else total + add
+    return total
+
+
+def early_kernel(sizes, load_ref, applied_ref, scatter_ref, n0, n2, out_ref):
+    out_ref[...] = load_ref[...] - applied_ref[...] - scattered(sizes, scatter_ref, (n0, n2), (0, 2))
+
+
+def resid_kernel(sizes, early_ref, scatter_ref, based_t_ref, n1, n3, resid_ref, coarse_ref):
+    resid = (early_ref[...] - scattered(sizes, scatter_ref, (n1, n3), (1, 3))).astype(BF)
     resid_ref[...] = resid
     coarse_ref[...] = dot(based_t_ref[...], resid).astype(BF)
+
+
+def fix_plain_kernel(pre_ref, sel_ref, resid_ref, fix_ref, *edges):
+    fix = dot(pre_ref[...], resid_ref[...]).astype(BF)
+    part = edges[0].shape[0]
+    for m, edge in enumerate(edges):
+        rows = slice(m * part, (m + 1) * part)
+        own = dot(sel_ref[rows, :], fix)
+        fix_ref[rows, :] = own
+        edge[...] = own.astype(BF)
 
 
 def fix_kernel(pre_sel_ref, resid_ref, fix_ref, *edges):
@@ -199,13 +229,11 @@
     return u + OMEGA * dot(scatter_ref[...], blended[...])
 
 
-def middle_kernel(sizes, op_ref, sel_ref, u_ref, fix_ref, scatter_ref, *refs):
-    near, (out_ref, applied_ref, edge_ref, blended) = refs[:4], refs[4:]
+def middle_kernel(sizes, op_ref, u_ref, fix_ref, scatter_ref, *refs):
+    near, (out_ref, applied_ref, blended) = refs[:4], refs[4:]
     u = smoothed(sizes, u_ref[...], fix_ref, scatter_ref, near, blended)
     out_ref[...] = u
-    applied = dot(op_ref[...], u.astype(BF))
-    applied_ref[...] = applied
-    edge_ref[...] = dot(sel_ref[...], applied.astype(BF))
+    applied_ref[...] = dot(op_ref[...], u.astype(BF))
 
 
 def solution_of(mine_ref, others):
@@ -215,15 +243,13 @@
     return solved.astype(BF)
 
 
-def next_kernel(lift_ref, lift_sel_ref, applied_ref, edge_ref, mine_ref, *refs):
+def next_kernel(lift_ref, sel_ref, applied_ref, mine_ref, *refs):
     others, (solved_ref, out_ref, *edges) = refs[:-6], refs[-6:]
     solved = solution_of(mine_ref, others)
     solved_ref[...] = solved
-    part = edges[0].shape[0]
-    for m, edge in enumerate(edges):
-        rows = slice(m * part, (m + 1) * part)
-        edge[...] = (edge_ref[rows, :] + OMEGA * dot(lift_sel_ref[rows, :], solved)).astype(BF)
-    out_ref[...] = applied_ref[...] + OMEGA * dot(lift_ref[...], solved)
+    applied = applied_ref[...] + OMEGA * dot(lift_ref[...], solved)
+    out_ref[...] = applied
+    split_edges(applied, sel_ref, edges)
 
 
 def late_kernel(sizes, u_ref, fix_ref, scatter_ref, based_ref, solved_ref, *refs):
@@ -256,21 +282,6 @@
             rows = pl.ds(pl.multiple_of((2 * line + parity) * nb, nb), nb)
             cols = pl.ds(pl.multiple_of(pair * 2 * nb, 2 * nb), 2 * nb)
             block[line * nb : (line + 1) * nb, :] = inverse_ref[rows, cols]
-
-
-def split_kernel(nb, inverse_hbm, keep_ref, give_ref, sems):
-    parity = lax.axis_index("col") % 2
-    copies = []
-    for line in range(keep_ref.shape[0] // nb):
-        for k, (ref, mine) in enumerate(((keep_ref, parity), (give_ref, 1 - parity))):
-            rows = pl.ds(pl.multiple_of((2 * line + mine) * nb, nb), nb)
-            copies.append(
-                pltpu.make_async_copy(inverse_hbm.at[rows], ref.at[pl.ds(line * nb, nb)], sems.at[2 * line + k])
-            )
-    for copy in copies:
-        copy.start()
-    for copy in copies:
-        copy.wait()
 
 
 def upper_kernel(top, mine_ref, got_ref, keep_ref, give_ref):
@@ -359,16 +370,17 @@
         return [send(e, p) for e, p in zip(edges, halo_pairs)]
 
     stepwise = in_steps(sizes)
+    half = shape((lines * nb, coarse_inverse.shape[1]), BF)
+    lists, sel, op, u, *halves = call(
+        functools.partial(load_kernel, sizes, nb),
+        [shape(lists.shape, lists.dtype), square, square, field] + [half, half] * stepwise,
+        [lists, op, u] + [coarse_inverse] * stepwise,
+        n * n,
+        [pltpu.SemaphoreType.DMA((1 + 2 * CHUNKS + 2 * lines,))],
+        far=(0, 1, 2, 3),
+    )
     if stepwise:
-        half = shape((lines * nb, coarse_inverse.shape[1]), BF)
-        keep, give = call(
-            functools.partial(split_kernel, nb),
-            [half, half],
-            [coarse_inverse],
-            n,
-            [pltpu.SemaphoreType.DMA((2 * lines,))],
-            far=(0,),
-        )
+        keep, give = halves
         got = send(give, swap_pairs(0, 0, 1))
     else:
         blocks = call(
@@ -378,26 +390,13 @@
             n,
         )
         blocks = [send(block, target(k)) for k, block in enumerate(blocks)]
-    sems = pltpu.SemaphoreType.DMA((2 * CHUNKS,))
-    sel, op, u, applied, *edges = call(
-        functools.partial(start_kernel, sizes),
-        [square, square, field, field] + [edge] * 4,
-        [lists, op, u],
-        2 * flops,
-        [sems],
-        far=(1, 2),
-    )
+    applied, *edges = call(apply_kernel, [field] + [edge] * 4, [op, u, sel], 2 * flops)
     near = halo(edges)
     if stepwise:
         keep, give = call(functools.partial(upper_kernel, cols // 2), [half, half], [keep, got], n)
         got = send(give, swap_pairs(0, 0, cols // 2))
-    scatter, based, based_t, pre_sel, load = call(
-        functools.partial(tables_kernel, sizes),
-        [square, thin, shape((nb, n), BF), square, field],
-        [lists, basis_t, slot, sel, pre, load],
-        2 * n * n * n,
-        [pltpu.VMEM((n, n), BF), sems],
-        far=(4, 5),
+    scatter, based, based_t = call(
+        functools.partial(tables_kernel, sizes), [square, thin, shape((nb, n), BF)], [lists, basis_t, slot], n * n
     )
     if stepwise:
         keep, give = call(lower_kernel, [half, half], [keep, got], n)
@@ -405,12 +404,16 @@
 
     scratch = [pltpu.VMEM((n, cases), BF)]
     for sweep in range(ITERS):
+        if sweep == 1:
+            pre_sel = call(product_kernel, square, [sel, pre], 2 * n * n * n)
+        early = call(
+            functools.partial(early_kernel, sizes), field, [load, applied, scatter, near[0], near[2]], flops // 2
+        )
         resid, coarse = call(
             functools.partial(resid_kernel, sizes),
             [shape((n, cases), BF), vector],
-            [load, applied, scatter, based_t, *near],
-            flops,
-            scratch,
+            [early, scatter, based_t, near[1], near[3]],
+            flops // 2,
         )
         vectors = {}
         for dr, dc in far_moves:
@@ -418,7 +421,10 @@
             vectors[0, dr, dc] = got
             for dg in range(1, grps):
                 vectors[dg, dr, dc] = send(got, swap_pairs(dg, 0, 0))
-        fix, *own = call(fix_kernel, [field] + [edge] * 4, [pre_sel, resid], flops)
+        if sweep:
+            fix, *own = call(fix_kernel, [field] + [edge] * 4, [pre_sel, resid], flops)
+        else:
+            fix, *own = call(fix_plain_kernel, [field] + [edge] * 4, [pre, sel, resid], 2 * flops)
         near = halo(own)
         mine, *others = call(
             functools.partial(coarse_kernel, stepwise, geometry, row_size, nb, moves),
@@ -429,16 +435,13 @@
         )
         others = [send(o, swap_pairs(0, 0, 2 * (k + 1))) for k, o in enumerate(others)]
         if sweep < ITERS - 1:
-            lift, lift_sel = call(lift_kernel, [thin, thin], [sel, op, based], n * n * nb)
-            inputs = [u, fix, scatter, *near]
-            u, applied, edge_part = call(
-                functools.partial(middle_kernel, sizes), [field] * 3, [op, sel, *inputs], 3 * flops, scratch
+            if sweep == 0:
+                lift = call(product_kernel, thin, [op, based], n * n * nb)
+            u, applied = call(
+                functools.partial(middle_kernel, sizes), [field] * 2, [op, u, fix, scatter, *near], 2 * flops, scratch
             )
             solved, applied, *edges = call(
-                next_kernel,
-                [vector, field] + [edge] * 4,
-                [lift, lift_sel, applied, edge_part, mine, *others],
-                n * nb * cases,
+                next_kernel, [vector, field] + [edge] * 4, [lift, sel, applied, mine, *others], flops
             )
             near = halo(edges)
         else:

time: 80.3 us -> 78.4 us (0.976)
  local copies, waits for them, and re-layouts: 4.47 us -> 0.02 us
  waiting for transfers between devices: 11.9 us -> 13.9 us
    unnamed x16 -> x8, local copies, waits for them, and re-layouts: 4.47 us -> 0.02 us
    ppermute x39, waiting for transfers between devices: 11.9 us -> 13.9 us  [send(): return lax.ppermute(value, AXES, pairs)]
    pallas_call x16 -> x19, Pallas kernels: 19.1 us -> 19.8 us  [call(): pl.pallas_call(kernel, out_shape=outs, in_specs=[hbm if k in far else vme...]
  transfers between devices with their start and end apart: 39 -> 39, of which waited for: 11 -> 11; matrix products, arithmetic and copies ran while one was open for 0% -> 0% of each run, Pallas kernels for 20% -> 19%
where the time goes in v4:
time: 78.4 us; the launch traced here: 78.2 us
  starting transfers between devices  44 us (56%)
  Pallas kernels  19.8 us (25%)
  waiting for transfers between devices  13.9 us (18%)
    ppermute x39, starting transfers between devices, send(): return lax.ppermute(value, AXES, pairs)  44 us
    pallas_call x19, Pallas kernels, call(): pl.pallas_call(kernel, out_shape=outs, in_specs=[hbm if k in far else vme...  19.8 us
    ppermute x39, waiting for transfers between devices, send(): return lax.ppermute(value, AXES, pairs)  13.9 us
  transfers between devices with their start and end apart: 39, of which 11 were waited for; matrix products, arithmetic and copies ran while one was open for 0% of the time, Pallas kernels for 19%

profile of v4, /device:TPU:0, one launch (start us, length us, event | category | flops | bytes accessed | tf_op | source)
XLA Modules:
  0.0 78.2 jit_solution(15736852902900250579)
XLA Ops:
  0.0 2.1 %shard_map.82 = (s32[1,1024]{1,0:T(1,128)S(1)}, bf16[1024,1024]{1,0:T(8,128)(2,1)S(1)}, bf16[1024,1024]{1,0:T(8,128)(2,1)S(1)}, f32[1024,256]{1,0:T(8,128)S(1)},...) custom-call(s32[1,1024]{1,0:T(1,128)} %bitcast.18, bf16[1024,1024]{1,0:T(8,128)(2,1)} %bitcast.16, ...), custom_call_target="tpu_custom_call" | custom-call | flops 1048576 | bytes 3411968 | tf_op jit(solution)/shard_map/pallas_call | solution.py:29
  2.2 3.0 %collective-permute-start.8 = (bf16[256,256]{1,0:T(8,128)(2,1)S(1)}, bf16[256,256]{1,0:T(8,128)(2,1)S(1)}, u32[]{:S(2)}, u32[]{:S(2)}) collective-permute-start(bf16[256,256]{1,0:T(8,128)(2,1)S(1)} %get-tuple-element.74), channel_id=1, source_target_pairs={{0,1},{1,0},{2,3},{3,2},{4,5},{5,4},{6,7},{7,6},{8,9},{9,8},{10,11... | collective-permute-start | bytes 393224 | tf_op jit(solution)/shard_map/ppermute | solution.py:84
  5.2 2.2 %shard_map.83 = (f32[1024,256]{1,0:T(8,128)S(1)}, bf16[256,256]{1,0:T(8,128)(2,1)S(1)}, bf16[256,256]{1,0:T(8,128)(2,1)S(1)}, bf16[256,256]{1,0:T(8,128)(2,1)S(1)}, bf16[256,256]{1,0:T(8,128)(2,1)S(1)}) custom-call(bf16[1024,1024]{1,0:T(8,128)(2,1)S(1)} %get-tuple-element.53.op_ref.left_ref, f32[1024,256]{1,0:T(8,128)S(1)} %get-tuple-element.54.u_ref, ...), custom_call_target="tpu_custom_call" | custom-call | flops 1073741824 | bytes 5242880 | tf_op jit(solution)/shard_map/pallas_call | solution.py:29
  7.5 2.0 %collective-permute-start.1 = (bf16[256,256]{1,0:T(8,128)(2,1)S(1)}, bf16[256,256]{1,0:T(8,128)(2,1)S(1)}, u32[]{:S(2)}, u32[]{:S(2)}) collective-permute-start(bf16[256,256]{1,0:T(8,128)(2,1)S(1)} %get-tuple-element.60), channel_id=1, source_target_pairs={{0,8},{1,9},{2,10},{3,11},{4,12},{5,13},{6,14},{7,15},{8,0},{9,1},... | collective-permute-start | bytes 393224 | tf_op jit(solution)/shard_map/ppermute | solution.py:84
  9.5 3.0 %collective-permute-start.3 = (bf16[256,256]{1,0:T(8,128)(2,1)S(1)}, bf16[256,256]{1,0:T(8,128)(2,1)S(1)}, u32[]{:S(2)}, u32[]{:S(2)}) collective-permute-start(bf16[256,256]{1,0:T(8,128)(2,1)S(1)} %get-tuple-element.63), channel_id=1, source_target_pairs={{0,2},{1,3},{2,0},{3,1},{4,6},{5,7},{6,4},{7,5},{8,16},{9,17},{10,... | collective-permute-start | bytes 393224 | tf_op jit(solution)/shard_map/ppermute | solution.py:84
  12.5 2.7 %collective-permute-start.9 = (bf16[256,256]{1,0:T(8,128)(2,1)S(1)}, bf16[256,256]{1,0:T(8,128)(2,1)S(1)}, u32[]{:S(2)}, u32[]{:S(2)}) collective-permute-start(bf16[256,256]{1,0:T(8,128)(2,1)S(1)} %get-tuple-element.76), channel_id=1, source_target_pairs={{0,4},{1,5},{2,6},{3,7},{4,0},{5,1},{6,2},{7,3},{8,12},{9,13},{10,... | collective-permute-start | bytes 393224 | tf_op jit(solution)/shard_map/ppermute | solution.py:84
  19.6 1.7 %collective-permute-start.14 = (bf16[64,256]{1,0:T(8,128)(2,1)S(1)}, bf16[64,256]{1,0:T(8,128)(2,1)S(1)}, u32[]{:S(2)}, u32[]{:S(2)}) collective-permute-start(bf16[64,256]{1,0:T(8,128)(2,1)S(1)} %get-tuple-element.79.refs_2_), channel_id=1, source_target_pairs={{0,8},{1,9},{2,10},{3,11},{4,12},{5,13},{6,14},{7,15},{8,0},{9,1},... | collective-permute-start | bytes 98312 | tf_op jit(solution)/shard_map/ppermute | solution.py:84
  23.5 2.6 %collective-permute-done.16.refs_8_ = bf16[64,256]{1,0:T(8,128)(2,1)S(1)} collective-permute-done((bf16[64,256]{1,0:T(8,128)(2,1)S(1)}, bf16[64,256]{1,0:T(8,128)(2,1)S(1)}, u32[]{:S(2)}, u32[]{:S(2)}) %collective-permute-start.16) | collective-permute-done | bytes 32800 | tf_op jit(solution)/shard_map/ppermute | solution.py:84
  26.9 2.2 %shard_map.87 = (f32[1024,256]{1,0:T(8,128)S(1)}, bf16[256,256]{1,0:T(8,128)(2,1)S(1)}, bf16[256,256]{1,0:T(8,128)(2,1)S(1)}, bf16[256,256]{1,0:T(8,128)(2,1)S(1)}, bf16[256,256]{1,0:T(8,128)(2,1)S(1)}) custom-call(bf16[1024,1024]{1,0:T(8,128)(2,1)S(1)} %bitcast.12, bf16[1024,1024]{1,0:T(8,128)(2,1)S(1)} %get-tuple-element.55.sel_ref.left_ref, ...), custom_call_target="tpu_custom_call" | custom-call | flops 1073741824 | bytes 4718592 | tf_op jit(solution)/shard_map/pallas_call | solution.py:29
  29.8 1.8 %collective-permute-start.6 = (bf16[256,256]{1,0:T(8,128)(2,1)S(1)}, bf16[256,256]{1,0:T(8,128)(2,1)S(1)}, u32[]{:S(2)}, u32[]{:S(2)}) collective-permute-start(bf16[256,256]{1,0:T(8,128)(2,1)S(1)} %get-tuple-element.68), channel_id=1, source_target_pairs={{0,8},{1,9},{2,10},{3,11},{4,12},{5,13},{6,14},{7,15},{8,0},{9,1},... | collective-permute-start | bytes 393224 | tf_op jit(solution)/shard_map/ppermute | solution.py:84
  31.6 3.2 %collective-permute-start.7 = (bf16[256,256]{1,0:T(8,128)(2,1)S(1)}, bf16[256,256]{1,0:T(8,128)(2,1)S(1)}, u32[]{:S(2)}, u32[]{:S(2)}) collective-permute-start(bf16[256,256]{1,0:T(8,128)(2,1)S(1)} %get-tuple-element.69), channel_id=1, source_target_pairs={{0,2},{1,3},{2,0},{3,1},{4,6},{5,7},{6,4},{7,5},{8,16},{9,17},{10,... | collective-permute-start | bytes 393224 | tf_op jit(solution)/shard_map/ppermute | solution.py:84
  35.9 3.6 %collective-permute-start.19 = (bf16[64,256]{1,0:T(8,128)(2,1)S(1)}, bf16[64,256]{1,0:T(8,128)(2,1)S(1)}, u32[]{:S(2)}, u32[]{:S(2)}) collective-permute-start(bf16[64,256]{1,0:T(8,128)(2,1)S(1)} %get-tuple-element.82), channel_id=1, source_target_pairs={{0,4},{1,5},{2,6},{3,7},{4,0},{5,1},{6,2},{7,3},{8,12},{9,13},{10,... | collective-permute-start | bytes 98312 | tf_op jit(solution)/shard_map/ppermute | solution.py:84
  39.5 1.8 %collective-permute-start.20 = (bf16[64,256]{1,0:T(8,128)(2,1)S(1)}, bf16[64,256]{1,0:T(8,128)(2,1)S(1)}, u32[]{:S(2)}, u32[]{:S(2)}) collective-permute-start(bf16[64,256]{1,0:T(8,128)(2,1)S(1)} %get-tuple-element.83), channel_id=1, source_target_pairs={{0,6},{1,7},{2,4},{3,5},{4,2},{5,3},{6,0},{7,1},{8,14},{9,15},{10,... | collective-permute-start | bytes 98312 | tf_op jit(solution)/shard_map/ppermute | solution.py:84
  41.4 2.2 %shard_map.88 = (f32[1024,256]{1,0:T(8,128)S(1)}, f32[1024,256]{1,0:T(8,128)S(1)}) custom-call(bf16[1024,1024]{1,0:T(8,128)(2,1)S(1)} %get-tuple-element.53.op_ref.left_ref, f32[1024,256]{1,0:T(8,128)S(1)} %get-tuple-element.54.u_ref, f32[1024,256]{1,0:T(8,128)S(1)} %get-tuple-element.65.fix_ref, bf16[1024,1024]{1,0:T(8,128)(2,1)S(1)} %get-tuple-element.58.scatter_ref, ...), custom_call_target="tpu_custom_call" | custom-call | flops 1073741824 | bytes 6815744 | tf_op jit(solution)/shard_map/pallas_call | solution.py:29
  43.6 1.6 %collective-permute-done.20.refs_2_ = bf16[64,256]{1,0:T(8,128)(2,1)S(1)} collective-permute-done((bf16[64,256]{1,0:T(8,128)(2,1)S(1)}, bf16[64,256]{1,0:T(8,128)(2,1)S(1)}, u32[]{:S(2)}, u32[]{:S(2)}) %collective-permute-start.20) | collective-permute-done | bytes 32800 | tf_op jit(solution)/shard_map/ppermute | solution.py:84
  47.0 1.3 %collective-permute-start.22 = (bf16[256,256]{1,0:T(8,128)(2,1)S(1)}, bf16[256,256]{1,0:T(8,128)(2,1)S(1)}, u32[]{:S(2)}, u32[]{:S(2)}) collective-permute-start(bf16[256,256]{1,0:T(8,128)(2,1)S(1)} %get-tuple-element.86), channel_id=1, source_target_pairs={{0,8},{1,9},{2,10},{3,11},{4,12},{5,13},{6,14},{7,15},{8,0},{9,1},... | collective-permute-start | bytes 393224 | tf_op jit(solution)/shard_map/ppermute | solution.py:84
  48.3 3.4 %collective-permute-start.24 = (bf16[256,256]{1,0:T(8,128)(2,1)S(1)}, bf16[256,256]{1,0:T(8,128)(2,1)S(1)}, u32[]{:S(2)}, u32[]{:S(2)}) collective-permute-start(bf16[256,256]{1,0:T(8,128)(2,1)S(1)} %get-tuple-element.88), channel_id=1, source_target_pairs={{0,2},{1,3},{2,0},{3,1},{4,6},{5,7},{6,4},{7,5},{8,16},{9,17},{10,... | collective-permute-start | bytes 393224 | tf_op jit(solution)/shard_map/ppermute | solution.py:84
  51.7 2.3 %shard_map.89.pre_sel_ref = bf16[1024,1024]{1,0:T(8,128)(2,1)S(1)} custom-call(bf16[1024,1024]{1,0:T(8,128)(2,1)S(1)} %get-tuple-element.55.sel_ref.left_ref, bf16[1024,1024]{1,0:T(8,128)(2,1)S(1)} %bitcast.13), custom_call_target="tpu_custom_call" | custom-call | flops 2147483648 | bytes 4194304 | tf_op jit(solution)/shard_map/pallas_call | solution.py:29
  54.6 1.5 %collective-permute-done.24.n3 = bf16[256,256]{1,0:T(8,128)(2,1)S(1)} collective-permute-done((bf16[256,256]{1,0:T(8,128)(2,1)S(1)}, bf16[256,256]{1,0:T(8,128)(2,1)S(1)}, u32[]{:S(2)}, u32[]{:S(2)}) %collective-permute-start.24) | collective-permute-done | bytes 131104 | tf_op jit(solution)/shard_map/ppermute | solution.py:84
  57.5 3.0 %collective-permute-start.34 = (bf16[64,256]{1,0:T(8,128)(2,1)S(1)}, bf16[64,256]{1,0:T(8,128)(2,1)S(1)}, u32[]{:S(2)}, u32[]{:S(2)}) collective-permute-start(bf16[64,256]{1,0:T(8,128)(2,1)S(1)} %get-tuple-element.96.refs_2_), channel_id=1, source_target_pairs={{0,9},{1,8},{2,11},{3,10},{4,13},{5,12},{6,15},{7,14},{8,1},{9,0},... | collective-permute-start | bytes 98312 | tf_op jit(solution)/shard_map/ppermute | solution.py:84
  62.0 2.9 %collective-permute-start.28 = (bf16[256,256]{1,0:T(8,128)(2,1)S(1)}, bf16[256,256]{1,0:T(8,128)(2,1)S(1)}, u32[]{:S(2)}, u32[]{:S(2)}) collective-permute-start(bf16[256,256]{1,0:T(8,128)(2,1)S(1)} %get-tuple-element.95), channel_id=1, source_target_pairs={{0,2},{1,3},{2,0},{3,1},{4,6},{5,7},{6,4},{7,5},{8,16},{9,17},{10,... | collective-permute-start | bytes 393224 | tf_op jit(solution)/shard_map/ppermute | solution.py:84
  68.9 1.8 %collective-permute-start.36 = (bf16[64,256]{1,0:T(8,128)(2,1)S(1)}, bf16[64,256]{1,0:T(8,128)(2,1)S(1)}, u32[]{:S(2)}, u32[]{:S(2)}) collective-permute-start(bf16[64,256]{1,0:T(8,128)(2,1)S(1)} %get-tuple-element.98), channel_id=1, source_target_pairs={{0,2},{1,3},{2,0},{3,1},{4,6},{5,7},{6,4},{7,5},{8,10},{9,11},{10,... | collective-permute-start | bytes 98312 | tf_op jit(solution)/shard_map/ppermute | solution.py:84
  71.0 2.3 %collective-permute-start.38 = (bf16[64,256]{1,0:T(8,128)(2,1)S(1)}, bf16[64,256]{1,0:T(8,128)(2,1)S(1)}, u32[]{:S(2)}, u32[]{:S(2)}) collective-permute-start(bf16[64,256]{1,0:T(8,128)(2,1)S(1)} %get-tuple-element.100), channel_id=1, source_target_pairs={{0,6},{1,7},{2,4},{3,5},{4,2},{5,3},{6,0},{7,1},{8,14},{9,15},{10,... | collective-permute-start | bytes 98312 | tf_op jit(solution)/shard_map/ppermute | solution.py:84
  74.2 1.9 %collective-permute-done.37.refs_1_ = bf16[64,256]{1,0:T(8,128)(2,1)S(1)} collective-permute-done((bf16[64,256]{1,0:T(8,128)(2,1)S(1)}, bf16[64,256]{1,0:T(8,128)(2,1)S(1)}, u32[]{:S(2)}, u32[]{:S(2)}) %collective-permute-start.37) | collective-permute-done | bytes 32800 | tf_op jit(solution)/shard_map/ppermute | solution.py:84
  (81 shorter events, 21.5 us)
Async XLA Ops:
  2.2 10.3 %collective-permute-start.8 = (bf16[256,256]{1,0:T(8,128)(2,1)S(1)}, bf16[256,256]{1,0:T(8,128)(2,1)S(1)}, u32[]{:S(2)}, u32[]{:S(2)}) collective-permute-start(bf16[256,256]{1,0:T(8,128)(2,1)S(1)} %get-tuple-element.74), channel_id=1, source_target_pairs={{0,1},{1,0},{2,3},{3,2},{4,5},{5,4},{6,7},{7,6},{8,9},{9,8},{10,11... | collective-permute-start | bytes 393224 | tf_op jit(solution)/shard_map/ppermute | solution.py:84
  7.4 9.0 %collective-permute-start = (bf16[256,256]{1,0:T(8,128)(2,1)S(1)}, bf16[256,256]{1,0:T(8,128)(2,1)S(1)}, u32[]{:S(2)}, u32[]{:S(2)}) collective-permute-start(bf16[256,256]{1,0:T(8,128)(2,1)S(1)} %get-tuple-element.59), channel_id=1, source_target_pairs={{0,1},{1,0},{2,3},{3,2},{4,5},{5,4},{6,7},{7,6},{8,9},{9,8},{10,11... | collective-permute-start | bytes 393224 | tf_op jit(solution)/shard_map/ppermute | solution.py:84
  7.5 8.9 %collective-permute-start.1 = (bf16[256,256]{1,0:T(8,128)(2,1)S(1)}, bf16[256,256]{1,0:T(8,128)(2,1)S(1)}, u32[]{:S(2)}, u32[]{:S(2)}) collective-permute-start(bf16[256,256]{1,0:T(8,128)(2,1)S(1)} %get-tuple-element.60), channel_id=1, source_target_pairs={{0,8},{1,9},{2,10},{3,11},{4,12},{5,13},{6,14},{7,15},{8,0},{9,1},... | collective-permute-start | bytes 393224 | tf_op jit(solution)/shard_map/ppermute | solution.py:84
  9.5 7.4 %collective-permute-start.2 = (bf16[256,256]{1,0:T(8,128)(2,1)S(1)}, bf16[256,256]{1,0:T(8,128)(2,1)S(1)}, u32[]{:S(2)}, u32[]{:S(2)}) collective-permute-start(bf16[256,256]{1,0:T(8,128)(2,1)S(1)} %get-tuple-element.62), channel_id=1, source_target_pairs={{0,16},{1,2},{2,1},{3,4},{4,3},{5,6},{6,5},{7,23},{8,24},{9,10},{1... | collective-permute-start | bytes 393224 | tf_op jit(solution)/shard_map/ppermute | solution.py:84
  9.5 8.2 %collective-permute-start.3 = (bf16[256,256]{1,0:T(8,128)(2,1)S(1)}, bf16[256,256]{1,0:T(8,128)(2,1)S(1)}, u32[]{:S(2)}, u32[]{:S(2)}) collective-permute-start(bf16[256,256]{1,0:T(8,128)(2,1)S(1)} %get-tuple-element.63), channel_id=1, source_target_pairs={{0,2},{1,3},{2,0},{3,1},{4,6},{5,7},{6,4},{7,5},{8,16},{9,17},{10,... | collective-permute-start | bytes 393224 | tf_op jit(solution)/shard_map/ppermute | solution.py:84
  12.5 13.6 %collective-permute-start.9 = (bf16[256,256]{1,0:T(8,128)(2,1)S(1)}, bf16[256,256]{1,0:T(8,128)(2,1)S(1)}, u32[]{:S(2)}, u32[]{:S(2)}) collective-permute-start(bf16[256,256]{1,0:T(8,128)(2,1)S(1)} %get-tuple-element.76), channel_id=1, source_target_pairs={{0,4},{1,5},{2,6},{3,7},{4,0},{5,1},{6,2},{7,3},{8,12},{9,13},{10,... | collective-permute-start | bytes 393224 | tf_op jit(solution)/shard_map/ppermute | solution.py:84
  22.0 7.2 %collective-permute-start.11 = (bf16[64,256]{1,0:T(8,128)(2,1)S(1)}, bf16[64,256]{1,0:T(8,128)(2,1)S(1)}, u32[]{:S(2)}, u32[]{:S(2)}) collective-permute-start(bf16[64,256]{1,0:T(8,128)(2,1)S(1)} %get-tuple-element.79.refs_2_), channel_id=1, source_target_pairs={{0,16},{1,17},{2,18},{3,19},{4,20},{5,21},{6,22},{7,23},{8,24},{9,... | collective-permute-start | bytes 98312 | tf_op jit(solution)/shard_map/ppermute | solution.py:84
  22.4 7.4 %collective-permute-start.13 = (bf16[64,256]{1,0:T(8,128)(2,1)S(1)}, bf16[64,256]{1,0:T(8,128)(2,1)S(1)}, u32[]{:S(2)}, u32[]{:S(2)}) collective-permute-start(bf16[64,256]{1,0:T(8,128)(2,1)S(1)} %collective-permute-done.12.refs_4_), channel_id=1, source_target_pairs={{0,16},{1,17},{2,18},{3,19},{4,20},{5,21},{6,22},{7,23},{8,24},{9,... | collective-permute-start | bytes 98312 | tf_op jit(solution)/shard_map/ppermute | solution.py:84
  23.5 6.3 %collective-permute-start.15 = (bf16[64,256]{1,0:T(8,128)(2,1)S(1)}, bf16[64,256]{1,0:T(8,128)(2,1)S(1)}, u32[]{:S(2)}, u32[]{:S(2)}) collective-permute-start(bf16[64,256]{1,0:T(8,128)(2,1)S(1)} %collective-permute-done.14.refs_6_), channel_id=1, source_target_pairs={{0,16},{1,17},{2,18},{3,19},{4,20},{5,21},{6,22},{7,23},{8,24},{9,... | collective-permute-start | bytes 98312 | tf_op jit(solution)/shard_map/ppermute | solution.py:84
  26.2 9.3 %collective-permute-start.10 = (bf16[256,256]{1,0:T(8,128)(2,1)S(1)}, bf16[256,256]{1,0:T(8,128)(2,1)S(1)}, u32[]{:S(2)}, u32[]{:S(2)}) collective-permute-start(bf16[256,256]{1,0:T(8,128)(2,1)S(1)} %get-tuple-element.78), channel_id=1, source_target_pairs={{0,2},{1,3},{2,0},{3,1},{4,6},{5,7},{6,4},{7,5},{8,10},{9,11},{10,... | collective-permute-start | bytes 393224 | tf_op jit(solution)/shard_map/ppermute | solution.py:84
  29.2 6.7 %collective-permute-start.4 = (bf16[256,256]{1,0:T(8,128)(2,1)S(1)}, bf16[256,256]{1,0:T(8,128)(2,1)S(1)}, u32[]{:S(2)}, u32[]{:S(2)}) collective-permute-start(bf16[256,256]{1,0:T(8,128)(2,1)S(1)} %get-tuple-element.66), channel_id=1, source_target_pairs={{0,1},{1,0},{2,3},{3,2},{4,5},{5,4},{6,7},{7,6},{8,9},{9,8},{10,11... | collective-permute-start | bytes 393224 | tf_op jit(solution)/shard_map/ppermute | solution.py:84
  29.8 9.7 %collective-permute-start.5 = (bf16[256,256]{1,0:T(8,128)(2,1)S(1)}, bf16[256,256]{1,0:T(8,128)(2,1)S(1)}, u32[]{:S(2)}, u32[]{:S(2)}) collective-permute-start(bf16[256,256]{1,0:T(8,128)(2,1)S(1)} %get-tuple-element.67), channel_id=1, source_target_pairs={{0,16},{1,2},{2,1},{3,4},{4,3},{5,6},{6,5},{7,23},{8,24},{9,10},{1... | collective-permute-start | bytes 393224 | tf_op jit(solution)/shard_map/ppermute | solution.py:84
  29.8 11.6 %collective-permute-start.6 = (bf16[256,256]{1,0:T(8,128)(2,1)S(1)}, bf16[256,256]{1,0:T(8,128)(2,1)S(1)}, u32[]{:S(2)}, u32[]{:S(2)}) collective-permute-start(bf16[256,256]{1,0:T(8,128)(2,1)S(1)} %get-tuple-element.68), channel_id=1, source_target_pairs={{0,8},{1,9},{2,10},{3,11},{4,12},{5,13},{6,14},{7,15},{8,0},{9,1},... | collective-permute-start | bytes 393224 | tf_op jit(solution)/shard_map/ppermute | solution.py:84
  31.6 9.8 %collective-permute-start.7 = (bf16[256,256]{1,0:T(8,128)(2,1)S(1)}, bf16[256,256]{1,0:T(8,128)(2,1)S(1)}, u32[]{:S(2)}, u32[]{:S(2)}) collective-permute-start(bf16[256,256]{1,0:T(8,128)(2,1)S(1)} %get-tuple-element.69), channel_id=1, source_target_pairs={{0,2},{1,3},{2,0},{3,1},{4,6},{5,7},{6,4},{7,5},{8,16},{9,17},{10,... | collective-permute-start | bytes 393224 | tf_op jit(solution)/shard_map/ppermute | solution.py:84
  35.8 7.8 %collective-permute-start.18 = (bf16[64,256]{1,0:T(8,128)(2,1)S(1)}, bf16[64,256]{1,0:T(8,128)(2,1)S(1)}, u32[]{:S(2)}, u32[]{:S(2)}) collective-permute-start(bf16[64,256]{1,0:T(8,128)(2,1)S(1)} %get-tuple-element.81), channel_id=1, source_target_pairs={{0,2},{1,3},{2,0},{3,1},{4,6},{5,7},{6,4},{7,5},{8,10},{9,11},{10,... | collective-permute-start | bytes 98312 | tf_op jit(solution)/shard_map/ppermute | solution.py:84
  35.9 7.7 %collective-permute-start.19 = (bf16[64,256]{1,0:T(8,128)(2,1)S(1)}, bf16[64,256]{1,0:T(8,128)(2,1)S(1)}, u32[]{:S(2)}, u32[]{:S(2)}) collective-permute-start(bf16[64,256]{1,0:T(8,128)(2,1)S(1)} %get-tuple-element.82), channel_id=1, source_target_pairs={{0,4},{1,5},{2,6},{3,7},{4,0},{5,1},{6,2},{7,3},{8,12},{9,13},{10,... | collective-permute-start | bytes 98312 | tf_op jit(solution)/shard_map/ppermute | solution.py:84
  46.2 7.9 %collective-permute-start.21 = (bf16[256,256]{1,0:T(8,128)(2,1)S(1)}, bf16[256,256]{1,0:T(8,128)(2,1)S(1)}, u32[]{:S(2)}, u32[]{:S(2)}) collective-permute-start(bf16[256,256]{1,0:T(8,128)(2,1)S(1)} %get-tuple-element.85), channel_id=1, source_target_pairs={{0,1},{1,0},{2,3},{3,2},{4,5},{5,4},{6,7},{7,6},{8,9},{9,8},{10,11... | collective-permute-start | bytes 393224 | tf_op jit(solution)/shard_map/ppermute | solution.py:84
  47.0 7.0 %collective-permute-start.22 = (bf16[256,256]{1,0:T(8,128)(2,1)S(1)}, bf16[256,256]{1,0:T(8,128)(2,1)S(1)}, u32[]{:S(2)}, u32[]{:S(2)}) collective-permute-start(bf16[256,256]{1,0:T(8,128)(2,1)S(1)} %get-tuple-element.86), channel_id=1, source_target_pairs={{0,8},{1,9},{2,10},{3,11},{4,12},{5,13},{6,14},{7,15},{8,0},{9,1},... | collective-permute-start | bytes 393224 | tf_op jit(solution)/shard_map/ppermute | solution.py:84
  48.3 7.8 %collective-permute-start.24 = (bf16[256,256]{1,0:T(8,128)(2,1)S(1)}, bf16[256,256]{1,0:T(8,128)(2,1)S(1)}, u32[]{:S(2)}, u32[]{:S(2)}) collective-permute-start(bf16[256,256]{1,0:T(8,128)(2,1)S(1)} %get-tuple-element.88), channel_id=1, source_target_pairs={{0,2},{1,3},{2,0},{3,1},{4,6},{5,7},{6,4},{7,5},{8,16},{9,17},{10,... | collective-permute-start | bytes 393224 | tf_op jit(solution)/shard_map/ppermute | solution.py:84
  57.5 7.4 %collective-permute-start.34 = (bf16[64,256]{1,0:T(8,128)(2,1)S(1)}, bf16[64,256]{1,0:T(8,128)(2,1)S(1)}, u32[]{:S(2)}, u32[]{:S(2)}) collective-permute-start(bf16[64,256]{1,0:T(8,128)(2,1)S(1)} %get-tuple-element.96.refs_2_), channel_id=1, source_target_pairs={{0,9},{1,8},{2,11},{3,10},{4,13},{5,12},{6,15},{7,14},{8,1},{9,0},... | collective-permute-start | bytes 98312 | tf_op jit(solution)/shard_map/ppermute | solution.py:84
  61.3 9.4 %collective-permute-start.25 = (bf16[256,256]{1,0:T(8,128)(2,1)S(1)}, bf16[256,256]{1,0:T(8,128)(2,1)S(1)}, u32[]{:S(2)}, u32[]{:S(2)}) collective-permute-start(bf16[256,256]{1,0:T(8,128)(2,1)S(1)} %get-tuple-element.92), channel_id=1, source_target_pairs={{0,1},{1,0},{2,3},{3,2},{4,5},{5,4},{6,7},{7,6},{8,9},{9,8},{10,11... | collective-permute-start | bytes 393224 | tf_op jit(solution)/shard_map/ppermute | solution.py:84
  61.4 9.6 %collective-permute-start.26 = (bf16[256,256]{1,0:T(8,128)(2,1)S(1)}, bf16[256,256]{1,0:T(8,128)(2,1)S(1)}, u32[]{:S(2)}, u32[]{:S(2)}) collective-permute-start(bf16[256,256]{1,0:T(8,128)(2,1)S(1)} %get-tuple-element.93), channel_id=1, source_target_pairs={{0,16},{1,2},{2,1},{3,4},{4,3},{5,6},{6,5},{7,23},{8,24},{9,10},{1... | collective-permute-start | bytes 393224 | tf_op jit(solution)/shard_map/ppermute | solution.py:84
  61.5 11.9 %collective-permute-start.27 = (bf16[256,256]{1,0:T(8,128)(2,1)S(1)}, bf16[256,256]{1,0:T(8,128)(2,1)S(1)}, u32[]{:S(2)}, u32[]{:S(2)}) collective-permute-start(bf16[256,256]{1,0:T(8,128)(2,1)S(1)} %get-tuple-element.94), channel_id=1, source_target_pairs={{0,8},{1,9},{2,10},{3,11},{4,12},{5,13},{6,14},{7,15},{8,0},{9,1},... | collective-permute-start | bytes 393224 | tf_op jit(solution)/shard_map/ppermute | solution.py:84
  62.0 11.4 %collective-permute-start.28 = (bf16[256,256]{1,0:T(8,128)(2,1)S(1)}, bf16[256,256]{1,0:T(8,128)(2,1)S(1)}, u32[]{:S(2)}, u32[]{:S(2)}) collective-permute-start(bf16[256,256]{1,0:T(8,128)(2,1)S(1)} %get-tuple-element.95), channel_id=1, source_target_pairs={{0,2},{1,3},{2,0},{3,1},{4,6},{5,7},{6,4},{7,5},{8,16},{9,17},{10,... | collective-permute-start | bytes 393224 | tf_op jit(solution)/shard_map/ppermute | solution.py:84
  (19 other events, 105.7 us)

commit v5 on v4

--- a/solution.py
+++ b/solution.py
@@ -73,8 +73,9 @@
             return (g, r, to) if along_cols else (to // rows, to % rows, c)
         if along_cols and grps == 2:
             return (1 - g, r, c)
-        if not along_cols and cols % 4 == 0:
-            return (g, r, c ^ 2)
+        if not along_cols:
+            to = count - 1 - at
+            return (to // rows, to % rows, c)
         return (g, r, c)
 
     return pairs_of(sizes, where)
@@ -219,19 +220,25 @@
         edge[...] = fix.astype(BF)
 
 
-def smoothed(sizes, u, fix_ref, scatter_ref, near, blended):
+def smoothed(sizes, u, fix_ref, scatter_ref, near, which):
     part = near[0].shape[0]
-    for m, there in enumerate(shared(sizes)):
+    there = shared(sizes)
+    total = None
+    for m, got in zip(which, near):
         rows = slice(m * part, (m + 1) * part)
         fix = fix_ref[rows, :]
-        both = 0.5 * (fix + near[m][...].astype(F32))
-        blended[rows, :] = jnp.where(there, both, fix).astype(BF)
-    return u + OMEGA * dot(scatter_ref[...], blended[...])
-
-
-def middle_kernel(sizes, op_ref, u_ref, fix_ref, scatter_ref, *refs):
-    near, (out_ref, applied_ref, blended) = refs[:4], refs[4:]
-    u = smoothed(sizes, u_ref[...], fix_ref, scatter_ref, near, blended)
+        both = jnp.where(there[m], 0.5 * (fix + got[...].astype(F32)), fix).astype(BF)
+        add = dot(scatter_ref[:, rows], both)
+        total = add if total is None else total + add
+    return u + OMEGA * total
+
+
+def first_kernel(sizes, u_ref, fix_ref, scatter_ref, n0, n2, out_ref):
+    out_ref[...] = smoothed(sizes, u_ref[...], fix_ref, scatter_ref, (n0, n2), (0, 2))
+
+
+def middle_kernel(sizes, op_ref, u_ref, fix_ref, scatter_ref, n1, n3, out_ref, applied_ref):
+    u = smoothed(sizes, u_ref[...], fix_ref, scatter_ref, (n1, n3), (1, 3))
     out_ref[...] = u
     applied_ref[...] = dot(op_ref[...], u.astype(BF))
 
@@ -252,10 +259,9 @@
     split_edges(applied, sel_ref, edges)
 
 
-def late_kernel(sizes, u_ref, fix_ref, scatter_ref, based_ref, solved_ref, *refs):
-    near, (out_ref, blended) = refs[:4], refs[4:]
+def late_kernel(sizes, u_ref, fix_ref, scatter_ref, based_ref, solved_ref, n1, n3, out_ref):
     u = u_ref[...] + OMEGA * dot(based_ref[...], solved_ref[...])
-    out_ref[...] = smoothed(sizes, u, fix_ref, scatter_ref, near, blended)
+    out_ref[...] = smoothed(sizes, u, fix_ref, scatter_ref, (n1, n3), (1, 3))
 
 
 def last_kernel(u_ref, based_ref, mine_ref, *refs):
@@ -401,8 +407,6 @@
     if stepwise:
         keep, give = call(lower_kernel, [half, half], [keep, got], n)
         blocks = [keep, send(give, swap_pairs(0, 0, 2))]
-
-    scratch = [pltpu.VMEM((n, cases), BF)]
     for sweep in range(ITERS):
         if sweep == 1:
             pre_sel = call(product_kernel, square, [sel, pre], 2 * n * n * n)
@@ -434,11 +438,12 @@
             [pltpu.VMEM((2 * grid_rows * nb, cases), BF), pltpu.VMEM((lines * nb, cases), F32)],
         )
         others = [send(o, swap_pairs(0, 0, 2 * (k + 1))) for k, o in enumerate(others)]
+        u = call(functools.partial(first_kernel, sizes), field, [u, fix, scatter, near[0], near[2]], flops // 2)
         if sweep < ITERS - 1:
             if sweep == 0:
                 lift = call(product_kernel, thin, [op, based], n * n * nb)
             u, applied = call(
-                functools.partial(middle_kernel, sizes), [field] * 2, [op, u, fix, scatter, *near], 2 * flops, scratch
+                functools.partial(middle_kernel, sizes), [field] * 2, [op, u, fix, scatter, near[1], near[3]], 2 * flops
             )
             solved, applied, *edges = call(
                 next_kernel, [vector, field] + [edge] * 4, [lift, sel, applied, mine, *others], flops
@@ -446,7 +451,10 @@
             near = halo(edges)
         else:
             u = call(
-                functools.partial(late_kernel, sizes), field, [u, fix, scatter, based, solved, *near], flops, scratch
+                functools.partial(late_kernel, sizes),
+                field,
+                [u, fix, scatter, based, solved, near[1], near[3]],
+                flops // 2,
             )
             u = call(
                 last_kernel,

time: 78.4 us -> 74.6 us (0.952)
  starting transfers between devices: 44 us -> 40.2 us
    ppermute x39, starting transfers between devices: 44 us -> 40.2 us  [send(): return lax.ppermute(value, AXES, pairs)]
    pallas_call x19 -> x21, Pallas kernels: 19.8 us -> 19.8 us  [call(): pl.pallas_call(kernel, out_shape=outs, in_specs=[hbm if k in far else vme...]
  transfers between devices with their start and end apart: 39 -> 39, of which waited for: 11 -> 11; matrix products, arithmetic and copies ran while one was open for 0% -> 0% of each run, Pallas kernels for 19% -> 20%
where the time goes in v5:
time: 74.6 us; the launch traced here: 74.5 us
  starting transfers between devices  40.2 us (54%)
  Pallas kernels  19.8 us (27%)
  waiting for transfers between devices  14 us (19%)
    ppermute x39, starting transfers between devices, send(): return lax.ppermute(value, AXES, pairs)  40.2 us
    pallas_call x21, Pallas kernels, call(): pl.pallas_call(kernel, out_shape=outs, in_specs=[hbm if k in far else vme...  19.8 us
    ppermute x39, waiting for transfers between devices, send(): return lax.ppermute(value, AXES, pairs)  14 us
  transfers between devices with their start and end apart: 39, of which 11 were waited for; matrix products, arithmetic and copies ran while one was open for 0% of the time, Pallas kernels for 20%

profile of v5, /device:TPU:0, one launch (start us, length us, event | category | flops | bytes accessed | tf_op | source)
XLA Modules:
  0.0 74.5 jit_solution(12970491519956225858)
XLA Ops:
  0.0 2.1 %shard_map.82 = (s32[1,1024]{1,0:T(1,128)S(1)}, bf16[1024,1024]{1,0:T(8,128)(2,1)S(1)}, bf16[1024,1024]{1,0:T(8,128)(2,1)S(1)}, f32[1024,256]{1,0:T(8,128)S(1)},...) custom-call(s32[1,1024]{1,0:T(1,128)} %bitcast.18, bf16[1024,1024]{1,0:T(8,128)(2,1)} %bitcast.16, ...), custom_call_target="tpu_custom_call" | custom-call | flops 1048576 | bytes 3411968 | tf_op jit(solution)/shard_map/pallas_call | solution.py:29
  2.2 3.0 %collective-permute-start.8 = (bf16[256,256]{1,0:T(8,128)(2,1)S(1)}, bf16[256,256]{1,0:T(8,128)(2,1)S(1)}, u32[]{:S(2)}, u32[]{:S(2)}) collective-permute-start(bf16[256,256]{1,0:T(8,128)(2,1)S(1)} %get-tuple-element.74), channel_id=1, source_target_pairs={{0,1},{1,0},{2,3},{3,2},{4,5},{5,4},{6,7},{7,6},{8,9},{9,8},{10,11... | collective-permute-start | bytes 393224 | tf_op jit(solution)/shard_map/ppermute | solution.py:85
  5.2 2.2 %shard_map.83 = (f32[1024,256]{1,0:T(8,128)S(1)}, bf16[256,256]{1,0:T(8,128)(2,1)S(1)}, bf16[256,256]{1,0:T(8,128)(2,1)S(1)}, bf16[256,256]{1,0:T(8,128)(2,1)S(1)}, bf16[256,256]{1,0:T(8,128)(2,1)S(1)}) custom-call(bf16[1024,1024]{1,0:T(8,128)(2,1)S(1)} %get-tuple-element.53.op_ref.left_ref, f32[1024,256]{1,0:T(8,128)S(1)} %get-tuple-element.54.u_ref, ...), custom_call_target="tpu_custom_call" | custom-call | flops 1073741824 | bytes 5242880 | tf_op jit(solution)/shard_map/pallas_call | solution.py:29
  7.5 2.0 %collective-permute-start.1 = (bf16[256,256]{1,0:T(8,128)(2,1)S(1)}, bf16[256,256]{1,0:T(8,128)(2,1)S(1)}, u32[]{:S(2)}, u32[]{:S(2)}) collective-permute-start(bf16[256,256]{1,0:T(8,128)(2,1)S(1)} %get-tuple-element.60), channel_id=1, source_target_pairs={{0,8},{1,9},{2,10},{3,11},{4,12},{5,13},{6,14},{7,15},{8,0},{9,1},... | collective-permute-start | bytes 393224 | tf_op jit(solution)/shard_map/ppermute | solution.py:85
  11.0 3.9 %collective-permute-start.9 = (bf16[256,256]{1,0:T(8,128)(2,1)S(1)}, bf16[256,256]{1,0:T(8,128)(2,1)S(1)}, u32[]{:S(2)}, u32[]{:S(2)}) collective-permute-start(bf16[256,256]{1,0:T(8,128)(2,1)S(1)} %get-tuple-element.76), channel_id=1, source_target_pairs={{0,4},{1,5},{2,6},{3,7},{4,0},{5,1},{6,2},{7,3},{8,12},{9,13},{10,... | collective-permute-start | bytes 393224 | tf_op jit(solution)/shard_map/ppermute | solution.py:85
  16.4 1.8 %collective-permute-start.12 = (bf16[64,256]{1,0:T(8,128)(2,1)S(1)}, bf16[64,256]{1,0:T(8,128)(2,1)S(1)}, u32[]{:S(2)}, u32[]{:S(2)}) collective-permute-start(bf16[64,256]{1,0:T(8,128)(2,1)S(1)} %get-tuple-element.79.refs_2_), channel_id=1, source_target_pairs={{0,1},{1,0},{2,3},{3,2},{4,5},{5,4},{6,7},{7,6},{8,9},{9,8},{10,11... | collective-permute-start | bytes 98312 | tf_op jit(solution)/shard_map/ppermute | solution.py:85
  19.7 2.2 %shard_map.87 = (f32[1024,256]{1,0:T(8,128)S(1)}, bf16[256,256]{1,0:T(8,128)(2,1)S(1)}, bf16[256,256]{1,0:T(8,128)(2,1)S(1)}, bf16[256,256]{1,0:T(8,128)(2,1)S(1)}, bf16[256,256]{1,0:T(8,128)(2,1)S(1)}) custom-call(bf16[1024,1024]{1,0:T(8,128)(2,1)S(1)} %bitcast.12, bf16[1024,1024]{1,0:T(8,128)(2,1)S(1)} %get-tuple-element.55.sel_ref.left_ref, ...), custom_call_target="tpu_custom_call" | custom-call | flops 1073741824 | bytes 4718592 | tf_op jit(solution)/shard_map/pallas_call | solution.py:29
  22.8 2.7 %collective-permute-start.16 = (bf16[64,256]{1,0:T(8,128)(2,1)S(1)}, bf16[64,256]{1,0:T(8,128)(2,1)S(1)}, u32[]{:S(2)}, u32[]{:S(2)}) collective-permute-start(bf16[64,256]{1,0:T(8,128)(2,1)S(1)} %get-tuple-element.79.refs_2_), channel_id=1, source_target_pairs={{0,9},{1,8},{2,11},{3,10},{4,13},{5,12},{6,15},{7,14},{8,1},{9,0},... | collective-permute-start | bytes 98312 | tf_op jit(solution)/shard_map/ppermute | solution.py:85
  25.5 1.6 %collective-permute-start.10 = (bf16[256,256]{1,0:T(8,128)(2,1)S(1)}, bf16[256,256]{1,0:T(8,128)(2,1)S(1)}, u32[]{:S(2)}, u32[]{:S(2)}) collective-permute-start(bf16[256,256]{1,0:T(8,128)(2,1)S(1)} %get-tuple-element.78), channel_id=1, source_target_pairs={{0,2},{1,3},{2,0},{3,1},{4,6},{5,7},{6,4},{7,5},{8,10},{9,11},{10,... | collective-permute-start | bytes 393224 | tf_op jit(solution)/shard_map/ppermute | solution.py:85
  28.0 1.5 %collective-permute-start.7 = (bf16[256,256]{1,0:T(8,128)(2,1)S(1)}, bf16[256,256]{1,0:T(8,128)(2,1)S(1)}, u32[]{:S(2)}, u32[]{:S(2)}) collective-permute-start(bf16[256,256]{1,0:T(8,128)(2,1)S(1)} %get-tuple-element.69), channel_id=1, source_target_pairs={{0,24},{1,25},{2,26},{3,27},{4,28},{5,29},{6,30},{7,31},{8,16},{9,... | collective-permute-start | bytes 393224 | tf_op jit(solution)/shard_map/ppermute | solution.py:85
  32.3 1.8 %collective-permute-start.18 = (bf16[64,256]{1,0:T(8,128)(2,1)S(1)}, bf16[64,256]{1,0:T(8,128)(2,1)S(1)}, u32[]{:S(2)}, u32[]{:S(2)}) collective-permute-start(bf16[64,256]{1,0:T(8,128)(2,1)S(1)} %get-tuple-element.81), channel_id=1, source_target_pairs={{0,2},{1,3},{2,0},{3,1},{4,6},{5,7},{6,4},{7,5},{8,10},{9,11},{10,... | collective-permute-start | bytes 98312 | tf_op jit(solution)/shard_map/ppermute | solution.py:85
  34.1 2.6 %collective-permute-start.19 = (bf16[64,256]{1,0:T(8,128)(2,1)S(1)}, bf16[64,256]{1,0:T(8,128)(2,1)S(1)}, u32[]{:S(2)}, u32[]{:S(2)}) collective-permute-start(bf16[64,256]{1,0:T(8,128)(2,1)S(1)} %get-tuple-element.82), channel_id=1, source_target_pairs={{0,4},{1,5},{2,6},{3,7},{4,0},{5,1},{6,2},{7,3},{8,12},{9,13},{10,... | collective-permute-start | bytes 98312 | tf_op jit(solution)/shard_map/ppermute | solution.py:85
  36.8 1.5 %shard_map.89 = (f32[1024,256]{1,0:T(8,128)S(1)}, f32[1024,256]{1,0:T(8,128)S(1)}) custom-call(bf16[1024,1024]{1,0:T(8,128)(2,1)S(1)} %get-tuple-element.53.op_ref.left_ref, f32[1024,256]{1,0:T(8,128)S(1)} %shard_map.88.u_ref, f32[1024,256]{1,0:T(8,128)S(1)} %get-tuple-element.65.fix_ref, bf16[1024,1024]{1,0:T(8,128)(2,1)S(1)} %get-tuple-element.58.scatter_ref, ...), custom_call_target="tpu_custom_call" | custom-call | flops 1073741824 | bytes 6553600 | tf_op jit(solution)/shard_map/pallas_call | solution.py:29
  39.5 2.9 %collective-permute-done.20.refs_2_ = bf16[64,256]{1,0:T(8,128)(2,1)S(1)} collective-permute-done((bf16[64,256]{1,0:T(8,128)(2,1)S(1)}, bf16[64,256]{1,0:T(8,128)(2,1)S(1)}, u32[]{:S(2)}, u32[]{:S(2)}) %collective-permute-start.20) | collective-permute-done | bytes 32800 | tf_op jit(solution)/shard_map/ppermute | solution.py:85
  44.3 1.6 %collective-permute-start.24 = (bf16[256,256]{1,0:T(8,128)(2,1)S(1)}, bf16[256,256]{1,0:T(8,128)(2,1)S(1)}, u32[]{:S(2)}, u32[]{:S(2)}) collective-permute-start(bf16[256,256]{1,0:T(8,128)(2,1)S(1)} %get-tuple-element.88), channel_id=1, source_target_pairs={{0,24},{1,25},{2,26},{3,27},{4,28},{5,29},{6,30},{7,31},{8,16},{9,... | collective-permute-start | bytes 393224 | tf_op jit(solution)/shard_map/ppermute | solution.py:85
  45.9 2.3 %shard_map.90.pre_sel_ref = bf16[1024,1024]{1,0:T(8,128)(2,1)S(1)} custom-call(bf16[1024,1024]{1,0:T(8,128)(2,1)S(1)} %get-tuple-element.55.sel_ref.left_ref, bf16[1024,1024]{1,0:T(8,128)(2,1)S(1)} %bitcast.13), custom_call_target="tpu_custom_call" | custom-call | flops 2147483648 | bytes 4194304 | tf_op jit(solution)/shard_map/pallas_call | solution.py:29
  48.4 1.7 %collective-permute-done.22.n2 = bf16[256,256]{1,0:T(8,128)(2,1)S(1)} collective-permute-done((bf16[256,256]{1,0:T(8,128)(2,1)S(1)}, bf16[256,256]{1,0:T(8,128)(2,1)S(1)}, u32[]{:S(2)}, u32[]{:S(2)}) %collective-permute-start.22) | collective-permute-done | bytes 131104 | tf_op jit(solution)/shard_map/ppermute | solution.py:85
  52.2 1.8 %collective-permute-start.30 = (bf16[64,256]{1,0:T(8,128)(2,1)S(1)}, bf16[64,256]{1,0:T(8,128)(2,1)S(1)}, u32[]{:S(2)}, u32[]{:S(2)}) collective-permute-start(bf16[64,256]{1,0:T(8,128)(2,1)S(1)} %get-tuple-element.96.refs_2_), channel_id=1, source_target_pairs={{0,1},{1,0},{2,3},{3,2},{4,5},{5,4},{6,7},{7,6},{8,9},{9,8},{10,11... | collective-permute-start | bytes 98312 | tf_op jit(solution)/shard_map/ppermute | solution.py:85
  56.4 1.8 %collective-permute-start.25 = (bf16[256,256]{1,0:T(8,128)(2,1)S(1)}, bf16[256,256]{1,0:T(8,128)(2,1)S(1)}, u32[]{:S(2)}, u32[]{:S(2)}) collective-permute-start(bf16[256,256]{1,0:T(8,128)(2,1)S(1)} %get-tuple-element.91), channel_id=1, source_target_pairs={{0,1},{1,0},{2,3},{3,2},{4,5},{5,4},{6,7},{7,6},{8,9},{9,8},{10,11... | collective-permute-start | bytes 393224 | tf_op jit(solution)/shard_map/ppermute | solution.py:85
  58.9 1.4 %collective-permute-start.28 = (bf16[256,256]{1,0:T(8,128)(2,1)S(1)}, bf16[256,256]{1,0:T(8,128)(2,1)S(1)}, u32[]{:S(2)}, u32[]{:S(2)}) collective-permute-start(bf16[256,256]{1,0:T(8,128)(2,1)S(1)} %get-tuple-element.95), channel_id=1, source_target_pairs={{0,24},{1,25},{2,26},{3,27},{4,28},{5,29},{6,30},{7,31},{8,16},{9,... | collective-permute-start | bytes 393224 | tf_op jit(solution)/shard_map/ppermute | solution.py:85
  64.3 1.5 %collective-permute-start.36 = (bf16[64,256]{1,0:T(8,128)(2,1)S(1)}, bf16[64,256]{1,0:T(8,128)(2,1)S(1)}, u32[]{:S(2)}, u32[]{:S(2)}) collective-permute-start(bf16[64,256]{1,0:T(8,128)(2,1)S(1)} %get-tuple-element.98), channel_id=1, source_target_pairs={{0,2},{1,3},{2,0},{3,1},{4,6},{5,7},{6,4},{7,5},{8,10},{9,11},{10,... | collective-permute-start | bytes 98312 | tf_op jit(solution)/shard_map/ppermute | solution.py:85
  65.8 1.6 %collective-permute-start.37 = (bf16[64,256]{1,0:T(8,128)(2,1)S(1)}, bf16[64,256]{1,0:T(8,128)(2,1)S(1)}, u32[]{:S(2)}, u32[]{:S(2)}) collective-permute-start(bf16[64,256]{1,0:T(8,128)(2,1)S(1)} %get-tuple-element.99), channel_id=1, source_target_pairs={{0,4},{1,5},{2,6},{3,7},{4,0},{5,1},{6,2},{7,3},{8,12},{9,13},{10,... | collective-permute-start | bytes 98312 | tf_op jit(solution)/shard_map/ppermute | solution.py:85
  67.4 1.4 %collective-permute-start.38 = (bf16[64,256]{1,0:T(8,128)(2,1)S(1)}, bf16[64,256]{1,0:T(8,128)(2,1)S(1)}, u32[]{:S(2)}, u32[]{:S(2)}) collective-permute-start(bf16[64,256]{1,0:T(8,128)(2,1)S(1)} %get-tuple-element.100), channel_id=1, source_target_pairs={{0,6},{1,7},{2,4},{3,5},{4,2},{5,3},{6,0},{7,1},{8,14},{9,15},{10,... | collective-permute-start | bytes 98312 | tf_op jit(solution)/shard_map/ppermute | solution.py:85
  70.7 2.4 %collective-permute-done.38.refs_2_ = bf16[64,256]{1,0:T(8,128)(2,1)S(1)} collective-permute-done((bf16[64,256]{1,0:T(8,128)(2,1)S(1)}, bf16[64,256]{1,0:T(8,128)(2,1)S(1)}, u32[]{:S(2)}, u32[]{:S(2)}) %collective-permute-start.38) | collective-permute-done | bytes 32800 | tf_op jit(solution)/shard_map/ppermute | solution.py:85
  (83 shorter events, 24.6 us)
Async XLA Ops:
  2.2 8.8 %collective-permute-start.8 = (bf16[256,256]{1,0:T(8,128)(2,1)S(1)}, bf16[256,256]{1,0:T(8,128)(2,1)S(1)}, u32[]{:S(2)}, u32[]{:S(2)}) collective-permute-start(bf16[256,256]{1,0:T(8,128)(2,1)S(1)} %get-tuple-element.74), channel_id=1, source_target_pairs={{0,1},{1,0},{2,3},{3,2},{4,5},{5,4},{6,7},{7,6},{8,9},{9,8},{10,11... | collective-permute-start | bytes 393224 | tf_op jit(solution)/shard_map/ppermute | solution.py:85
  7.4 7.4 %collective-permute-start = (bf16[256,256]{1,0:T(8,128)(2,1)S(1)}, bf16[256,256]{1,0:T(8,128)(2,1)S(1)}, u32[]{:S(2)}, u32[]{:S(2)}) collective-permute-start(bf16[256,256]{1,0:T(8,128)(2,1)S(1)} %get-tuple-element.59), channel_id=1, source_target_pairs={{0,1},{1,0},{2,3},{3,2},{4,5},{5,4},{6,7},{7,6},{8,9},{9,8},{10,11... | collective-permute-start | bytes 393224 | tf_op jit(solution)/shard_map/ppermute | solution.py:85
  7.5 7.3 %collective-permute-start.1 = (bf16[256,256]{1,0:T(8,128)(2,1)S(1)}, bf16[256,256]{1,0:T(8,128)(2,1)S(1)}, u32[]{:S(2)}, u32[]{:S(2)}) collective-permute-start(bf16[256,256]{1,0:T(8,128)(2,1)S(1)} %get-tuple-element.60), channel_id=1, source_target_pairs={{0,8},{1,9},{2,10},{3,11},{4,12},{5,13},{6,14},{7,15},{8,0},{9,1},... | collective-permute-start | bytes 393224 | tf_op jit(solution)/shard_map/ppermute | solution.py:85
  9.5 5.8 %collective-permute-start.2 = (bf16[256,256]{1,0:T(8,128)(2,1)S(1)}, bf16[256,256]{1,0:T(8,128)(2,1)S(1)}, u32[]{:S(2)}, u32[]{:S(2)}) collective-permute-start(bf16[256,256]{1,0:T(8,128)(2,1)S(1)} %get-tuple-element.62), channel_id=1, source_target_pairs={{0,16},{1,2},{2,1},{3,4},{4,3},{5,6},{6,5},{7,23},{8,24},{9,10},{1... | collective-permute-start | bytes 393224 | tf_op jit(solution)/shard_map/ppermute | solution.py:85
  9.5 5.8 %collective-permute-start.3 = (bf16[256,256]{1,0:T(8,128)(2,1)S(1)}, bf16[256,256]{1,0:T(8,128)(2,1)S(1)}, u32[]{:S(2)}, u32[]{:S(2)}) collective-permute-start(bf16[256,256]{1,0:T(8,128)(2,1)S(1)} %get-tuple-element.63), channel_id=1, source_target_pairs={{0,24},{1,25},{2,26},{3,27},{4,28},{5,29},{6,30},{7,31},{8,16},{9,... | collective-permute-start | bytes 393224 | tf_op jit(solution)/shard_map/ppermute | solution.py:85
  11.0 14.5 %collective-permute-start.9 = (bf16[256,256]{1,0:T(8,128)(2,1)S(1)}, bf16[256,256]{1,0:T(8,128)(2,1)S(1)}, u32[]{:S(2)}, u32[]{:S(2)}) collective-permute-start(bf16[256,256]{1,0:T(8,128)(2,1)S(1)} %get-tuple-element.76), channel_id=1, source_target_pairs={{0,4},{1,5},{2,6},{3,7},{4,0},{5,1},{6,2},{7,3},{8,12},{9,13},{10,... | collective-permute-start | bytes 393224 | tf_op jit(solution)/shard_map/ppermute | solution.py:85
  16.0 6.2 %collective-permute-start.11 = (bf16[64,256]{1,0:T(8,128)(2,1)S(1)}, bf16[64,256]{1,0:T(8,128)(2,1)S(1)}, u32[]{:S(2)}, u32[]{:S(2)}) collective-permute-start(bf16[64,256]{1,0:T(8,128)(2,1)S(1)} %get-tuple-element.79.refs_2_), channel_id=1, source_target_pairs={{0,16},{1,17},{2,18},{3,19},{4,20},{5,21},{6,22},{7,23},{8,24},{9,... | collective-permute-start | bytes 98312 | tf_op jit(solution)/shard_map/ppermute | solution.py:85
  16.4 6.4 %collective-permute-start.12 = (bf16[64,256]{1,0:T(8,128)(2,1)S(1)}, bf16[64,256]{1,0:T(8,128)(2,1)S(1)}, u32[]{:S(2)}, u32[]{:S(2)}) collective-permute-start(bf16[64,256]{1,0:T(8,128)(2,1)S(1)} %get-tuple-element.79.refs_2_), channel_id=1, source_target_pairs={{0,1},{1,0},{2,3},{3,2},{4,5},{5,4},{6,7},{7,6},{8,9},{9,8},{10,11... | collective-permute-start | bytes 98312 | tf_op jit(solution)/shard_map/ppermute | solution.py:85
  18.2 7.3 %collective-permute-start.14 = (bf16[64,256]{1,0:T(8,128)(2,1)S(1)}, bf16[64,256]{1,0:T(8,128)(2,1)S(1)}, u32[]{:S(2)}, u32[]{:S(2)}) collective-permute-start(bf16[64,256]{1,0:T(8,128)(2,1)S(1)} %get-tuple-element.79.refs_2_), channel_id=1, source_target_pairs={{0,8},{1,9},{2,10},{3,11},{4,12},{5,13},{6,14},{7,15},{8,0},{9,1},... | collective-permute-start | bytes 98312 | tf_op jit(solution)/shard_map/ppermute | solution.py:85
  21.9 7.6 %collective-permute-start.4 = (bf16[256,256]{1,0:T(8,128)(2,1)S(1)}, bf16[256,256]{1,0:T(8,128)(2,1)S(1)}, u32[]{:S(2)}, u32[]{:S(2)}) collective-permute-start(bf16[256,256]{1,0:T(8,128)(2,1)S(1)} %get-tuple-element.66), channel_id=1, source_target_pairs={{0,1},{1,0},{2,3},{3,2},{4,5},{5,4},{6,7},{7,6},{8,9},{9,8},{10,11... | collective-permute-start | bytes 393224 | tf_op jit(solution)/shard_map/ppermute | solution.py:85
  22.3 7.2 %collective-permute-start.5 = (bf16[256,256]{1,0:T(8,128)(2,1)S(1)}, bf16[256,256]{1,0:T(8,128)(2,1)S(1)}, u32[]{:S(2)}, u32[]{:S(2)}) collective-permute-start(bf16[256,256]{1,0:T(8,128)(2,1)S(1)} %get-tuple-element.67), channel_id=1, source_target_pairs={{0,8},{1,9},{2,10},{3,11},{4,12},{5,13},{6,14},{7,15},{8,0},{9,1},... | collective-permute-start | bytes 393224 | tf_op jit(solution)/shard_map/ppermute | solution.py:85
  25.5 6.4 %collective-permute-start.10 = (bf16[256,256]{1,0:T(8,128)(2,1)S(1)}, bf16[256,256]{1,0:T(8,128)(2,1)S(1)}, u32[]{:S(2)}, u32[]{:S(2)}) collective-permute-start(bf16[256,256]{1,0:T(8,128)(2,1)S(1)} %get-tuple-element.78), channel_id=1, source_target_pairs={{0,2},{1,3},{2,0},{3,1},{4,6},{5,7},{6,4},{7,5},{8,10},{9,11},{10,... | collective-permute-start | bytes 393224 | tf_op jit(solution)/shard_map/ppermute | solution.py:85
  28.0 8.8 %collective-permute-start.6 = (bf16[256,256]{1,0:T(8,128)(2,1)S(1)}, bf16[256,256]{1,0:T(8,128)(2,1)S(1)}, u32[]{:S(2)}, u32[]{:S(2)}) collective-permute-start(bf16[256,256]{1,0:T(8,128)(2,1)S(1)} %get-tuple-element.68), channel_id=1, source_target_pairs={{0,16},{1,2},{2,1},{3,4},{4,3},{5,6},{6,5},{7,23},{8,24},{9,10},{1... | collective-permute-start | bytes 393224 | tf_op jit(solution)/shard_map/ppermute | solution.py:85
  28.0 8.8 %collective-permute-start.7 = (bf16[256,256]{1,0:T(8,128)(2,1)S(1)}, bf16[256,256]{1,0:T(8,128)(2,1)S(1)}, u32[]{:S(2)}, u32[]{:S(2)}) collective-permute-start(bf16[256,256]{1,0:T(8,128)(2,1)S(1)} %get-tuple-element.69), channel_id=1, source_target_pairs={{0,24},{1,25},{2,26},{3,27},{4,28},{5,29},{6,30},{7,31},{8,16},{9,... | collective-permute-start | bytes 393224 | tf_op jit(solution)/shard_map/ppermute | solution.py:85
  32.3 6.0 %collective-permute-start.18 = (bf16[64,256]{1,0:T(8,128)(2,1)S(1)}, bf16[64,256]{1,0:T(8,128)(2,1)S(1)}, u32[]{:S(2)}, u32[]{:S(2)}) collective-permute-start(bf16[64,256]{1,0:T(8,128)(2,1)S(1)} %get-tuple-element.81), channel_id=1, source_target_pairs={{0,2},{1,3},{2,0},{3,1},{4,6},{5,7},{6,4},{7,5},{8,10},{9,11},{10,... | collective-permute-start | bytes 98312 | tf_op jit(solution)/shard_map/ppermute | solution.py:85
  43.7 6.3 %collective-permute-start.22 = (bf16[256,256]{1,0:T(8,128)(2,1)S(1)}, bf16[256,256]{1,0:T(8,128)(2,1)S(1)}, u32[]{:S(2)}, u32[]{:S(2)}) collective-permute-start(bf16[256,256]{1,0:T(8,128)(2,1)S(1)} %get-tuple-element.86), channel_id=1, source_target_pairs={{0,8},{1,9},{2,10},{3,11},{4,12},{5,13},{6,14},{7,15},{8,0},{9,1},... | collective-permute-start | bytes 393224 | tf_op jit(solution)/shard_map/ppermute | solution.py:85
  44.3 6.2 %collective-permute-start.23 = (bf16[256,256]{1,0:T(8,128)(2,1)S(1)}, bf16[256,256]{1,0:T(8,128)(2,1)S(1)}, u32[]{:S(2)}, u32[]{:S(2)}) collective-permute-start(bf16[256,256]{1,0:T(8,128)(2,1)S(1)} %get-tuple-element.87), channel_id=1, source_target_pairs={{0,16},{1,2},{2,1},{3,4},{4,3},{5,6},{6,5},{7,23},{8,24},{9,10},{1... | collective-permute-start | bytes 393224 | tf_op jit(solution)/shard_map/ppermute | solution.py:85
  44.3 6.3 %collective-permute-start.24 = (bf16[256,256]{1,0:T(8,128)(2,1)S(1)}, bf16[256,256]{1,0:T(8,128)(2,1)S(1)}, u32[]{:S(2)}, u32[]{:S(2)}) collective-permute-start(bf16[256,256]{1,0:T(8,128)(2,1)S(1)} %get-tuple-element.88), channel_id=1, source_target_pairs={{0,24},{1,25},{2,26},{3,27},{4,28},{5,29},{6,30},{7,31},{8,16},{9,... | collective-permute-start | bytes 393224 | tf_op jit(solution)/shard_map/ppermute | solution.py:85
  51.4 6.8 %collective-permute-start.29 = (bf16[64,256]{1,0:T(8,128)(2,1)S(1)}, bf16[64,256]{1,0:T(8,128)(2,1)S(1)}, u32[]{:S(2)}, u32[]{:S(2)}) collective-permute-start(bf16[64,256]{1,0:T(8,128)(2,1)S(1)} %get-tuple-element.96.refs_2_), channel_id=1, source_target_pairs={{0,16},{1,17},{2,18},{3,19},{4,20},{5,21},{6,22},{7,23},{8,24},{9,... | collective-permute-start | bytes 98312 | tf_op jit(solution)/shard_map/ppermute | solution.py:85
  52.2 6.7 %collective-permute-start.30 = (bf16[64,256]{1,0:T(8,128)(2,1)S(1)}, bf16[64,256]{1,0:T(8,128)(2,1)S(1)}, u32[]{:S(2)}, u32[]{:S(2)}) collective-permute-start(bf16[64,256]{1,0:T(8,128)(2,1)S(1)} %get-tuple-element.96.refs_2_), channel_id=1, source_target_pairs={{0,1},{1,0},{2,3},{3,2},{4,5},{5,4},{6,7},{7,6},{8,9},{9,8},{10,11... | collective-permute-start | bytes 98312 | tf_op jit(solution)/shard_map/ppermute | solution.py:85
  56.4 9.4 %collective-permute-start.25 = (bf16[256,256]{1,0:T(8,128)(2,1)S(1)}, bf16[256,256]{1,0:T(8,128)(2,1)S(1)}, u32[]{:S(2)}, u32[]{:S(2)}) collective-permute-start(bf16[256,256]{1,0:T(8,128)(2,1)S(1)} %get-tuple-element.91), channel_id=1, source_target_pairs={{0,1},{1,0},{2,3},{3,2},{4,5},{5,4},{6,7},{7,6},{8,9},{9,8},{10,11... | collective-permute-start | bytes 393224 | tf_op jit(solution)/shard_map/ppermute | solution.py:85
  58.2 9.2 %collective-permute-start.26 = (bf16[256,256]{1,0:T(8,128)(2,1)S(1)}, bf16[256,256]{1,0:T(8,128)(2,1)S(1)}, u32[]{:S(2)}, u32[]{:S(2)}) collective-permute-start(bf16[256,256]{1,0:T(8,128)(2,1)S(1)} %get-tuple-element.92), channel_id=1, source_target_pairs={{0,8},{1,9},{2,10},{3,11},{4,12},{5,13},{6,14},{7,15},{8,0},{9,1},... | collective-permute-start | bytes 393224 | tf_op jit(solution)/shard_map/ppermute | solution.py:85
  58.9 10.4 %collective-permute-start.27 = (bf16[256,256]{1,0:T(8,128)(2,1)S(1)}, bf16[256,256]{1,0:T(8,128)(2,1)S(1)}, u32[]{:S(2)}, u32[]{:S(2)}) collective-permute-start(bf16[256,256]{1,0:T(8,128)(2,1)S(1)} %get-tuple-element.94), channel_id=1, source_target_pairs={{0,16},{1,2},{2,1},{3,4},{4,3},{5,6},{6,5},{7,23},{8,24},{9,10},{1... | collective-permute-start | bytes 393224 | tf_op jit(solution)/shard_map/ppermute | solution.py:85
  58.9 10.4 %collective-permute-start.28 = (bf16[256,256]{1,0:T(8,128)(2,1)S(1)}, bf16[256,256]{1,0:T(8,128)(2,1)S(1)}, u32[]{:S(2)}, u32[]{:S(2)}) collective-permute-start(bf16[256,256]{1,0:T(8,128)(2,1)S(1)} %get-tuple-element.95), channel_id=1, source_target_pairs={{0,24},{1,25},{2,26},{3,27},{4,28},{5,29},{6,30},{7,31},{8,16},{9,... | collective-permute-start | bytes 393224 | tf_op jit(solution)/shard_map/ppermute | solution.py:85
  (19 other events, 80.9 us)

commit v6 on v5

--- a/solution.py
+++ b/solution.py
@@ -306,6 +306,14 @@
         give_ref[:, k * half : (k + 1) * half] = jnp.where(low == 0, right, left)
 
 
+def pair_kernel(mine_ref, *refs):
+    others, out_ref = refs[:-1], refs[-1]
+    nb = mine_ref.shape[0]
+    g = lax.axis_index("grp")
+    for dg, ref in enumerate((mine_ref, *others)):
+        out_ref[pl.ds(pl.multiple_of((g ^ dg) * nb, nb), nb), :] = ref[...]
+
+
 def coarse_kernel(stepwise, geometry, row_size, nb, moves, *refs):
     grid_rows, _, lines = geometry
     width = 2 * nb
@@ -313,11 +321,12 @@
     arrays, refs = refs[:count], refs[count:]
     vectors, refs = refs[: len(moves)], refs[len(moves) :]
     mine_ref, others, (stack, total) = refs[0], refs[1:lines], refs[lines:]
-    g, r, c = (lax.axis_index(axis) for axis in AXES)
+    r, c = lax.axis_index("row"), lax.axis_index("col")
     line = c // 2
-    for (dg, dr, dc), vector in zip(moves, vectors):
-        at = (((g ^ dg) * row_size + (r ^ dr)) * 2 + ((c % 2) ^ dc)) * nb
-        stack[pl.ds(pl.multiple_of(at, nb), nb), :] = vector[...]
+    for (dr, dc), vector in zip(moves, vectors):
+        for core in range(vector.shape[0] // nb):
+            at = ((core * row_size + (r ^ dr)) * 2 + ((c % 2) ^ dc)) * nb
+            stack[pl.ds(pl.multiple_of(at, nb), nb), :] = vector[core * nb : (core + 1) * nb, :]
     if stepwise:
         blocks = [
             (arrays[k // 2][:, (k % 2) * width : (k % 2 + 1) * width], line ^ (2 * (k % 2) + k // 2)) for k in range(4)
@@ -357,7 +366,6 @@
 
     halo_pairs = [matching(sizes, m % 2, m < 2) for m in range(4)]
     far_moves = [(dr, dc) for dr in range(row_size) for dc in range(2)]
-    moves = [(dg, dr, dc) for dr, dc in far_moves for dg in range(grps)]
 
     def swap_pairs(dg, dr, dc):
         return pairs_of(sizes, lambda g, r, c: (g ^ dg, r ^ dr, c ^ dc))
@@ -419,21 +427,18 @@
             [early, scatter, based_t, near[1], near[3]],
             flops // 2,
         )
-        vectors = {}
-        for dr, dc in far_moves:
-            got = coarse if dr + dc == 0 else send(coarse, swap_pairs(0, dr, dc))
-            vectors[0, dr, dc] = got
-            for dg in range(1, grps):
-                vectors[dg, dr, dc] = send(got, swap_pairs(dg, 0, 0))
+        cores = [coarse] + [send(coarse, swap_pairs(dg, 0, 0)) for dg in range(1, grps)]
+        pair = call(pair_kernel, shape((grps * nb, cases), BF), cores, n)
+        vectors = [send(pair, swap_pairs(0, dr, dc)) if dr + dc else pair for dr, dc in far_moves]
         if sweep:
             fix, *own = call(fix_kernel, [field] + [edge] * 4, [pre_sel, resid], flops)
         else:
             fix, *own = call(fix_plain_kernel, [field] + [edge] * 4, [pre, sel, resid], 2 * flops)
         near = halo(own)
         mine, *others = call(
-            functools.partial(coarse_kernel, stepwise, geometry, row_size, nb, moves),
+            functools.partial(coarse_kernel, stepwise, geometry, row_size, nb, far_moves),
             [shape((nb, cases), F32)] + [vector] * (lines - 1),
-            [*blocks, *(vectors[move] for move in moves)],
+            [*blocks, *vectors],
             2 * lines * nb * 2 * nb * grid_rows * cases,
             [pltpu.VMEM((2 * grid_rows * nb, cases), BF), pltpu.VMEM((lines * nb, cases), F32)],
         )

time: 74.6 us -> 80.6 us (1.080)
  waiting for transfers between devices: 14 us -> 19.8 us
    ppermute x39 -> x33, waiting for transfers between devices: 14 us -> 19.8 us  [send(): return lax.ppermute(value, AXES, pairs)]
    pallas_call x21 -> x23, Pallas kernels: 19.8 us -> 19.7 us  [call(): pl.pallas_call(kernel, out_shape=outs, in_specs=[hbm if k in far else vme...]
    ppermute x39 -> x33, starting transfers between devices: 40.2 us -> 40 us  [send(): return lax.ppermute(value, AXES, pairs)]
  transfers between devices with their start and end apart: 39 -> 33, of which waited for: 11 -> 10; matrix products, arithmetic and copies ran while one was open for 0% -> 0% of each run, Pallas kernels for 20% -> 18%
where the time goes in v6:
time: 80.6 us; the launch traced here: 80.4 us
  starting transfers between devices  40 us (50%)
  waiting for transfers between devices  19.8 us (25%)
  Pallas kernels  19.7 us (24%)
    ppermute x33, starting transfers between devices, send(): return lax.ppermute(value, AXES, pairs)  40 us
    ppermute x33, waiting for transfers between devices, send(): return lax.ppermute(value, AXES, pairs)  19.8 us
    pallas_call x23, Pallas kernels, call(): pl.pallas_call(kernel, out_shape=outs, in_specs=[hbm if k in far else vme...  19.7 us
  transfers between devices with their start and end apart: 33, of which 10 were waited for; matrix products, arithmetic and copies ran while one was open for 0% of the time, Pallas kernels for 18%

profile of v6, /device:TPU:0, one launch (start us, length us, event | category | flops | bytes accessed | tf_op | source)
XLA Modules:
  0.0 80.4 jit_solution(10598959850576905889)
XLA Ops:
  0.0 2.1 %shard_map.82 = (s32[1,1024]{1,0:T(1,128)S(1)}, bf16[1024,1024]{1,0:T(8,128)(2,1)S(1)}, bf16[1024,1024]{1,0:T(8,128)(2,1)S(1)}, f32[1024,256]{1,0:T(8,128)S(1)},...) custom-call(s32[1,1024]{1,0:T(1,128)} %bitcast.18, bf16[1024,1024]{1,0:T(8,128)(2,1)} %bitcast.16, ...), custom_call_target="tpu_custom_call" | custom-call | flops 1048576 | bytes 3411968 | tf_op jit(solution)/shard_map/pallas_call | solution.py:29
  2.2 3.0 %collective-permute-start.8 = (bf16[256,256]{1,0:T(8,128)(2,1)S(1)}, bf16[256,256]{1,0:T(8,128)(2,1)S(1)}, u32[]{:S(2)}, u32[]{:S(2)}) collective-permute-start(bf16[256,256]{1,0:T(8,128)(2,1)S(1)} %get-tuple-element.74), channel_id=1, source_target_pairs={{0,1},{1,0},{2,3},{3,2},{4,5},{5,4},{6,7},{7,6},{8,9},{9,8},{10,11... | collective-permute-start | bytes 393224 | tf_op jit(solution)/shard_map/ppermute | solution.py:85
  5.2 2.2 %shard_map.83 = (f32[1024,256]{1,0:T(8,128)S(1)}, bf16[256,256]{1,0:T(8,128)(2,1)S(1)}, bf16[256,256]{1,0:T(8,128)(2,1)S(1)}, bf16[256,256]{1,0:T(8,128)(2,1)S(1)}, bf16[256,256]{1,0:T(8,128)(2,1)S(1)}) custom-call(bf16[1024,1024]{1,0:T(8,128)(2,1)S(1)} %get-tuple-element.53.op_ref.left_ref, f32[1024,256]{1,0:T(8,128)S(1)} %get-tuple-element.54.u_ref, ...), custom_call_target="tpu_custom_call" | custom-call | flops 1073741824 | bytes 5242880 | tf_op jit(solution)/shard_map/pallas_call | solution.py:29
  7.5 2.0 %collective-permute-start.1 = (bf16[256,256]{1,0:T(8,128)(2,1)S(1)}, bf16[256,256]{1,0:T(8,128)(2,1)S(1)}, u32[]{:S(2)}, u32[]{:S(2)}) collective-permute-start(bf16[256,256]{1,0:T(8,128)(2,1)S(1)} %get-tuple-element.60), channel_id=1, source_target_pairs={{0,8},{1,9},{2,10},{3,11},{4,12},{5,13},{6,14},{7,15},{8,0},{9,1},... | collective-permute-start | bytes 393224 | tf_op jit(solution)/shard_map/ppermute | solution.py:85
  11.0 3.9 %collective-permute-start.9 = (bf16[256,256]{1,0:T(8,128)(2,1)S(1)}, bf16[256,256]{1,0:T(8,128)(2,1)S(1)}, u32[]{:S(2)}, u32[]{:S(2)}) collective-permute-start(bf16[256,256]{1,0:T(8,128)(2,1)S(1)} %get-tuple-element.76), channel_id=1, source_target_pairs={{0,4},{1,5},{2,6},{3,7},{4,0},{5,1},{6,2},{7,3},{8,12},{9,13},{10,... | collective-permute-start | bytes 393224 | tf_op jit(solution)/shard_map/ppermute | solution.py:85
  16.9 2.2 %shard_map.87 = (f32[1024,256]{1,0:T(8,128)S(1)}, bf16[256,256]{1,0:T(8,128)(2,1)S(1)}, bf16[256,256]{1,0:T(8,128)(2,1)S(1)}, bf16[256,256]{1,0:T(8,128)(2,1)S(1)}, bf16[256,256]{1,0:T(8,128)(2,1)S(1)}) custom-call(bf16[1024,1024]{1,0:T(8,128)(2,1)S(1)} %bitcast.12, bf16[1024,1024]{1,0:T(8,128)(2,1)S(1)} %get-tuple-element.55.sel_ref.left_ref, ...), custom_call_target="tpu_custom_call" | custom-call | flops 1073741824 | bytes 4718592 | tf_op jit(solution)/shard_map/pallas_call | solution.py:29
  19.2 1.7 %collective-permute-start.4 = (bf16[256,256]{1,0:T(8,128)(2,1)S(1)}, bf16[256,256]{1,0:T(8,128)(2,1)S(1)}, u32[]{:S(2)}, u32[]{:S(2)}) collective-permute-start(bf16[256,256]{1,0:T(8,128)(2,1)S(1)} %get-tuple-element.66), channel_id=1, source_target_pairs={{0,1},{1,0},{2,3},{3,2},{4,5},{5,4},{6,7},{7,6},{8,9},{9,8},{10,11... | collective-permute-start | bytes 393224 | tf_op jit(solution)/shard_map/ppermute | solution.py:85
  22.4 2.5 %collective-permute-start.10 = (bf16[256,256]{1,0:T(8,128)(2,1)S(1)}, bf16[256,256]{1,0:T(8,128)(2,1)S(1)}, u32[]{:S(2)}, u32[]{:S(2)}) collective-permute-start(bf16[256,256]{1,0:T(8,128)(2,1)S(1)} %get-tuple-element.78), channel_id=1, source_target_pairs={{0,2},{1,3},{2,0},{3,1},{4,6},{5,7},{6,4},{7,5},{8,10},{9,11},{10,... | collective-permute-start | bytes 393224 | tf_op jit(solution)/shard_map/ppermute | solution.py:85
  24.9 1.4 %collective-permute-done.12.refs_3_ = bf16[128,256]{1,0:T(8,128)(2,1)S(1)} collective-permute-done((bf16[128,256]{1,0:T(8,128)(2,1)S(1)}, bf16[128,256]{1,0:T(8,128)(2,1)S(1)}, u32[]{:S(2)}, u32[]{:S(2)}) %collective-permute-start.12) | collective-permute-done | bytes 65568 | tf_op jit(solution)/shard_map/ppermute | solution.py:85
  27.9 2.8 %collective-permute-start.14 = (bf16[128,256]{1,0:T(8,128)(2,1)S(1)}, bf16[128,256]{1,0:T(8,128)(2,1)S(1)}, u32[]{:S(2)}, u32[]{:S(2)}) collective-permute-start(bf16[128,256]{1,0:T(8,128)(2,1)S(1)} %shard_map.94.refs_2_), channel_id=1, source_target_pairs={{0,9},{1,8},{2,11},{3,10},{4,13},{5,12},{6,15},{7,14},{8,1},{9,0},... | collective-permute-start | bytes 196616 | tf_op jit(solution)/shard_map/ppermute | solution.py:85
  31.9 3.0 %collective-permute-done.13.refs_4_ = bf16[128,256]{1,0:T(8,128)(2,1)S(1)} collective-permute-done((bf16[128,256]{1,0:T(8,128)(2,1)S(1)}, bf16[128,256]{1,0:T(8,128)(2,1)S(1)}, u32[]{:S(2)}, u32[]{:S(2)}) %collective-permute-start.13) | collective-permute-done | bytes 65568 | tf_op jit(solution)/shard_map/ppermute | solution.py:85
  35.3 1.9 %collective-permute-start.15 = (bf16[64,256]{1,0:T(8,128)(2,1)S(1)}, bf16[64,256]{1,0:T(8,128)(2,1)S(1)}, u32[]{:S(2)}, u32[]{:S(2)}) collective-permute-start(bf16[64,256]{1,0:T(8,128)(2,1)S(1)} %get-tuple-element.81), channel_id=1, source_target_pairs={{0,2},{1,3},{2,0},{3,1},{4,6},{5,7},{6,4},{7,5},{8,10},{9,11},{10,... | collective-permute-start | bytes 98312 | tf_op jit(solution)/shard_map/ppermute | solution.py:85
  37.2 2.1 %collective-permute-start.16 = (bf16[64,256]{1,0:T(8,128)(2,1)S(1)}, bf16[64,256]{1,0:T(8,128)(2,1)S(1)}, u32[]{:S(2)}, u32[]{:S(2)}) collective-permute-start(bf16[64,256]{1,0:T(8,128)(2,1)S(1)} %get-tuple-element.82), channel_id=1, source_target_pairs={{0,4},{1,5},{2,6},{3,7},{4,0},{5,1},{6,2},{7,3},{8,12},{9,13},{10,... | collective-permute-start | bytes 98312 | tf_op jit(solution)/shard_map/ppermute | solution.py:85
  39.8 1.5 %shard_map.89 = (f32[1024,256]{1,0:T(8,128)S(1)}, f32[1024,256]{1,0:T(8,128)S(1)}) custom-call(bf16[1024,1024]{1,0:T(8,128)(2,1)S(1)} %get-tuple-element.53.op_ref.left_ref, f32[1024,256]{1,0:T(8,128)S(1)} %shard_map.88.u_ref, f32[1024,256]{1,0:T(8,128)S(1)} %get-tuple-element.65.fix_ref, bf16[1024,1024]{1,0:T(8,128)(2,1)S(1)} %get-tuple-element.58.scatter_ref, ...), custom_call_target="tpu_custom_call" | custom-call | flops 1073741824 | bytes 6553600 | tf_op jit(solution)/shard_map/pallas_call | solution.py:29
  42.3 2.7 %collective-permute-done.17.refs_2_ = bf16[64,256]{1,0:T(8,128)(2,1)S(1)} collective-permute-done((bf16[64,256]{1,0:T(8,128)(2,1)S(1)}, bf16[64,256]{1,0:T(8,128)(2,1)S(1)}, u32[]{:S(2)}, u32[]{:S(2)}) %collective-permute-start.17) | collective-permute-done | bytes 32800 | tf_op jit(solution)/shard_map/ppermute | solution.py:85
  48.6 2.4 %collective-permute-done.18.n0 = bf16[256,256]{1,0:T(8,128)(2,1)S(1)} collective-permute-done((bf16[256,256]{1,0:T(8,128)(2,1)S(1)}, bf16[256,256]{1,0:T(8,128)(2,1)S(1)}, u32[]{:S(2)}, u32[]{:S(2)}) %collective-permute-start.18) | collective-permute-done | bytes 131104 | tf_op jit(solution)/shard_map/ppermute | solution.py:85
  54.8 2.3 %shard_map.90.pre_sel_ref = bf16[1024,1024]{1,0:T(8,128)(2,1)S(1)} custom-call(bf16[1024,1024]{1,0:T(8,128)(2,1)S(1)} %get-tuple-element.55.sel_ref.left_ref, bf16[1024,1024]{1,0:T(8,128)(2,1)S(1)} %bitcast.13), custom_call_target="tpu_custom_call" | custom-call | flops 2147483648 | bytes 4194304 | tf_op jit(solution)/shard_map/pallas_call | solution.py:29
  57.2 1.9 %collective-permute-start.27 = (bf16[128,256]{1,0:T(8,128)(2,1)S(1)}, bf16[128,256]{1,0:T(8,128)(2,1)S(1)}, u32[]{:S(2)}, u32[]{:S(2)}) collective-permute-start(bf16[128,256]{1,0:T(8,128)(2,1)S(1)} %shard_map.102.refs_2_), channel_id=1, source_target_pairs={{0,1},{1,0},{2,3},{3,2},{4,5},{5,4},{6,7},{7,6},{8,9},{9,8},{10,11... | collective-permute-start | bytes 196616 | tf_op jit(solution)/shard_map/ppermute | solution.py:85
  60.1 1.3 %collective-permute-start.22 = (bf16[256,256]{1,0:T(8,128)(2,1)S(1)}, bf16[256,256]{1,0:T(8,128)(2,1)S(1)}, u32[]{:S(2)}, u32[]{:S(2)}) collective-permute-start(bf16[256,256]{1,0:T(8,128)(2,1)S(1)} %get-tuple-element.91), channel_id=1, source_target_pairs={{0,1},{1,0},{2,3},{3,2},{4,5},{5,4},{6,7},{7,6},{8,9},{9,8},{10,11... | collective-permute-start | bytes 393224 | tf_op jit(solution)/shard_map/ppermute | solution.py:85
  63.6 1.7 %collective-permute-start.29 = (bf16[128,256]{1,0:T(8,128)(2,1)S(1)}, bf16[128,256]{1,0:T(8,128)(2,1)S(1)}, u32[]{:S(2)}, u32[]{:S(2)}) collective-permute-start(bf16[128,256]{1,0:T(8,128)(2,1)S(1)} %shard_map.102.refs_2_), channel_id=1, source_target_pairs={{0,9},{1,8},{2,11},{3,10},{4,13},{5,12},{6,15},{7,14},{8,1},{9,0},... | collective-permute-start | bytes 196616 | tf_op jit(solution)/shard_map/ppermute | solution.py:85
  65.3 3.5 %collective-permute-done.29.refs_5_ = bf16[128,256]{1,0:T(8,128)(2,1)S(1)} collective-permute-done((bf16[128,256]{1,0:T(8,128)(2,1)S(1)}, bf16[128,256]{1,0:T(8,128)(2,1)S(1)}, u32[]{:S(2)}, u32[]{:S(2)}) %collective-permute-start.29) | collective-permute-done | bytes 65568 | tf_op jit(solution)/shard_map/ppermute | solution.py:85
  69.1 2.5 %collective-permute-start.30 = (bf16[64,256]{1,0:T(8,128)(2,1)S(1)}, bf16[64,256]{1,0:T(8,128)(2,1)S(1)}, u32[]{:S(2)}, u32[]{:S(2)}) collective-permute-start(bf16[64,256]{1,0:T(8,128)(2,1)S(1)} %get-tuple-element.98), channel_id=1, source_target_pairs={{0,2},{1,3},{2,0},{3,1},{4,6},{5,7},{6,4},{7,5},{8,10},{9,11},{10,... | collective-permute-start | bytes 98312 | tf_op jit(solution)/shard_map/ppermute | solution.py:85
  71.6 1.8 %collective-permute-start.31 = (bf16[64,256]{1,0:T(8,128)(2,1)S(1)}, bf16[64,256]{1,0:T(8,128)(2,1)S(1)}, u32[]{:S(2)}, u32[]{:S(2)}) collective-permute-start(bf16[64,256]{1,0:T(8,128)(2,1)S(1)} %get-tuple-element.99), channel_id=1, source_target_pairs={{0,4},{1,5},{2,6},{3,7},{4,0},{5,1},{6,2},{7,3},{8,12},{9,13},{10,... | collective-permute-start | bytes 98312 | tf_op jit(solution)/shard_map/ppermute | solution.py:85
  76.7 2.3 %collective-permute-done.32.refs_2_ = bf16[64,256]{1,0:T(8,128)(2,1)S(1)} collective-permute-done((bf16[64,256]{1,0:T(8,128)(2,1)S(1)}, bf16[64,256]{1,0:T(8,128)(2,1)S(1)}, u32[]{:S(2)}, u32[]{:S(2)}) %collective-permute-start.32) | collective-permute-done | bytes 32800 | tf_op jit(solution)/shard_map/ppermute | solution.py:85
  (73 shorter events, 25.1 us)
Async XLA Ops:
  2.2 8.8 %collective-permute-start.8 = (bf16[256,256]{1,0:T(8,128)(2,1)S(1)}, bf16[256,256]{1,0:T(8,128)(2,1)S(1)}, u32[]{:S(2)}, u32[]{:S(2)}) collective-permute-start(bf16[256,256]{1,0:T(8,128)(2,1)S(1)} %get-tuple-element.74), channel_id=1, source_target_pairs={{0,1},{1,0},{2,3},{3,2},{4,5},{5,4},{6,7},{7,6},{8,9},{9,8},{10,11... | collective-permute-start | bytes 393224 | tf_op jit(solution)/shard_map/ppermute | solution.py:85
  7.4 7.4 %collective-permute-start = (bf16[256,256]{1,0:T(8,128)(2,1)S(1)}, bf16[256,256]{1,0:T(8,128)(2,1)S(1)}, u32[]{:S(2)}, u32[]{:S(2)}) collective-permute-start(bf16[256,256]{1,0:T(8,128)(2,1)S(1)} %get-tuple-element.59), channel_id=1, source_target_pairs={{0,1},{1,0},{2,3},{3,2},{4,5},{5,4},{6,7},{7,6},{8,9},{9,8},{10,11... | collective-permute-start | bytes 393224 | tf_op jit(solution)/shard_map/ppermute | solution.py:85
  7.5 7.3 %collective-permute-start.1 = (bf16[256,256]{1,0:T(8,128)(2,1)S(1)}, bf16[256,256]{1,0:T(8,128)(2,1)S(1)}, u32[]{:S(2)}, u32[]{:S(2)}) collective-permute-start(bf16[256,256]{1,0:T(8,128)(2,1)S(1)} %get-tuple-element.60), channel_id=1, source_target_pairs={{0,8},{1,9},{2,10},{3,11},{4,12},{5,13},{6,14},{7,15},{8,0},{9,1},... | collective-permute-start | bytes 393224 | tf_op jit(solution)/shard_map/ppermute | solution.py:85
  9.5 5.8 %collective-permute-start.2 = (bf16[256,256]{1,0:T(8,128)(2,1)S(1)}, bf16[256,256]{1,0:T(8,128)(2,1)S(1)}, u32[]{:S(2)}, u32[]{:S(2)}) collective-permute-start(bf16[256,256]{1,0:T(8,128)(2,1)S(1)} %get-tuple-element.62), channel_id=1, source_target_pairs={{0,16},{1,2},{2,1},{3,4},{4,3},{5,6},{6,5},{7,23},{8,24},{9,10},{1... | collective-permute-start | bytes 393224 | tf_op jit(solution)/shard_map/ppermute | solution.py:85
  9.5 5.8 %collective-permute-start.3 = (bf16[256,256]{1,0:T(8,128)(2,1)S(1)}, bf16[256,256]{1,0:T(8,128)(2,1)S(1)}, u32[]{:S(2)}, u32[]{:S(2)}) collective-permute-start(bf16[256,256]{1,0:T(8,128)(2,1)S(1)} %get-tuple-element.63), channel_id=1, source_target_pairs={{0,24},{1,25},{2,26},{3,27},{4,28},{5,29},{6,30},{7,31},{8,16},{9,... | collective-permute-start | bytes 393224 | tf_op jit(solution)/shard_map/ppermute | solution.py:85
  11.0 11.4 %collective-permute-start.9 = (bf16[256,256]{1,0:T(8,128)(2,1)S(1)}, bf16[256,256]{1,0:T(8,128)(2,1)S(1)}, u32[]{:S(2)}, u32[]{:S(2)}) collective-permute-start(bf16[256,256]{1,0:T(8,128)(2,1)S(1)} %get-tuple-element.76), channel_id=1, source_target_pairs={{0,4},{1,5},{2,6},{3,7},{4,0},{5,1},{6,2},{7,3},{8,12},{9,13},{10,... | collective-permute-start | bytes 393224 | tf_op jit(solution)/shard_map/ppermute | solution.py:85
  16.0 5.9 %collective-permute-start.11 = (bf16[64,256]{1,0:T(8,128)(2,1)S(1)}, bf16[64,256]{1,0:T(8,128)(2,1)S(1)}, u32[]{:S(2)}, u32[]{:S(2)}) collective-permute-start(bf16[64,256]{1,0:T(8,128)(2,1)S(1)} %get-tuple-element.79.mine_ref), channel_id=1, source_target_pairs={{0,16},{1,17},{2,18},{3,19},{4,20},{5,21},{6,22},{7,23},{8,24},{9,... | collective-permute-start | bytes 98312 | tf_op jit(solution)/shard_map/ppermute | solution.py:85
  19.2 8.3 %collective-permute-start.4 = (bf16[256,256]{1,0:T(8,128)(2,1)S(1)}, bf16[256,256]{1,0:T(8,128)(2,1)S(1)}, u32[]{:S(2)}, u32[]{:S(2)}) collective-permute-start(bf16[256,256]{1,0:T(8,128)(2,1)S(1)} %get-tuple-element.66), channel_id=1, source_target_pairs={{0,1},{1,0},{2,3},{3,2},{4,5},{5,4},{6,7},{7,6},{8,9},{9,8},{10,11... | collective-permute-start | bytes 393224 | tf_op jit(solution)/shard_map/ppermute | solution.py:85
  20.9 7.0 %collective-permute-start.5 = (bf16[256,256]{1,0:T(8,128)(2,1)S(1)}, bf16[256,256]{1,0:T(8,128)(2,1)S(1)}, u32[]{:S(2)}, u32[]{:S(2)}) collective-permute-start(bf16[256,256]{1,0:T(8,128)(2,1)S(1)} %get-tuple-element.67), channel_id=1, source_target_pairs={{0,8},{1,9},{2,10},{3,11},{4,12},{5,13},{6,14},{7,15},{8,0},{9,1},... | collective-permute-start | bytes 393224 | tf_op jit(solution)/shard_map/ppermute | solution.py:85
  22.4 12.5 %collective-permute-start.10 = (bf16[256,256]{1,0:T(8,128)(2,1)S(1)}, bf16[256,256]{1,0:T(8,128)(2,1)S(1)}, u32[]{:S(2)}, u32[]{:S(2)}) collective-permute-start(bf16[256,256]{1,0:T(8,128)(2,1)S(1)} %get-tuple-element.78), channel_id=1, source_target_pairs={{0,2},{1,3},{2,0},{3,1},{4,6},{5,7},{6,4},{7,5},{8,10},{9,11},{10,... | collective-permute-start | bytes 393224 | tf_op jit(solution)/shard_map/ppermute | solution.py:85
  24.9 14.8 %collective-permute-start.6 = (bf16[256,256]{1,0:T(8,128)(2,1)S(1)}, bf16[256,256]{1,0:T(8,128)(2,1)S(1)}, u32[]{:S(2)}, u32[]{:S(2)}) collective-permute-start(bf16[256,256]{1,0:T(8,128)(2,1)S(1)} %get-tuple-element.68), channel_id=1, source_target_pairs={{0,16},{1,2},{2,1},{3,4},{4,3},{5,6},{6,5},{7,23},{8,24},{9,10},{1... | collective-permute-start | bytes 393224 | tf_op jit(solution)/shard_map/ppermute | solution.py:85
  26.4 13.4 %collective-permute-start.7 = (bf16[256,256]{1,0:T(8,128)(2,1)S(1)}, bf16[256,256]{1,0:T(8,128)(2,1)S(1)}, u32[]{:S(2)}, u32[]{:S(2)}) collective-permute-start(bf16[256,256]{1,0:T(8,128)(2,1)S(1)} %get-tuple-element.69), channel_id=1, source_target_pairs={{0,24},{1,25},{2,26},{3,27},{4,28},{5,29},{6,30},{7,31},{8,16},{9,... | collective-permute-start | bytes 393224 | tf_op jit(solution)/shard_map/ppermute | solution.py:85
  27.5 7.5 %collective-permute-start.13 = (bf16[128,256]{1,0:T(8,128)(2,1)S(1)}, bf16[128,256]{1,0:T(8,128)(2,1)S(1)}, u32[]{:S(2)}, u32[]{:S(2)}) collective-permute-start(bf16[128,256]{1,0:T(8,128)(2,1)S(1)} %shard_map.94.refs_2_), channel_id=1, source_target_pairs={{0,8},{1,9},{2,10},{3,11},{4,12},{5,13},{6,14},{7,15},{8,0},{9,1},... | collective-permute-start | bytes 196616 | tf_op jit(solution)/shard_map/ppermute | solution.py:85
  27.9 7.1 %collective-permute-start.14 = (bf16[128,256]{1,0:T(8,128)(2,1)S(1)}, bf16[128,256]{1,0:T(8,128)(2,1)S(1)}, u32[]{:S(2)}, u32[]{:S(2)}) collective-permute-start(bf16[128,256]{1,0:T(8,128)(2,1)S(1)} %shard_map.94.refs_2_), channel_id=1, source_target_pairs={{0,9},{1,8},{2,11},{3,10},{4,13},{5,12},{6,15},{7,14},{8,1},{9,0},... | collective-permute-start | bytes 196616 | tf_op jit(solution)/shard_map/ppermute | solution.py:85
  35.3 6.0 %collective-permute-start.15 = (bf16[64,256]{1,0:T(8,128)(2,1)S(1)}, bf16[64,256]{1,0:T(8,128)(2,1)S(1)}, u32[]{:S(2)}, u32[]{:S(2)}) collective-permute-start(bf16[64,256]{1,0:T(8,128)(2,1)S(1)} %get-tuple-element.81), channel_id=1, source_target_pairs={{0,2},{1,3},{2,0},{3,1},{4,6},{5,7},{6,4},{7,5},{8,10},{9,11},{10,... | collective-permute-start | bytes 98312 | tf_op jit(solution)/shard_map/ppermute | solution.py:85
  39.3 5.7 %collective-permute-start.17 = (bf16[64,256]{1,0:T(8,128)(2,1)S(1)}, bf16[64,256]{1,0:T(8,128)(2,1)S(1)}, u32[]{:S(2)}, u32[]{:S(2)}) collective-permute-start(bf16[64,256]{1,0:T(8,128)(2,1)S(1)} %get-tuple-element.83), channel_id=1, source_target_pairs={{0,6},{1,7},{2,4},{3,5},{4,2},{5,3},{6,0},{7,1},{8,14},{9,15},{10,... | collective-permute-start | bytes 98312 | tf_op jit(solution)/shard_map/ppermute | solution.py:85
  46.5 5.7 %collective-permute-start.19 = (bf16[256,256]{1,0:T(8,128)(2,1)S(1)}, bf16[256,256]{1,0:T(8,128)(2,1)S(1)}, u32[]{:S(2)}, u32[]{:S(2)}) collective-permute-start(bf16[256,256]{1,0:T(8,128)(2,1)S(1)} %get-tuple-element.86), channel_id=1, source_target_pairs={{0,8},{1,9},{2,10},{3,11},{4,12},{5,13},{6,14},{7,15},{8,0},{9,1},... | collective-permute-start | bytes 393224 | tf_op jit(solution)/shard_map/ppermute | solution.py:85
  47.7 5.8 %collective-permute-start.21 = (bf16[256,256]{1,0:T(8,128)(2,1)S(1)}, bf16[256,256]{1,0:T(8,128)(2,1)S(1)}, u32[]{:S(2)}, u32[]{:S(2)}) collective-permute-start(bf16[256,256]{1,0:T(8,128)(2,1)S(1)} %get-tuple-element.88), channel_id=1, source_target_pairs={{0,24},{1,25},{2,26},{3,27},{4,28},{5,29},{6,30},{7,31},{8,16},{9,... | collective-permute-start | bytes 393224 | tf_op jit(solution)/shard_map/ppermute | solution.py:85
  60.1 11.5 %collective-permute-start.22 = (bf16[256,256]{1,0:T(8,128)(2,1)S(1)}, bf16[256,256]{1,0:T(8,128)(2,1)S(1)}, u32[]{:S(2)}, u32[]{:S(2)}) collective-permute-start(bf16[256,256]{1,0:T(8,128)(2,1)S(1)} %get-tuple-element.91), channel_id=1, source_target_pairs={{0,1},{1,0},{2,3},{3,2},{4,5},{5,4},{6,7},{7,6},{8,9},{9,8},{10,11... | collective-permute-start | bytes 393224 | tf_op jit(solution)/shard_map/ppermute | solution.py:85
  61.4 11.9 %collective-permute-start.23 = (bf16[256,256]{1,0:T(8,128)(2,1)S(1)}, bf16[256,256]{1,0:T(8,128)(2,1)S(1)}, u32[]{:S(2)}, u32[]{:S(2)}) collective-permute-start(bf16[256,256]{1,0:T(8,128)(2,1)S(1)} %get-tuple-element.92), channel_id=1, source_target_pairs={{0,8},{1,9},{2,10},{3,11},{4,12},{5,13},{6,14},{7,15},{8,0},{9,1},... | collective-permute-start | bytes 393224 | tf_op jit(solution)/shard_map/ppermute | solution.py:85
  62.2 12.6 %collective-permute-start.24 = (bf16[256,256]{1,0:T(8,128)(2,1)S(1)}, bf16[256,256]{1,0:T(8,128)(2,1)S(1)}, u32[]{:S(2)}, u32[]{:S(2)}) collective-permute-start(bf16[256,256]{1,0:T(8,128)(2,1)S(1)} %get-tuple-element.94), channel_id=1, source_target_pairs={{0,16},{1,2},{2,1},{3,4},{4,3},{5,6},{6,5},{7,23},{8,24},{9,10},{1... | collective-permute-start | bytes 393224 | tf_op jit(solution)/shard_map/ppermute | solution.py:85
  62.2 12.6 %collective-permute-start.25 = (bf16[256,256]{1,0:T(8,128)(2,1)S(1)}, bf16[256,256]{1,0:T(8,128)(2,1)S(1)}, u32[]{:S(2)}, u32[]{:S(2)}) collective-permute-start(bf16[256,256]{1,0:T(8,128)(2,1)S(1)} %get-tuple-element.95), channel_id=1, source_target_pairs={{0,24},{1,25},{2,26},{3,27},{4,28},{5,29},{6,30},{7,31},{8,16},{9,... | collective-permute-start | bytes 393224 | tf_op jit(solution)/shard_map/ppermute | solution.py:85
  69.1 6.4 %collective-permute-start.30 = (bf16[64,256]{1,0:T(8,128)(2,1)S(1)}, bf16[64,256]{1,0:T(8,128)(2,1)S(1)}, u32[]{:S(2)}, u32[]{:S(2)}) collective-permute-start(bf16[64,256]{1,0:T(8,128)(2,1)S(1)} %get-tuple-element.98), channel_id=1, source_target_pairs={{0,2},{1,3},{2,0},{3,1},{4,6},{5,7},{6,4},{7,5},{8,10},{9,11},{10,... | collective-permute-start | bytes 98312 | tf_op jit(solution)/shard_map/ppermute | solution.py:85
  73.3 5.7 %collective-permute-start.32 = (bf16[64,256]{1,0:T(8,128)(2,1)S(1)}, bf16[64,256]{1,0:T(8,128)(2,1)S(1)}, u32[]{:S(2)}, u32[]{:S(2)}) collective-permute-start(bf16[64,256]{1,0:T(8,128)(2,1)S(1)} %get-tuple-element.100), channel_id=1, source_target_pairs={{0,6},{1,7},{2,4},{3,5},{4,2},{5,3},{6,0},{7,1},{8,14},{9,15},{10,... | collective-permute-start | bytes 98312 | tf_op jit(solution)/shard_map/ppermute | solution.py:85
  (13 other events, 62.7 us)

commit v7 on v6

--- a/solution.py
+++ b/solution.py
@@ -201,12 +201,11 @@
     coarse_ref[...] = dot(based_t_ref[...], resid).astype(BF)
 
 
-def fix_plain_kernel(pre_ref, sel_ref, resid_ref, fix_ref, *edges):
-    fix = dot(pre_ref[...], resid_ref[...]).astype(BF)
+def pick_kernel(sel_ref, whole_ref, fix_ref, *edges):
     part = edges[0].shape[0]
     for m, edge in enumerate(edges):
         rows = slice(m * part, (m + 1) * part)
-        own = dot(sel_ref[rows, :], fix)
+        own = dot(sel_ref[rows, :], whole_ref[...])
         fix_ref[rows, :] = own
         edge[...] = own.astype(BF)
 
@@ -433,7 +432,8 @@
         if sweep:
             fix, *own = call(fix_kernel, [field] + [edge] * 4, [pre_sel, resid], flops)
         else:
-            fix, *own = call(fix_plain_kernel, [field] + [edge] * 4, [pre, sel, resid], 2 * flops)
+            whole = call(product_kernel, shape((n, cases), BF), [pre, resid], flops)
+            fix, *own = call(pick_kernel, [field] + [edge] * 4, [sel, whole], flops)
         near = halo(own)
         mine, *others = call(
             functools.partial(coarse_kernel, stepwise, geometry, row_size, nb, far_moves),

time: 80.6 us -> 79.7 us (0.989)
  starting transfers between devices: 40 us -> 39.1 us
    ppermute x33, starting transfers between devices: 40 us -> 39.1 us  [send(): return lax.ppermute(value, AXES, pairs)]
    pallas_call x23 -> x24, Pallas kernels: 19.7 us -> 19.1 us  [call(): pl.pallas_call(kernel, out_shape=outs, in_specs=[hbm if k in far else vme...]
  transfers between devices with their start and end apart: 33 -> 33, of which waited for: 10 -> 11; matrix products, arithmetic and copies ran while one was open for 0% -> 0% of each run, Pallas kernels for 18% -> 18%
where the time goes in v7:
time: 79.7 us; the launch traced here: 79.5 us
  starting transfers between devices  39.1 us (49%)
  waiting for transfers between devices  20.4 us (26%)
  Pallas kernels  19.1 us (24%)
    ppermute x33, starting transfers between devices, send(): return lax.ppermute(value, AXES, pairs)  39.1 us
    ppermute x33, waiting for transfers between devices, send(): return lax.ppermute(value, AXES, pairs)  20.4 us
    pallas_call x24, Pallas kernels, call(): pl.pallas_call(kernel, out_shape=outs, in_specs=[hbm if k in far else vme...  19.1 us
  transfers between devices with their start and end apart: 33, of which 11 were waited for; matrix products, arithmetic and copies ran while one was open for 0% of the time, Pallas kernels for 18%

profile of v7, /device:TPU:0, one launch (start us, length us, event | category | flops | bytes accessed | tf_op | source)
XLA Modules:
  0.0 79.5 jit_solution(6756370150527742459)
XLA Ops:
  0.0 2.1 %shard_map.82 = (s32[1,1024]{1,0:T(1,128)S(1)}, bf16[1024,1024]{1,0:T(8,128)(2,1)S(1)}, bf16[1024,1024]{1,0:T(8,128)(2,1)S(1)}, f32[1024,256]{1,0:T(8,128)S(1)},...) custom-call(s32[1,1024]{1,0:T(1,128)} %bitcast.18, bf16[1024,1024]{1,0:T(8,128)(2,1)} %bitcast.16, ...), custom_call_target="tpu_custom_call" | custom-call | flops 1048576 | bytes 3411968 | tf_op jit(solution)/shard_map/pallas_call | solution.py:29
  2.2 3.0 %collective-permute-start.8 = (bf16[256,256]{1,0:T(8,128)(2,1)S(1)}, bf16[256,256]{1,0:T(8,128)(2,1)S(1)}, u32[]{:S(2)}, u32[]{:S(2)}) collective-permute-start(bf16[256,256]{1,0:T(8,128)(2,1)S(1)} %get-tuple-element.74), channel_id=1, source_target_pairs={{0,1},{1,0},{2,3},{3,2},{4,5},{5,4},{6,7},{7,6},{8,9},{9,8},{10,11... | collective-permute-start | bytes 393224 | tf_op jit(solution)/shard_map/ppermute | solution.py:85
  5.2 2.2 %shard_map.83 = (f32[1024,256]{1,0:T(8,128)S(1)}, bf16[256,256]{1,0:T(8,128)(2,1)S(1)}, bf16[256,256]{1,0:T(8,128)(2,1)S(1)}, bf16[256,256]{1,0:T(8,128)(2,1)S(1)}, bf16[256,256]{1,0:T(8,128)(2,1)S(1)}) custom-call(bf16[1024,1024]{1,0:T(8,128)(2,1)S(1)} %get-tuple-element.53.op_ref.left_ref, f32[1024,256]{1,0:T(8,128)S(1)} %get-tuple-element.54.u_ref, ...), custom_call_target="tpu_custom_call" | custom-call | flops 1073741824 | bytes 5242880 | tf_op jit(solution)/shard_map/pallas_call | solution.py:29
  7.5 2.0 %collective-permute-start.1 = (bf16[256,256]{1,0:T(8,128)(2,1)S(1)}, bf16[256,256]{1,0:T(8,128)(2,1)S(1)}, u32[]{:S(2)}, u32[]{:S(2)}) collective-permute-start(bf16[256,256]{1,0:T(8,128)(2,1)S(1)} %get-tuple-element.60), channel_id=1, source_target_pairs={{0,8},{1,9},{2,10},{3,11},{4,12},{5,13},{6,14},{7,15},{8,0},{9,1},... | collective-permute-start | bytes 393224 | tf_op jit(solution)/shard_map/ppermute | solution.py:85
  11.0 3.9 %collective-permute-start.9 = (bf16[256,256]{1,0:T(8,128)(2,1)S(1)}, bf16[256,256]{1,0:T(8,128)(2,1)S(1)}, u32[]{:S(2)}, u32[]{:S(2)}) collective-permute-start(bf16[256,256]{1,0:T(8,128)(2,1)S(1)} %get-tuple-element.76), channel_id=1, source_target_pairs={{0,4},{1,5},{2,6},{3,7},{4,0},{5,1},{6,2},{7,3},{8,12},{9,13},{10,... | collective-permute-start | bytes 393224 | tf_op jit(solution)/shard_map/ppermute | solution.py:85
  18.4 1.7 %collective-permute-start.4 = (bf16[256,256]{1,0:T(8,128)(2,1)S(1)}, bf16[256,256]{1,0:T(8,128)(2,1)S(1)}, u32[]{:S(2)}, u32[]{:S(2)}) collective-permute-start(bf16[256,256]{1,0:T(8,128)(2,1)S(1)} %get-tuple-element.66), channel_id=1, source_target_pairs={{0,1},{1,0},{2,3},{3,2},{4,5},{5,4},{6,7},{7,6},{8,9},{9,8},{10,11... | collective-permute-start | bytes 393224 | tf_op jit(solution)/shard_map/ppermute | solution.py:85
  22.1 2.0 %collective-permute-start.10 = (bf16[256,256]{1,0:T(8,128)(2,1)S(1)}, bf16[256,256]{1,0:T(8,128)(2,1)S(1)}, u32[]{:S(2)}, u32[]{:S(2)}) collective-permute-start(bf16[256,256]{1,0:T(8,128)(2,1)S(1)} %get-tuple-element.78), channel_id=1, source_target_pairs={{0,2},{1,3},{2,0},{3,1},{4,6},{5,7},{6,4},{7,5},{8,10},{9,11},{10,... | collective-permute-start | bytes 393224 | tf_op jit(solution)/shard_map/ppermute | solution.py:85
  24.2 1.4 %collective-permute-done.12.refs_3_ = bf16[128,256]{1,0:T(8,128)(2,1)S(1)} collective-permute-done((bf16[128,256]{1,0:T(8,128)(2,1)S(1)}, bf16[128,256]{1,0:T(8,128)(2,1)S(1)}, u32[]{:S(2)}, u32[]{:S(2)}) %collective-permute-start.12) | collective-permute-done | bytes 65568 | tf_op jit(solution)/shard_map/ppermute | solution.py:85
  27.1 2.7 %collective-permute-start.14 = (bf16[128,256]{1,0:T(8,128)(2,1)S(1)}, bf16[128,256]{1,0:T(8,128)(2,1)S(1)}, u32[]{:S(2)}, u32[]{:S(2)}) collective-permute-start(bf16[128,256]{1,0:T(8,128)(2,1)S(1)} %shard_map.95.refs_2_), channel_id=1, source_target_pairs={{0,9},{1,8},{2,11},{3,10},{4,13},{5,12},{6,15},{7,14},{8,1},{9,0},... | collective-permute-start | bytes 196616 | tf_op jit(solution)/shard_map/ppermute | solution.py:85
  31.0 3.2 %collective-permute-done.13.refs_4_ = bf16[128,256]{1,0:T(8,128)(2,1)S(1)} collective-permute-done((bf16[128,256]{1,0:T(8,128)(2,1)S(1)}, bf16[128,256]{1,0:T(8,128)(2,1)S(1)}, u32[]{:S(2)}, u32[]{:S(2)}) %collective-permute-start.13) | collective-permute-done | bytes 65568 | tf_op jit(solution)/shard_map/ppermute | solution.py:85
  34.5 1.6 %collective-permute-start.15 = (bf16[64,256]{1,0:T(8,128)(2,1)S(1)}, bf16[64,256]{1,0:T(8,128)(2,1)S(1)}, u32[]{:S(2)}, u32[]{:S(2)}) collective-permute-start(bf16[64,256]{1,0:T(8,128)(2,1)S(1)} %get-tuple-element.81), channel_id=1, source_target_pairs={{0,2},{1,3},{2,0},{3,1},{4,6},{5,7},{6,4},{7,5},{8,10},{9,11},{10,... | collective-permute-start | bytes 98312 | tf_op jit(solution)/shard_map/ppermute | solution.py:85
  36.2 2.3 %collective-permute-start.16 = (bf16[64,256]{1,0:T(8,128)(2,1)S(1)}, bf16[64,256]{1,0:T(8,128)(2,1)S(1)}, u32[]{:S(2)}, u32[]{:S(2)}) collective-permute-start(bf16[64,256]{1,0:T(8,128)(2,1)S(1)} %get-tuple-element.82), channel_id=1, source_target_pairs={{0,4},{1,5},{2,6},{3,7},{4,0},{5,1},{6,2},{7,3},{8,12},{9,13},{10,... | collective-permute-start | bytes 98312 | tf_op jit(solution)/shard_map/ppermute | solution.py:85
  39.0 1.5 %shard_map.90 = (f32[1024,256]{1,0:T(8,128)S(1)}, f32[1024,256]{1,0:T(8,128)S(1)}) custom-call(bf16[1024,1024]{1,0:T(8,128)(2,1)S(1)} %get-tuple-element.53.op_ref.left_ref, f32[1024,256]{1,0:T(8,128)S(1)} %shard_map.89.u_ref, f32[1024,256]{1,0:T(8,128)S(1)} %get-tuple-element.65.fix_ref, bf16[1024,1024]{1,0:T(8,128)(2,1)S(1)} %get-tuple-element.58.scatter_ref, ...), custom_call_target="tpu_custom_call" | custom-call | flops 1073741824 | bytes 6553600 | tf_op jit(solution)/shard_map/pallas_call | solution.py:29
  41.6 2.7 %collective-permute-done.17.refs_2_ = bf16[64,256]{1,0:T(8,128)(2,1)S(1)} collective-permute-done((bf16[64,256]{1,0:T(8,128)(2,1)S(1)}, bf16[64,256]{1,0:T(8,128)(2,1)S(1)}, u32[]{:S(2)}, u32[]{:S(2)}) %collective-permute-start.17) | collective-permute-done | bytes 32800 | tf_op jit(solution)/shard_map/ppermute | solution.py:85
  47.8 2.4 %collective-permute-done.18.n0 = bf16[256,256]{1,0:T(8,128)(2,1)S(1)} collective-permute-done((bf16[256,256]{1,0:T(8,128)(2,1)S(1)}, bf16[256,256]{1,0:T(8,128)(2,1)S(1)}, u32[]{:S(2)}, u32[]{:S(2)}) %collective-permute-start.18) | collective-permute-done | bytes 131104 | tf_op jit(solution)/shard_map/ppermute | solution.py:85
  53.9 2.3 %shard_map.91.pre_sel_ref = bf16[1024,1024]{1,0:T(8,128)(2,1)S(1)} custom-call(bf16[1024,1024]{1,0:T(8,128)(2,1)S(1)} %get-tuple-element.55.sel_ref.left_ref, bf16[1024,1024]{1,0:T(8,128)(2,1)S(1)} %bitcast.13), custom_call_target="tpu_custom_call" | custom-call | flops 2147483648 | bytes 4194304 | tf_op jit(solution)/shard_map/pallas_call | solution.py:29
  56.3 1.8 %collective-permute-start.27 = (bf16[128,256]{1,0:T(8,128)(2,1)S(1)}, bf16[128,256]{1,0:T(8,128)(2,1)S(1)}, u32[]{:S(2)}, u32[]{:S(2)}) collective-permute-start(bf16[128,256]{1,0:T(8,128)(2,1)S(1)} %shard_map.103.refs_2_), channel_id=1, source_target_pairs={{0,1},{1,0},{2,3},{3,2},{4,5},{5,4},{6,7},{7,6},{8,9},{9,8},{10,11... | collective-permute-start | bytes 196616 | tf_op jit(solution)/shard_map/ppermute | solution.py:85
  59.3 1.4 %collective-permute-start.22 = (bf16[256,256]{1,0:T(8,128)(2,1)S(1)}, bf16[256,256]{1,0:T(8,128)(2,1)S(1)}, u32[]{:S(2)}, u32[]{:S(2)}) collective-permute-start(bf16[256,256]{1,0:T(8,128)(2,1)S(1)} %get-tuple-element.91), channel_id=1, source_target_pairs={{0,1},{1,0},{2,3},{3,2},{4,5},{5,4},{6,7},{7,6},{8,9},{9,8},{10,11... | collective-permute-start | bytes 393224 | tf_op jit(solution)/shard_map/ppermute | solution.py:85
  61.4 1.4 %collective-permute-start.25 = (bf16[256,256]{1,0:T(8,128)(2,1)S(1)}, bf16[256,256]{1,0:T(8,128)(2,1)S(1)}, u32[]{:S(2)}, u32[]{:S(2)}) collective-permute-start(bf16[256,256]{1,0:T(8,128)(2,1)S(1)} %get-tuple-element.95), channel_id=1, source_target_pairs={{0,24},{1,25},{2,26},{3,27},{4,28},{5,29},{6,30},{7,31},{8,16},{9,... | collective-permute-start | bytes 393224 | tf_op jit(solution)/shard_map/ppermute | solution.py:85
  62.8 1.6 %collective-permute-start.29 = (bf16[128,256]{1,0:T(8,128)(2,1)S(1)}, bf16[128,256]{1,0:T(8,128)(2,1)S(1)}, u32[]{:S(2)}, u32[]{:S(2)}) collective-permute-start(bf16[128,256]{1,0:T(8,128)(2,1)S(1)} %shard_map.103.refs_2_), channel_id=1, source_target_pairs={{0,9},{1,8},{2,11},{3,10},{4,13},{5,12},{6,15},{7,14},{8,1},{9,0},... | collective-permute-start | bytes 196616 | tf_op jit(solution)/shard_map/ppermute | solution.py:85
  64.5 3.5 %collective-permute-done.29.refs_5_ = bf16[128,256]{1,0:T(8,128)(2,1)S(1)} collective-permute-done((bf16[128,256]{1,0:T(8,128)(2,1)S(1)}, bf16[128,256]{1,0:T(8,128)(2,1)S(1)}, u32[]{:S(2)}, u32[]{:S(2)}) %collective-permute-start.29) | collective-permute-done | bytes 65568 | tf_op jit(solution)/shard_map/ppermute | solution.py:85
  68.3 2.4 %collective-permute-start.30 = (bf16[64,256]{1,0:T(8,128)(2,1)S(1)}, bf16[64,256]{1,0:T(8,128)(2,1)S(1)}, u32[]{:S(2)}, u32[]{:S(2)}) collective-permute-start(bf16[64,256]{1,0:T(8,128)(2,1)S(1)} %get-tuple-element.98), channel_id=1, source_target_pairs={{0,2},{1,3},{2,0},{3,1},{4,6},{5,7},{6,4},{7,5},{8,10},{9,11},{10,... | collective-permute-start | bytes 98312 | tf_op jit(solution)/shard_map/ppermute | solution.py:85
  70.8 1.6 %collective-permute-start.31 = (bf16[64,256]{1,0:T(8,128)(2,1)S(1)}, bf16[64,256]{1,0:T(8,128)(2,1)S(1)}, u32[]{:S(2)}, u32[]{:S(2)}) collective-permute-start(bf16[64,256]{1,0:T(8,128)(2,1)S(1)} %get-tuple-element.99), channel_id=1, source_target_pairs={{0,4},{1,5},{2,6},{3,7},{4,0},{5,1},{6,2},{7,3},{8,12},{9,13},{10,... | collective-permute-start | bytes 98312 | tf_op jit(solution)/shard_map/ppermute | solution.py:85
  76.0 2.2 %collective-permute-done.32.refs_2_ = bf16[64,256]{1,0:T(8,128)(2,1)S(1)} collective-permute-done((bf16[64,256]{1,0:T(8,128)(2,1)S(1)}, bf16[64,256]{1,0:T(8,128)(2,1)S(1)}, u32[]{:S(2)}, u32[]{:S(2)}) %collective-permute-start.32) | collective-permute-done | bytes 32800 | tf_op jit(solution)/shard_map/ppermute | solution.py:85
  (74 shorter events, 25.8 us)
Async XLA Ops:
  2.2 8.8 %collective-permute-start.8 = (bf16[256,256]{1,0:T(8,128)(2,1)S(1)}, bf16[256,256]{1,0:T(8,128)(2,1)S(1)}, u32[]{:S(2)}, u32[]{:S(2)}) collective-permute-start(bf16[256,256]{1,0:T(8,128)(2,1)S(1)} %get-tuple-element.74), channel_id=1, source_target_pairs={{0,1},{1,0},{2,3},{3,2},{4,5},{5,4},{6,7},{7,6},{8,9},{9,8},{10,11... | collective-permute-start | bytes 393224 | tf_op jit(solution)/shard_map/ppermute | solution.py:85
  7.4 7.4 %collective-permute-start = (bf16[256,256]{1,0:T(8,128)(2,1)S(1)}, bf16[256,256]{1,0:T(8,128)(2,1)S(1)}, u32[]{:S(2)}, u32[]{:S(2)}) collective-permute-start(bf16[256,256]{1,0:T(8,128)(2,1)S(1)} %get-tuple-element.59), channel_id=1, source_target_pairs={{0,1},{1,0},{2,3},{3,2},{4,5},{5,4},{6,7},{7,6},{8,9},{9,8},{10,11... | collective-permute-start | bytes 393224 | tf_op jit(solution)/shard_map/ppermute | solution.py:85
  7.5 7.3 %collective-permute-start.1 = (bf16[256,256]{1,0:T(8,128)(2,1)S(1)}, bf16[256,256]{1,0:T(8,128)(2,1)S(1)}, u32[]{:S(2)}, u32[]{:S(2)}) collective-permute-start(bf16[256,256]{1,0:T(8,128)(2,1)S(1)} %get-tuple-element.60), channel_id=1, source_target_pairs={{0,8},{1,9},{2,10},{3,11},{4,12},{5,13},{6,14},{7,15},{8,0},{9,1},... | collective-permute-start | bytes 393224 | tf_op jit(solution)/shard_map/ppermute | solution.py:85
  9.5 5.8 %collective-permute-start.2 = (bf16[256,256]{1,0:T(8,128)(2,1)S(1)}, bf16[256,256]{1,0:T(8,128)(2,1)S(1)}, u32[]{:S(2)}, u32[]{:S(2)}) collective-permute-start(bf16[256,256]{1,0:T(8,128)(2,1)S(1)} %get-tuple-element.62), channel_id=1, source_target_pairs={{0,16},{1,2},{2,1},{3,4},{4,3},{5,6},{6,5},{7,23},{8,24},{9,10},{1... | collective-permute-start | bytes 393224 | tf_op jit(solution)/shard_map/ppermute | solution.py:85
  9.5 5.8 %collective-permute-start.3 = (bf16[256,256]{1,0:T(8,128)(2,1)S(1)}, bf16[256,256]{1,0:T(8,128)(2,1)S(1)}, u32[]{:S(2)}, u32[]{:S(2)}) collective-permute-start(bf16[256,256]{1,0:T(8,128)(2,1)S(1)} %get-tuple-element.63), channel_id=1, source_target_pairs={{0,24},{1,25},{2,26},{3,27},{4,28},{5,29},{6,30},{7,31},{8,16},{9,... | collective-permute-start | bytes 393224 | tf_op jit(solution)/shard_map/ppermute | solution.py:85
  11.0 11.1 %collective-permute-start.9 = (bf16[256,256]{1,0:T(8,128)(2,1)S(1)}, bf16[256,256]{1,0:T(8,128)(2,1)S(1)}, u32[]{:S(2)}, u32[]{:S(2)}) collective-permute-start(bf16[256,256]{1,0:T(8,128)(2,1)S(1)} %get-tuple-element.76), channel_id=1, source_target_pairs={{0,4},{1,5},{2,6},{3,7},{4,0},{5,1},{6,2},{7,3},{8,12},{9,13},{10,... | collective-permute-start | bytes 393224 | tf_op jit(solution)/shard_map/ppermute | solution.py:85
  18.4 8.3 %collective-permute-start.4 = (bf16[256,256]{1,0:T(8,128)(2,1)S(1)}, bf16[256,256]{1,0:T(8,128)(2,1)S(1)}, u32[]{:S(2)}, u32[]{:S(2)}) collective-permute-start(bf16[256,256]{1,0:T(8,128)(2,1)S(1)} %get-tuple-element.66), channel_id=1, source_target_pairs={{0,1},{1,0},{2,3},{3,2},{4,5},{5,4},{6,7},{7,6},{8,9},{9,8},{10,11... | collective-permute-start | bytes 393224 | tf_op jit(solution)/shard_map/ppermute | solution.py:85
  20.1 7.0 %collective-permute-start.5 = (bf16[256,256]{1,0:T(8,128)(2,1)S(1)}, bf16[256,256]{1,0:T(8,128)(2,1)S(1)}, u32[]{:S(2)}, u32[]{:S(2)}) collective-permute-start(bf16[256,256]{1,0:T(8,128)(2,1)S(1)} %get-tuple-element.67), channel_id=1, source_target_pairs={{0,8},{1,9},{2,10},{3,11},{4,12},{5,13},{6,14},{7,15},{8,0},{9,1},... | collective-permute-start | bytes 393224 | tf_op jit(solution)/shard_map/ppermute | solution.py:85
  22.1 12.1 %collective-permute-start.10 = (bf16[256,256]{1,0:T(8,128)(2,1)S(1)}, bf16[256,256]{1,0:T(8,128)(2,1)S(1)}, u32[]{:S(2)}, u32[]{:S(2)}) collective-permute-start(bf16[256,256]{1,0:T(8,128)(2,1)S(1)} %get-tuple-element.78), channel_id=1, source_target_pairs={{0,2},{1,3},{2,0},{3,1},{4,6},{5,7},{6,4},{7,5},{8,10},{9,11},{10,... | collective-permute-start | bytes 393224 | tf_op jit(solution)/shard_map/ppermute | solution.py:85
  24.2 14.8 %collective-permute-start.6 = (bf16[256,256]{1,0:T(8,128)(2,1)S(1)}, bf16[256,256]{1,0:T(8,128)(2,1)S(1)}, u32[]{:S(2)}, u32[]{:S(2)}) collective-permute-start(bf16[256,256]{1,0:T(8,128)(2,1)S(1)} %get-tuple-element.68), channel_id=1, source_target_pairs={{0,16},{1,2},{2,1},{3,4},{4,3},{5,6},{6,5},{7,23},{8,24},{9,10},{1... | collective-permute-start | bytes 393224 | tf_op jit(solution)/shard_map/ppermute | solution.py:85
  25.6 13.4 %collective-permute-start.7 = (bf16[256,256]{1,0:T(8,128)(2,1)S(1)}, bf16[256,256]{1,0:T(8,128)(2,1)S(1)}, u32[]{:S(2)}, u32[]{:S(2)}) collective-permute-start(bf16[256,256]{1,0:T(8,128)(2,1)S(1)} %get-tuple-element.69), channel_id=1, source_target_pairs={{0,24},{1,25},{2,26},{3,27},{4,28},{5,29},{6,30},{7,31},{8,16},{9,... | collective-permute-start | bytes 393224 | tf_op jit(solution)/shard_map/ppermute | solution.py:85
  26.7 7.5 %collective-permute-start.13 = (bf16[128,256]{1,0:T(8,128)(2,1)S(1)}, bf16[128,256]{1,0:T(8,128)(2,1)S(1)}, u32[]{:S(2)}, u32[]{:S(2)}) collective-permute-start(bf16[128,256]{1,0:T(8,128)(2,1)S(1)} %shard_map.95.refs_2_), channel_id=1, source_target_pairs={{0,8},{1,9},{2,10},{3,11},{4,12},{5,13},{6,14},{7,15},{8,0},{9,1},... | collective-permute-start | bytes 196616 | tf_op jit(solution)/shard_map/ppermute | solution.py:85
  27.1 7.1 %collective-permute-start.14 = (bf16[128,256]{1,0:T(8,128)(2,1)S(1)}, bf16[128,256]{1,0:T(8,128)(2,1)S(1)}, u32[]{:S(2)}, u32[]{:S(2)}) collective-permute-start(bf16[128,256]{1,0:T(8,128)(2,1)S(1)} %shard_map.95.refs_2_), channel_id=1, source_target_pairs={{0,9},{1,8},{2,11},{3,10},{4,13},{5,12},{6,15},{7,14},{8,1},{9,0},... | collective-permute-start | bytes 196616 | tf_op jit(solution)/shard_map/ppermute | solution.py:85
  34.5 6.0 %collective-permute-start.15 = (bf16[64,256]{1,0:T(8,128)(2,1)S(1)}, bf16[64,256]{1,0:T(8,128)(2,1)S(1)}, u32[]{:S(2)}, u32[]{:S(2)}) collective-permute-start(bf16[64,256]{1,0:T(8,128)(2,1)S(1)} %get-tuple-element.81), channel_id=1, source_target_pairs={{0,2},{1,3},{2,0},{3,1},{4,6},{5,7},{6,4},{7,5},{8,10},{9,11},{10,... | collective-permute-start | bytes 98312 | tf_op jit(solution)/shard_map/ppermute | solution.py:85
  36.2 5.4 %collective-permute-start.16 = (bf16[64,256]{1,0:T(8,128)(2,1)S(1)}, bf16[64,256]{1,0:T(8,128)(2,1)S(1)}, u32[]{:S(2)}, u32[]{:S(2)}) collective-permute-start(bf16[64,256]{1,0:T(8,128)(2,1)S(1)} %get-tuple-element.82), channel_id=1, source_target_pairs={{0,4},{1,5},{2,6},{3,7},{4,0},{5,1},{6,2},{7,3},{8,12},{9,13},{10,... | collective-permute-start | bytes 98312 | tf_op jit(solution)/shard_map/ppermute | solution.py:85
  38.5 5.7 %collective-permute-start.17 = (bf16[64,256]{1,0:T(8,128)(2,1)S(1)}, bf16[64,256]{1,0:T(8,128)(2,1)S(1)}, u32[]{:S(2)}, u32[]{:S(2)}) collective-permute-start(bf16[64,256]{1,0:T(8,128)(2,1)S(1)} %get-tuple-element.83), channel_id=1, source_target_pairs={{0,6},{1,7},{2,4},{3,5},{4,2},{5,3},{6,0},{7,1},{8,14},{9,15},{10,... | collective-permute-start | bytes 98312 | tf_op jit(solution)/shard_map/ppermute | solution.py:85
  45.6 5.6 %collective-permute-start.19 = (bf16[256,256]{1,0:T(8,128)(2,1)S(1)}, bf16[256,256]{1,0:T(8,128)(2,1)S(1)}, u32[]{:S(2)}, u32[]{:S(2)}) collective-permute-start(bf16[256,256]{1,0:T(8,128)(2,1)S(1)} %get-tuple-element.86), channel_id=1, source_target_pairs={{0,8},{1,9},{2,10},{3,11},{4,12},{5,13},{6,14},{7,15},{8,0},{9,1},... | collective-permute-start | bytes 393224 | tf_op jit(solution)/shard_map/ppermute | solution.py:85
  46.9 5.8 %collective-permute-start.21 = (bf16[256,256]{1,0:T(8,128)(2,1)S(1)}, bf16[256,256]{1,0:T(8,128)(2,1)S(1)}, u32[]{:S(2)}, u32[]{:S(2)}) collective-permute-start(bf16[256,256]{1,0:T(8,128)(2,1)S(1)} %get-tuple-element.88), channel_id=1, source_target_pairs={{0,24},{1,25},{2,26},{3,27},{4,28},{5,29},{6,30},{7,31},{8,16},{9,... | collective-permute-start | bytes 393224 | tf_op jit(solution)/shard_map/ppermute | solution.py:85
  59.3 11.5 %collective-permute-start.22 = (bf16[256,256]{1,0:T(8,128)(2,1)S(1)}, bf16[256,256]{1,0:T(8,128)(2,1)S(1)}, u32[]{:S(2)}, u32[]{:S(2)}) collective-permute-start(bf16[256,256]{1,0:T(8,128)(2,1)S(1)} %get-tuple-element.91), channel_id=1, source_target_pairs={{0,1},{1,0},{2,3},{3,2},{4,5},{5,4},{6,7},{7,6},{8,9},{9,8},{10,11... | collective-permute-start | bytes 393224 | tf_op jit(solution)/shard_map/ppermute | solution.py:85
  60.7 11.7 %collective-permute-start.23 = (bf16[256,256]{1,0:T(8,128)(2,1)S(1)}, bf16[256,256]{1,0:T(8,128)(2,1)S(1)}, u32[]{:S(2)}, u32[]{:S(2)}) collective-permute-start(bf16[256,256]{1,0:T(8,128)(2,1)S(1)} %get-tuple-element.92), channel_id=1, source_target_pairs={{0,8},{1,9},{2,10},{3,11},{4,12},{5,13},{6,14},{7,15},{8,0},{9,1},... | collective-permute-start | bytes 393224 | tf_op jit(solution)/shard_map/ppermute | solution.py:85
  61.4 12.6 %collective-permute-start.24 = (bf16[256,256]{1,0:T(8,128)(2,1)S(1)}, bf16[256,256]{1,0:T(8,128)(2,1)S(1)}, u32[]{:S(2)}, u32[]{:S(2)}) collective-permute-start(bf16[256,256]{1,0:T(8,128)(2,1)S(1)} %get-tuple-element.94), channel_id=1, source_target_pairs={{0,16},{1,2},{2,1},{3,4},{4,3},{5,6},{6,5},{7,23},{8,24},{9,10},{1... | collective-permute-start | bytes 393224 | tf_op jit(solution)/shard_map/ppermute | solution.py:85
  61.4 12.6 %collective-permute-start.25 = (bf16[256,256]{1,0:T(8,128)(2,1)S(1)}, bf16[256,256]{1,0:T(8,128)(2,1)S(1)}, u32[]{:S(2)}, u32[]{:S(2)}) collective-permute-start(bf16[256,256]{1,0:T(8,128)(2,1)S(1)} %get-tuple-element.95), channel_id=1, source_target_pairs={{0,24},{1,25},{2,26},{3,27},{4,28},{5,29},{6,30},{7,31},{8,16},{9,... | collective-permute-start | bytes 393224 | tf_op jit(solution)/shard_map/ppermute | solution.py:85
  68.3 6.3 %collective-permute-start.30 = (bf16[64,256]{1,0:T(8,128)(2,1)S(1)}, bf16[64,256]{1,0:T(8,128)(2,1)S(1)}, u32[]{:S(2)}, u32[]{:S(2)}) collective-permute-start(bf16[64,256]{1,0:T(8,128)(2,1)S(1)} %get-tuple-element.98), channel_id=1, source_target_pairs={{0,2},{1,3},{2,0},{3,1},{4,6},{5,7},{6,4},{7,5},{8,10},{9,11},{10,... | collective-permute-start | bytes 98312 | tf_op jit(solution)/shard_map/ppermute | solution.py:85
  72.4 5.7 %collective-permute-start.32 = (bf16[64,256]{1,0:T(8,128)(2,1)S(1)}, bf16[64,256]{1,0:T(8,128)(2,1)S(1)}, u32[]{:S(2)}, u32[]{:S(2)}) collective-permute-start(bf16[64,256]{1,0:T(8,128)(2,1)S(1)} %get-tuple-element.100), channel_id=1, source_target_pairs={{0,6},{1,7},{2,4},{3,5},{4,2},{5,3},{6,0},{7,1},{8,14},{9,15},{10,... | collective-permute-start | bytes 98312 | tf_op jit(solution)/shard_map/ppermute | solution.py:85
  (13 other events, 62.7 us)

commit v8 on v7

--- a/solution.py
+++ b/solution.py
@@ -145,7 +145,7 @@
         edge[...] = dot(sel_ref[m * part : (m + 1) * part, :], field).astype(BF)
 
 
-def tables_kernel(sizes, lists_ref, basis_t_ref, slot_ref, scatter_ref, based_ref, based_t_ref):
+def tables_kernel(sizes, lists_ref, basis_t_ref, slot_ref, scatter_ref, based_ref, based_t_ref, listed_ref):
     n = scatter_ref.shape[0]
     part = n // 4
     for m in range(4):
@@ -157,6 +157,7 @@
     based_t = dot(jnp.where(pick, 1.0, 0.0).astype(BF), basis_t_ref[...])
     based_t_ref[...] = based_t.astype(BF)
     based_ref[...] = based_t.T.astype(BF)
+    listed_ref[...] = dot(based_t.astype(BF), scatter_ref[...]).astype(BF)
 
 
 def product_kernel(left_ref, right_ref, out_ref):
@@ -191,14 +192,24 @@
     return total
 
 
-def early_kernel(sizes, load_ref, applied_ref, scatter_ref, n0, n2, out_ref):
-    out_ref[...] = load_ref[...] - applied_ref[...] - scattered(sizes, scatter_ref, (n0, n2), (0, 2))
-
-
-def resid_kernel(sizes, early_ref, scatter_ref, based_t_ref, n1, n3, resid_ref, coarse_ref):
-    resid = (early_ref[...] - scattered(sizes, scatter_ref, (n1, n3), (1, 3))).astype(BF)
-    resid_ref[...] = resid
-    coarse_ref[...] = dot(based_t_ref[...], resid).astype(BF)
+def early_kernel(sizes, load_ref, applied_ref, scatter_ref, based_t_ref, n0, n2, out_ref, coarse_ref):
+    early = load_ref[...] - applied_ref[...] - scattered(sizes, scatter_ref, (n0, n2), (0, 2))
+    out_ref[...] = early
+    coarse_ref[...] = dot(based_t_ref[...], early.astype(BF))
+
+
+def vector_kernel(sizes, early_ref, lists_ref, n1, n3, coarse_ref):
+    part = n1.shape[0]
+    there = shared(sizes)
+    total = early_ref[...]
+    for m, got in ((1, n1), (3, n3)):
+        got = jnp.where(there[m], got[...], jnp.zeros_like(got))
+        total = total - dot(lists_ref[:, m * part : (m + 1) * part], got)
+    coarse_ref[...] = total.astype(BF)
+
+
+def resid_kernel(sizes, early_ref, scatter_ref, n1, n3, resid_ref):
+    resid_ref[...] = (early_ref[...] - scattered(sizes, scatter_ref, (n1, n3), (1, 3))).astype(BF)
 
 
 def pick_kernel(sel_ref, whole_ref, fix_ref, *edges):
@@ -408,8 +419,11 @@
     if stepwise:
         keep, give = call(functools.partial(upper_kernel, cols // 2), [half, half], [keep, got], n)
         got = send(give, swap_pairs(0, 0, cols // 2))
-    scatter, based, based_t = call(
-        functools.partial(tables_kernel, sizes), [square, thin, shape((nb, n), BF)], [lists, basis_t, slot], n * n
+    scatter, based, based_t, listed = call(
+        functools.partial(tables_kernel, sizes),
+        [square, thin, shape((nb, n), BF), shape((nb, n), BF)],
+        [lists, basis_t, slot],
+        n * n,
     )
     if stepwise:
         keep, give = call(lower_kernel, [half, half], [keep, got], n)
@@ -417,13 +431,19 @@
     for sweep in range(ITERS):
         if sweep == 1:
             pre_sel = call(product_kernel, square, [sel, pre], 2 * n * n * n)
-        early = call(
-            functools.partial(early_kernel, sizes), field, [load, applied, scatter, near[0], near[2]], flops // 2
+        early, coarse_part = call(
+            functools.partial(early_kernel, sizes),
+            [field, shape((nb, cases), F32)],
+            [load, applied, scatter, based_t, near[0], near[2]],
+            flops // 2,
         )
-        resid, coarse = call(
+        coarse = call(
+            functools.partial(vector_kernel, sizes), vector, [coarse_part, listed, near[1], near[3]], n * nb * cases
+        )
+        resid = call(
             functools.partial(resid_kernel, sizes),
-            [shape((n, cases), BF), vector],
-            [early, scatter, based_t, near[1], near[3]],
+            shape((n, cases), BF),
+            [early, scatter, near[1], near[3]],
             flops // 2,
         )
         cores = [coarse] + [send(coarse, swap_pairs(dg, 0, 0)) for dg in range(1, grps)]

time: 79.7 us -> 81.8 us (1.026)
  waiting for transfers between devices: 20.4 us -> 22.6 us
    ppermute x33, waiting for transfers between devices: 20.4 us -> 22.6 us  [send(): return lax.ppermute(value, AXES, pairs)]
    ppermute x33, starting transfers between devices: 39.1 us -> 39.9 us  [send(): return lax.ppermute(value, AXES, pairs)]
    pallas_call x24 -> x26, Pallas kernels: 19.1 us -> 18.8 us  [call(): pl.pallas_call(kernel, out_shape=outs, in_specs=[hbm if k in far else vme...]
  transfers between devices with their start and end apart: 33 -> 33, of which waited for: 11 -> 14; matrix products, arithmetic and copies ran while one was open for 0% -> 0% of each run, Pallas kernels for 18% -> 15%
where the time goes in v8:
time: 81.8 us; the launch traced here: 81.7 us
  starting transfers between devices  39.9 us (49%)
  waiting for transfers between devices  22.6 us (28%)
  Pallas kernels  18.8 us (23%)
    ppermute x33, starting transfers between devices, send(): return lax.ppermute(value, AXES, pairs)  39.9 us
    ppermute x33, waiting for transfers between devices, send(): return lax.ppermute(value, AXES, pairs)  22.6 us
    pallas_call x26, Pallas kernels, call(): pl.pallas_call(kernel, out_shape=outs, in_specs=[hbm if k in far else vme...  18.8 us
  transfers between devices with their start and end apart: 33, of which 14 were waited for; matrix products, arithmetic and copies ran while one was open for 0% of the time, Pallas kernels for 15%

profile of v8, /device:TPU:0, one launch (start us, length us, event | category | flops | bytes accessed | tf_op | source)
XLA Modules:
  0.0 81.7 jit_solution(2611004276931576444)
XLA Ops:
  0.0 2.1 %shard_map.82 = (s32[1,1024]{1,0:T(1,128)S(1)}, bf16[1024,1024]{1,0:T(8,128)(2,1)S(1)}, bf16[1024,1024]{1,0:T(8,128)(2,1)S(1)}, f32[1024,256]{1,0:T(8,128)S(1)},...) custom-call(s32[1,1024]{1,0:T(1,128)} %bitcast.18, bf16[1024,1024]{1,0:T(8,128)(2,1)} %bitcast.16, ...), custom_call_target="tpu_custom_call" | custom-call | flops 1048576 | bytes 3411968 | tf_op jit(solution)/shard_map/pallas_call | solution.py:29
  2.2 2.2 %shard_map.83 = (f32[1024,256]{1,0:T(8,128)S(1)}, bf16[256,256]{1,0:T(8,128)(2,1)S(1)}, bf16[256,256]{1,0:T(8,128)(2,1)S(1)}, bf16[256,256]{1,0:T(8,128)(2,1)S(1)}, bf16[256,256]{1,0:T(8,128)(2,1)S(1)}) custom-call(bf16[1024,1024]{1,0:T(8,128)(2,1)S(1)} %get-tuple-element.54.op_ref.left_ref, f32[1024,256]{1,0:T(8,128)S(1)} %get-tuple-element.55.u_ref, ...), custom_call_target="tpu_custom_call" | custom-call | flops 1073741824 | bytes 5242880 | tf_op jit(solution)/shard_map/pallas_call | solution.py:29
  4.4 3.0 %collective-permute-start = (bf16[256,256]{1,0:T(8,128)(2,1)S(1)}, bf16[256,256]{1,0:T(8,128)(2,1)S(1)}, u32[]{:S(2)}, u32[]{:S(2)}) collective-permute-start(bf16[256,256]{1,0:T(8,128)(2,1)S(1)} %get-tuple-element.61), channel_id=1, source_target_pairs={{0,1},{1,0},{2,3},{3,2},{4,5},{5,4},{6,7},{7,6},{8,9},{9,8},{10,11... | collective-permute-start | bytes 393224 | tf_op jit(solution)/shard_map/ppermute | solution.py:85
  7.5 1.5 %collective-permute-start.1 = (bf16[256,256]{1,0:T(8,128)(2,1)S(1)}, bf16[256,256]{1,0:T(8,128)(2,1)S(1)}, u32[]{:S(2)}, u32[]{:S(2)}) collective-permute-start(bf16[256,256]{1,0:T(8,128)(2,1)S(1)} %get-tuple-element.62), channel_id=1, source_target_pairs={{0,8},{1,9},{2,10},{3,11},{4,12},{5,13},{6,14},{7,15},{8,0},{9,1},... | collective-permute-start | bytes 393224 | tf_op jit(solution)/shard_map/ppermute | solution.py:85
  9.6 2.4 %collective-permute-start.8 = (bf16[256,256]{1,0:T(8,128)(2,1)S(1)}, bf16[256,256]{1,0:T(8,128)(2,1)S(1)}, u32[]{:S(2)}, u32[]{:S(2)}) collective-permute-start(bf16[256,256]{1,0:T(8,128)(2,1)S(1)} %get-tuple-element.75), channel_id=1, source_target_pairs={{0,1},{1,0},{2,3},{3,2},{4,5},{5,4},{6,7},{7,6},{8,9},{9,8},{10,11... | collective-permute-start | bytes 393224 | tf_op jit(solution)/shard_map/ppermute | solution.py:85
  16.3 4.0 %collective-permute-start.9 = (bf16[256,256]{1,0:T(8,128)(2,1)S(1)}, bf16[256,256]{1,0:T(8,128)(2,1)S(1)}, u32[]{:S(2)}, u32[]{:S(2)}) collective-permute-start(bf16[256,256]{1,0:T(8,128)(2,1)S(1)} %get-tuple-element.77), channel_id=1, source_target_pairs={{0,4},{1,5},{2,6},{3,7},{4,0},{5,1},{6,2},{7,3},{8,12},{9,13},{10,... | collective-permute-start | bytes 393224 | tf_op jit(solution)/shard_map/ppermute | solution.py:85
  23.0 1.5 %collective-permute-start.5 = (bf16[256,256]{1,0:T(8,128)(2,1)S(1)}, bf16[256,256]{1,0:T(8,128)(2,1)S(1)}, u32[]{:S(2)}, u32[]{:S(2)}) collective-permute-start(bf16[256,256]{1,0:T(8,128)(2,1)S(1)} %get-tuple-element.68), channel_id=1, source_target_pairs={{0,8},{1,9},{2,10},{3,11},{4,12},{5,13},{6,14},{7,15},{8,0},{9,1},... | collective-permute-start | bytes 393224 | tf_op jit(solution)/shard_map/ppermute | solution.py:85
  25.1 1.8 %collective-permute-done.9.second_ref = bf16[256,256]{1,0:T(8,128)(2,1)S(1)} collective-permute-done((bf16[256,256]{1,0:T(8,128)(2,1)S(1)}, bf16[256,256]{1,0:T(8,128)(2,1)S(1)}, u32[]{:S(2)}, u32[]{:S(2)}) %collective-permute-start.9) | collective-permute-done | bytes 131104 | tf_op jit(solution)/shard_map/ppermute | solution.py:85
  29.7 2.4 %collective-permute-start.14 = (bf16[128,256]{1,0:T(8,128)(2,1)S(1)}, bf16[128,256]{1,0:T(8,128)(2,1)S(1)}, u32[]{:S(2)}, u32[]{:S(2)}) collective-permute-start(bf16[128,256]{1,0:T(8,128)(2,1)S(1)} %shard_map.96.refs_2_), channel_id=1, source_target_pairs={{0,9},{1,8},{2,11},{3,10},{4,13},{5,12},{6,15},{7,14},{8,1},{9,0},... | collective-permute-start | bytes 196616 | tf_op jit(solution)/shard_map/ppermute | solution.py:85
  33.3 2.9 %collective-permute-done.13.refs_4_ = bf16[128,256]{1,0:T(8,128)(2,1)S(1)} collective-permute-done((bf16[128,256]{1,0:T(8,128)(2,1)S(1)}, bf16[128,256]{1,0:T(8,128)(2,1)S(1)}, u32[]{:S(2)}, u32[]{:S(2)}) %collective-permute-start.13) | collective-permute-done | bytes 65568 | tf_op jit(solution)/shard_map/ppermute | solution.py:85
  36.6 1.4 %collective-permute-start.15 = (bf16[64,256]{1,0:T(8,128)(2,1)S(1)}, bf16[64,256]{1,0:T(8,128)(2,1)S(1)}, u32[]{:S(2)}, u32[]{:S(2)}) collective-permute-start(bf16[64,256]{1,0:T(8,128)(2,1)S(1)} %get-tuple-element.83), channel_id=1, source_target_pairs={{0,2},{1,3},{2,0},{3,1},{4,6},{5,7},{6,4},{7,5},{8,10},{9,11},{10,... | collective-permute-start | bytes 98312 | tf_op jit(solution)/shard_map/ppermute | solution.py:85
  38.0 1.9 %collective-permute-start.16 = (bf16[64,256]{1,0:T(8,128)(2,1)S(1)}, bf16[64,256]{1,0:T(8,128)(2,1)S(1)}, u32[]{:S(2)}, u32[]{:S(2)}) collective-permute-start(bf16[64,256]{1,0:T(8,128)(2,1)S(1)} %get-tuple-element.84), channel_id=1, source_target_pairs={{0,4},{1,5},{2,6},{3,7},{4,0},{5,1},{6,2},{7,3},{8,12},{9,13},{10,... | collective-permute-start | bytes 98312 | tf_op jit(solution)/shard_map/ppermute | solution.py:85
  41.0 1.5 %shard_map.90 = (f32[1024,256]{1,0:T(8,128)S(1)}, f32[1024,256]{1,0:T(8,128)S(1)}) custom-call(bf16[1024,1024]{1,0:T(8,128)(2,1)S(1)} %get-tuple-element.54.op_ref.left_ref, f32[1024,256]{1,0:T(8,128)S(1)} %shard_map.89.u_ref, f32[1024,256]{1,0:T(8,128)S(1)} %get-tuple-element.66.fix_ref, bf16[1024,1024]{1,0:T(8,128)(2,1)S(1)} %get-tuple-element.59.scatter_ref, ...), custom_call_target="tpu_custom_call" | custom-call | flops 1073741824 | bytes 6553600 | tf_op jit(solution)/shard_map/pallas_call | solution.py:29
  43.1 2.5 %collective-permute-done.17.refs_2_ = bf16[64,256]{1,0:T(8,128)(2,1)S(1)} collective-permute-done((bf16[64,256]{1,0:T(8,128)(2,1)S(1)}, bf16[64,256]{1,0:T(8,128)(2,1)S(1)}, u32[]{:S(2)}, u32[]{:S(2)}) %collective-permute-start.17) | collective-permute-done | bytes 32800 | tf_op jit(solution)/shard_map/ppermute | solution.py:85
  47.8 1.4 %collective-permute-start.19 = (bf16[256,256]{1,0:T(8,128)(2,1)S(1)}, bf16[256,256]{1,0:T(8,128)(2,1)S(1)}, u32[]{:S(2)}, u32[]{:S(2)}) collective-permute-start(bf16[256,256]{1,0:T(8,128)(2,1)S(1)} %get-tuple-element.88), channel_id=1, source_target_pairs={{0,8},{1,9},{2,10},{3,11},{4,12},{5,13},{6,14},{7,15},{8,0},{9,1},... | collective-permute-start | bytes 393224 | tf_op jit(solution)/shard_map/ppermute | solution.py:85
  50.0 1.7 %collective-permute-done.18.n0 = bf16[256,256]{1,0:T(8,128)(2,1)S(1)} collective-permute-done((bf16[256,256]{1,0:T(8,128)(2,1)S(1)}, bf16[256,256]{1,0:T(8,128)(2,1)S(1)}, u32[]{:S(2)}, u32[]{:S(2)}) %collective-permute-start.18) | collective-permute-done | bytes 131104 | tf_op jit(solution)/shard_map/ppermute | solution.py:85
  51.7 1.7 %collective-permute-done.19.n2 = bf16[256,256]{1,0:T(8,128)(2,1)S(1)} collective-permute-done((bf16[256,256]{1,0:T(8,128)(2,1)S(1)}, bf16[256,256]{1,0:T(8,128)(2,1)S(1)}, u32[]{:S(2)}, u32[]{:S(2)}) %collective-permute-start.19) | collective-permute-done | bytes 131104 | tf_op jit(solution)/shard_map/ppermute | solution.py:85
  55.7 2.3 %shard_map.91.pre_sel_ref = bf16[1024,1024]{1,0:T(8,128)(2,1)S(1)} custom-call(bf16[1024,1024]{1,0:T(8,128)(2,1)S(1)} %get-tuple-element.56.sel_ref.left_ref, bf16[1024,1024]{1,0:T(8,128)(2,1)S(1)} %bitcast.13), custom_call_target="tpu_custom_call" | custom-call | flops 2147483648 | bytes 4194304 | tf_op jit(solution)/shard_map/pallas_call | solution.py:29
  63.4 1.5 %collective-permute-start.25 = (bf16[256,256]{1,0:T(8,128)(2,1)S(1)}, bf16[256,256]{1,0:T(8,128)(2,1)S(1)}, u32[]{:S(2)}, u32[]{:S(2)}) collective-permute-start(bf16[256,256]{1,0:T(8,128)(2,1)S(1)} %get-tuple-element.97), channel_id=1, source_target_pairs={{0,24},{1,25},{2,26},{3,27},{4,28},{5,29},{6,30},{7,31},{8,16},{9,... | collective-permute-start | bytes 393224 | tf_op jit(solution)/shard_map/ppermute | solution.py:85
  64.9 1.9 %collective-permute-start.29 = (bf16[128,256]{1,0:T(8,128)(2,1)S(1)}, bf16[128,256]{1,0:T(8,128)(2,1)S(1)}, u32[]{:S(2)}, u32[]{:S(2)}) collective-permute-start(bf16[128,256]{1,0:T(8,128)(2,1)S(1)} %shard_map.105.refs_2_), channel_id=1, source_target_pairs={{0,9},{1,8},{2,11},{3,10},{4,13},{5,12},{6,15},{7,14},{8,1},{9,0},... | collective-permute-start | bytes 196616 | tf_op jit(solution)/shard_map/ppermute | solution.py:85
  66.9 3.2 %collective-permute-done.29.refs_5_ = bf16[128,256]{1,0:T(8,128)(2,1)S(1)} collective-permute-done((bf16[128,256]{1,0:T(8,128)(2,1)S(1)}, bf16[128,256]{1,0:T(8,128)(2,1)S(1)}, u32[]{:S(2)}, u32[]{:S(2)}) %collective-permute-start.29) | collective-permute-done | bytes 65568 | tf_op jit(solution)/shard_map/ppermute | solution.py:85
  70.4 2.6 %collective-permute-start.30 = (bf16[64,256]{1,0:T(8,128)(2,1)S(1)}, bf16[64,256]{1,0:T(8,128)(2,1)S(1)}, u32[]{:S(2)}, u32[]{:S(2)}) collective-permute-start(bf16[64,256]{1,0:T(8,128)(2,1)S(1)} %get-tuple-element.100), channel_id=1, source_target_pairs={{0,2},{1,3},{2,0},{3,1},{4,6},{5,7},{6,4},{7,5},{8,10},{9,11},{10,... | collective-permute-start | bytes 98312 | tf_op jit(solution)/shard_map/ppermute | solution.py:85
  73.1 1.7 %collective-permute-start.31 = (bf16[64,256]{1,0:T(8,128)(2,1)S(1)}, bf16[64,256]{1,0:T(8,128)(2,1)S(1)}, u32[]{:S(2)}, u32[]{:S(2)}) collective-permute-start(bf16[64,256]{1,0:T(8,128)(2,1)S(1)} %get-tuple-element.101), channel_id=1, source_target_pairs={{0,4},{1,5},{2,6},{3,7},{4,0},{5,1},{6,2},{7,3},{8,12},{9,13},{10,... | collective-permute-start | bytes 98312 | tf_op jit(solution)/shard_map/ppermute | solution.py:85
  77.9 2.6 %collective-permute-done.32.refs_2_ = bf16[64,256]{1,0:T(8,128)(2,1)S(1)} collective-permute-done((bf16[64,256]{1,0:T(8,128)(2,1)S(1)}, bf16[64,256]{1,0:T(8,128)(2,1)S(1)}, u32[]{:S(2)}, u32[]{:S(2)}) %collective-permute-start.32) | collective-permute-done | bytes 32800 | tf_op jit(solution)/shard_map/ppermute | solution.py:85
  (76 shorter events, 29.4 us)
Async XLA Ops:
  4.4 8.4 %collective-permute-start = (bf16[256,256]{1,0:T(8,128)(2,1)S(1)}, bf16[256,256]{1,0:T(8,128)(2,1)S(1)}, u32[]{:S(2)}, u32[]{:S(2)}) collective-permute-start(bf16[256,256]{1,0:T(8,128)(2,1)S(1)} %get-tuple-element.61), channel_id=1, source_target_pairs={{0,1},{1,0},{2,3},{3,2},{4,5},{5,4},{6,7},{7,6},{8,9},{9,8},{10,11... | collective-permute-start | bytes 393224 | tf_op jit(solution)/shard_map/ppermute | solution.py:85
  7.5 5.4 %collective-permute-start.1 = (bf16[256,256]{1,0:T(8,128)(2,1)S(1)}, bf16[256,256]{1,0:T(8,128)(2,1)S(1)}, u32[]{:S(2)}, u32[]{:S(2)}) collective-permute-start(bf16[256,256]{1,0:T(8,128)(2,1)S(1)} %get-tuple-element.62), channel_id=1, source_target_pairs={{0,8},{1,9},{2,10},{3,11},{4,12},{5,13},{6,14},{7,15},{8,0},{9,1},... | collective-permute-start | bytes 393224 | tf_op jit(solution)/shard_map/ppermute | solution.py:85
  9.0 5.8 %collective-permute-start.3 = (bf16[256,256]{1,0:T(8,128)(2,1)S(1)}, bf16[256,256]{1,0:T(8,128)(2,1)S(1)}, u32[]{:S(2)}, u32[]{:S(2)}) collective-permute-start(bf16[256,256]{1,0:T(8,128)(2,1)S(1)} %get-tuple-element.65), channel_id=1, source_target_pairs={{0,24},{1,25},{2,26},{3,27},{4,28},{5,29},{6,30},{7,31},{8,16},{9,... | collective-permute-start | bytes 393224 | tf_op jit(solution)/shard_map/ppermute | solution.py:85
  9.6 6.7 %collective-permute-start.8 = (bf16[256,256]{1,0:T(8,128)(2,1)S(1)}, bf16[256,256]{1,0:T(8,128)(2,1)S(1)}, u32[]{:S(2)}, u32[]{:S(2)}) collective-permute-start(bf16[256,256]{1,0:T(8,128)(2,1)S(1)} %get-tuple-element.75), channel_id=1, source_target_pairs={{0,1},{1,0},{2,3},{3,2},{4,5},{5,4},{6,7},{7,6},{8,9},{9,8},{10,11... | collective-permute-start | bytes 393224 | tf_op jit(solution)/shard_map/ppermute | solution.py:85
  15.0 9.5 %collective-permute-start.11 = (bf16[64,256]{1,0:T(8,128)(2,1)S(1)}, bf16[64,256]{1,0:T(8,128)(2,1)S(1)}, u32[]{:S(2)}, u32[]{:S(2)}) collective-permute-start(bf16[64,256]{1,0:T(8,128)(2,1)S(1)} %shard_map.95.mine_ref), channel_id=1, source_target_pairs={{0,16},{1,17},{2,18},{3,19},{4,20},{5,21},{6,22},{7,23},{8,24},{9,... | collective-permute-start | bytes 98312 | tf_op jit(solution)/shard_map/ppermute | solution.py:85
  16.3 10.6 %collective-permute-start.9 = (bf16[256,256]{1,0:T(8,128)(2,1)S(1)}, bf16[256,256]{1,0:T(8,128)(2,1)S(1)}, u32[]{:S(2)}, u32[]{:S(2)}) collective-permute-start(bf16[256,256]{1,0:T(8,128)(2,1)S(1)} %get-tuple-element.77), channel_id=1, source_target_pairs={{0,4},{1,5},{2,6},{3,7},{4,0},{5,1},{6,2},{7,3},{8,12},{9,13},{10,... | collective-permute-start | bytes 393224 | tf_op jit(solution)/shard_map/ppermute | solution.py:85
  22.2 6.7 %collective-permute-start.4 = (bf16[256,256]{1,0:T(8,128)(2,1)S(1)}, bf16[256,256]{1,0:T(8,128)(2,1)S(1)}, u32[]{:S(2)}, u32[]{:S(2)}) collective-permute-start(bf16[256,256]{1,0:T(8,128)(2,1)S(1)} %get-tuple-element.67), channel_id=1, source_target_pairs={{0,1},{1,0},{2,3},{3,2},{4,5},{5,4},{6,7},{7,6},{8,9},{9,8},{10,11... | collective-permute-start | bytes 393224 | tf_op jit(solution)/shard_map/ppermute | solution.py:85
  23.0 6.8 %collective-permute-start.5 = (bf16[256,256]{1,0:T(8,128)(2,1)S(1)}, bf16[256,256]{1,0:T(8,128)(2,1)S(1)}, u32[]{:S(2)}, u32[]{:S(2)}) collective-permute-start(bf16[256,256]{1,0:T(8,128)(2,1)S(1)} %get-tuple-element.68), channel_id=1, source_target_pairs={{0,8},{1,9},{2,10},{3,11},{4,12},{5,13},{6,14},{7,15},{8,0},{9,1},... | collective-permute-start | bytes 393224 | tf_op jit(solution)/shard_map/ppermute | solution.py:85
  27.0 9.2 %collective-permute-start.10 = (bf16[256,256]{1,0:T(8,128)(2,1)S(1)}, bf16[256,256]{1,0:T(8,128)(2,1)S(1)}, u32[]{:S(2)}, u32[]{:S(2)}) collective-permute-start(bf16[256,256]{1,0:T(8,128)(2,1)S(1)} %get-tuple-element.79), channel_id=1, source_target_pairs={{0,2},{1,3},{2,0},{3,1},{4,6},{5,7},{6,4},{7,5},{8,10},{9,11},{10,... | collective-permute-start | bytes 393224 | tf_op jit(solution)/shard_map/ppermute | solution.py:85
  27.6 13.4 %collective-permute-start.6 = (bf16[256,256]{1,0:T(8,128)(2,1)S(1)}, bf16[256,256]{1,0:T(8,128)(2,1)S(1)}, u32[]{:S(2)}, u32[]{:S(2)}) collective-permute-start(bf16[256,256]{1,0:T(8,128)(2,1)S(1)} %get-tuple-element.69), channel_id=1, source_target_pairs={{0,16},{1,2},{2,1},{3,4},{4,3},{5,6},{6,5},{7,23},{8,24},{9,10},{1... | collective-permute-start | bytes 393224 | tf_op jit(solution)/shard_map/ppermute | solution.py:85
  28.9 12.1 %collective-permute-start.7 = (bf16[256,256]{1,0:T(8,128)(2,1)S(1)}, bf16[256,256]{1,0:T(8,128)(2,1)S(1)}, u32[]{:S(2)}, u32[]{:S(2)}) collective-permute-start(bf16[256,256]{1,0:T(8,128)(2,1)S(1)} %get-tuple-element.70), channel_id=1, source_target_pairs={{0,24},{1,25},{2,26},{3,27},{4,28},{5,29},{6,30},{7,31},{8,16},{9,... | collective-permute-start | bytes 393224 | tf_op jit(solution)/shard_map/ppermute | solution.py:85
  28.9 7.3 %collective-permute-start.13 = (bf16[128,256]{1,0:T(8,128)(2,1)S(1)}, bf16[128,256]{1,0:T(8,128)(2,1)S(1)}, u32[]{:S(2)}, u32[]{:S(2)}) collective-permute-start(bf16[128,256]{1,0:T(8,128)(2,1)S(1)} %shard_map.96.refs_2_), channel_id=1, source_target_pairs={{0,8},{1,9},{2,10},{3,11},{4,12},{5,13},{6,14},{7,15},{8,0},{9,1},... | collective-permute-start | bytes 196616 | tf_op jit(solution)/shard_map/ppermute | solution.py:85
  29.7 6.5 %collective-permute-start.14 = (bf16[128,256]{1,0:T(8,128)(2,1)S(1)}, bf16[128,256]{1,0:T(8,128)(2,1)S(1)}, u32[]{:S(2)}, u32[]{:S(2)}) collective-permute-start(bf16[128,256]{1,0:T(8,128)(2,1)S(1)} %shard_map.96.refs_2_), channel_id=1, source_target_pairs={{0,9},{1,8},{2,11},{3,10},{4,13},{5,12},{6,15},{7,14},{8,1},{9,0},... | collective-permute-start | bytes 196616 | tf_op jit(solution)/shard_map/ppermute | solution.py:85
  36.6 6.0 %collective-permute-start.15 = (bf16[64,256]{1,0:T(8,128)(2,1)S(1)}, bf16[64,256]{1,0:T(8,128)(2,1)S(1)}, u32[]{:S(2)}, u32[]{:S(2)}) collective-permute-start(bf16[64,256]{1,0:T(8,128)(2,1)S(1)} %get-tuple-element.83), channel_id=1, source_target_pairs={{0,2},{1,3},{2,0},{3,1},{4,6},{5,7},{6,4},{7,5},{8,10},{9,11},{10,... | collective-permute-start | bytes 98312 | tf_op jit(solution)/shard_map/ppermute | solution.py:85
  39.9 5.7 %collective-permute-start.17 = (bf16[64,256]{1,0:T(8,128)(2,1)S(1)}, bf16[64,256]{1,0:T(8,128)(2,1)S(1)}, u32[]{:S(2)}, u32[]{:S(2)}) collective-permute-start(bf16[64,256]{1,0:T(8,128)(2,1)S(1)} %get-tuple-element.85), channel_id=1, source_target_pairs={{0,6},{1,7},{2,4},{3,5},{4,2},{5,3},{6,0},{7,1},{8,14},{9,15},{10,... | collective-permute-start | bytes 98312 | tf_op jit(solution)/shard_map/ppermute | solution.py:85
  47.8 5.5 %collective-permute-start.19 = (bf16[256,256]{1,0:T(8,128)(2,1)S(1)}, bf16[256,256]{1,0:T(8,128)(2,1)S(1)}, u32[]{:S(2)}, u32[]{:S(2)}) collective-permute-start(bf16[256,256]{1,0:T(8,128)(2,1)S(1)} %get-tuple-element.88), channel_id=1, source_target_pairs={{0,8},{1,9},{2,10},{3,11},{4,12},{5,13},{6,14},{7,15},{8,0},{9,1},... | collective-permute-start | bytes 393224 | tf_op jit(solution)/shard_map/ppermute | solution.py:85
  49.2 5.8 %collective-permute-start.21 = (bf16[256,256]{1,0:T(8,128)(2,1)S(1)}, bf16[256,256]{1,0:T(8,128)(2,1)S(1)}, u32[]{:S(2)}, u32[]{:S(2)}) collective-permute-start(bf16[256,256]{1,0:T(8,128)(2,1)S(1)} %get-tuple-element.91), channel_id=1, source_target_pairs={{0,24},{1,25},{2,26},{3,27},{4,28},{5,29},{6,30},{7,31},{8,16},{9,... | collective-permute-start | bytes 393224 | tf_op jit(solution)/shard_map/ppermute | solution.py:85
  59.7 5.3 %collective-permute-start.28 = (bf16[128,256]{1,0:T(8,128)(2,1)S(1)}, bf16[128,256]{1,0:T(8,128)(2,1)S(1)}, u32[]{:S(2)}, u32[]{:S(2)}) collective-permute-start(bf16[128,256]{1,0:T(8,128)(2,1)S(1)} %shard_map.105.refs_2_), channel_id=1, source_target_pairs={{0,8},{1,9},{2,10},{3,11},{4,12},{5,13},{6,14},{7,15},{8,0},{9,1},... | collective-permute-start | bytes 196616 | tf_op jit(solution)/shard_map/ppermute | solution.py:85
  61.6 11.4 %collective-permute-start.22 = (bf16[256,256]{1,0:T(8,128)(2,1)S(1)}, bf16[256,256]{1,0:T(8,128)(2,1)S(1)}, u32[]{:S(2)}, u32[]{:S(2)}) collective-permute-start(bf16[256,256]{1,0:T(8,128)(2,1)S(1)} %get-tuple-element.93), channel_id=1, source_target_pairs={{0,1},{1,0},{2,3},{3,2},{4,5},{5,4},{6,7},{7,6},{8,9},{9,8},{10,11... | collective-permute-start | bytes 393224 | tf_op jit(solution)/shard_map/ppermute | solution.py:85
  62.8 12.0 %collective-permute-start.23 = (bf16[256,256]{1,0:T(8,128)(2,1)S(1)}, bf16[256,256]{1,0:T(8,128)(2,1)S(1)}, u32[]{:S(2)}, u32[]{:S(2)}) collective-permute-start(bf16[256,256]{1,0:T(8,128)(2,1)S(1)} %get-tuple-element.94), channel_id=1, source_target_pairs={{0,8},{1,9},{2,10},{3,11},{4,12},{5,13},{6,14},{7,15},{8,0},{9,1},... | collective-permute-start | bytes 393224 | tf_op jit(solution)/shard_map/ppermute | solution.py:85
  63.4 12.6 %collective-permute-start.24 = (bf16[256,256]{1,0:T(8,128)(2,1)S(1)}, bf16[256,256]{1,0:T(8,128)(2,1)S(1)}, u32[]{:S(2)}, u32[]{:S(2)}) collective-permute-start(bf16[256,256]{1,0:T(8,128)(2,1)S(1)} %get-tuple-element.96), channel_id=1, source_target_pairs={{0,16},{1,2},{2,1},{3,4},{4,3},{5,6},{6,5},{7,23},{8,24},{9,10},{1... | collective-permute-start | bytes 393224 | tf_op jit(solution)/shard_map/ppermute | solution.py:85
  63.4 12.6 %collective-permute-start.25 = (bf16[256,256]{1,0:T(8,128)(2,1)S(1)}, bf16[256,256]{1,0:T(8,128)(2,1)S(1)}, u32[]{:S(2)}, u32[]{:S(2)}) collective-permute-start(bf16[256,256]{1,0:T(8,128)(2,1)S(1)} %get-tuple-element.97), channel_id=1, source_target_pairs={{0,24},{1,25},{2,26},{3,27},{4,28},{5,29},{6,30},{7,31},{8,16},{9,... | collective-permute-start | bytes 393224 | tf_op jit(solution)/shard_map/ppermute | solution.py:85
  70.4 6.2 %collective-permute-start.30 = (bf16[64,256]{1,0:T(8,128)(2,1)S(1)}, bf16[64,256]{1,0:T(8,128)(2,1)S(1)}, u32[]{:S(2)}, u32[]{:S(2)}) collective-permute-start(bf16[64,256]{1,0:T(8,128)(2,1)S(1)} %get-tuple-element.100), channel_id=1, source_target_pairs={{0,2},{1,3},{2,0},{3,1},{4,6},{5,7},{6,4},{7,5},{8,10},{9,11},{10,... | collective-permute-start | bytes 98312 | tf_op jit(solution)/shard_map/ppermute | solution.py:85
  74.8 5.7 %collective-permute-start.32 = (bf16[64,256]{1,0:T(8,128)(2,1)S(1)}, bf16[64,256]{1,0:T(8,128)(2,1)S(1)}, u32[]{:S(2)}, u32[]{:S(2)}) collective-permute-start(bf16[64,256]{1,0:T(8,128)(2,1)S(1)} %get-tuple-element.102), channel_id=1, source_target_pairs={{0,6},{1,7},{2,4},{3,5},{4,2},{5,3},{6,0},{7,1},{8,14},{9,15},{10,... | collective-permute-start | bytes 98312 | tf_op jit(solution)/shard_map/ppermute | solution.py:85
  (13 other events, 77.3 us)
